TPU v7x, 32 devices: a whole 2x2x4 slice. The times are simulated.
32 devices in a mesh: dp: 4 (over x, core), fsdp: 8 (over z, y).
Axes of the slice: x: 2, y: 2, z: 4, core: 2. Of those that a mesh axis runs over, the one named last changes fastest.
Arguments:
- tokens: bfloat16 [18432, 576], P(('dp', 'fsdp')), may hold values from -6 to 6
- cotangent: bfloat16 [18432, 576], P(('dp', 'fsdp')), may hold values from -6 to 6
- w_query: bfloat16 [576, 576], P(None, 'fsdp'), may hold values from -0.25 to 0.25
- key_projection_weight: bfloat16 [576, 192], P(None, 'fsdp'), may hold values from -0.25 to 0.25
- value_projection_weight: bfloat16 [576, 192], P(None, 'fsdp'), may hold values from -0.25 to 0.25
- output_projection_weight: bfloat16 [576, 576], P(None, 'fsdp'), may hold values from -0.75 to 0.75
- w_gate: bfloat16 [576, 1536], P(None, 'fsdp'), may hold values from -0.25 to 0.25
- w_up: bfloat16 [576, 1536], P(None, 'fsdp'), may hold values from -0.25 to 0.25
- w_down: bfloat16 [1536, 576], P(None, 'fsdp'), may hold values from -0.21875 to 0.21875
- gain_attn: bfloat16 [576], P('fsdp'), may hold values from 0.099609375 to 1.8984375
- gain_mlp: bfloat16 [576], P('fsdp'), may hold values from 0.099609375 to 1.8984375
Outputs:
- output: bfloat16 [18432, 576], P(('dp', 'fsdp'))
- grad_tokens: bfloat16 [18432, 576], P(('dp', 'fsdp'))
- grad_query: float32 [576, 576], P(None, 'fsdp')
- grad_key: float32 [576, 192], P(None, 'fsdp')
- grad_value: float32 [576, 192], P(None, 'fsdp')
- grad_out: float32 [576, 576], P(None, 'fsdp')
- grad_gate: float32 [576, 1536], P(None, 'fsdp')
- grad_up: float32 [576, 1536], P(None, 'fsdp')
- grad_down: float32 [1536, 576], P(None, 'fsdp')
- grad_gain_attn: float32 [576], P('fsdp')
- grad_gain_mlp: float32 [576], P('fsdp')
All inputs are finite; a program needn't handle non-finite values.
Results may differ from a plain program's by a relative error of at most 0.017.
Values may be sent and summed in bfloat16 or wider, within the bound.
No kernel may reach another device: no remote copies, remote signals or barrier semaphores. Data moves between devices by JAX's collectives and lax.ppermute only.
A program may use at most 128 MiB of HBM per device.

v0:
```python
import functools

import jax
import jax.numpy as jnp
import numpy as np
from jax import lax
from jax.experimental import pallas as pl
from jax.experimental.pallas import tpu as pltpu
from jax.sharding import PartitionSpec as P


QUERY_HEADS = 9
KEY_VALUE_HEADS = 3
HEAD_SIZE = 64
SEQUENCE_LENGTH = 192

EPS_NORM = 1e-05
ROPE_BASE = 100000.0


F32 = jnp.float32
BF16 = jnp.bfloat16
LANES = 128


def up_to(value, step):
    return -(-value // step) * step


def dot_nn(left, right):
    return lax.dot_general(left, right, (((1,), (0,)), ((), ())), preferred_element_type=F32)


def dot_nt(left, right):
    return lax.dot_general(left, right, (((1,), (1,)), ((), ())), preferred_element_type=F32)


def dot_tn(left, right):
    return lax.dot_general(left, right, (((0,), (0,)), ((), ())), preferred_element_type=F32)


def rope_tables():
    half = HEAD_SIZE // 2
    position = np.arange(SEQUENCE_LENGTH).astype(np.float32)
    freqs = np.power(
        np.float32(ROPE_BASE), -(np.arange(half).astype(np.float32) * np.float32(2.0 / HEAD_SIZE))
    ).astype(np.float32)
    angles = (position[:, None] * freqs[None, :]).astype(np.float32)
    cosine = np.cos(angles.astype(np.float64)).astype(np.float32)
    sine = np.sin(angles.astype(np.float64)).astype(np.float32)
    reps = LANES // HEAD_SIZE
    return (
        jnp.asarray(np.concatenate([cosine, cosine] * reps, 1)),
        jnp.asarray(np.concatenate([-sine, sine] * reps, 1)),
    )


def swap_halves(block):
    half = HEAD_SIZE // 2
    lane = lax.broadcasted_iota(jnp.int32, block.shape, block.ndim - 1)
    return jnp.where(
        lane % HEAD_SIZE < half,
        pltpu.roll(block, LANES - half, block.ndim - 1),
        pltpu.roll(block, half, block.ndim - 1),
    )


def lane_half(block, odd):
    lane = lax.broadcasted_iota(jnp.int32, block.shape, block.ndim - 1)
    keep = (lane >= HEAD_SIZE) if odd else (lane < HEAD_SIZE)
    return jnp.where(keep, block, jnp.zeros_like(block))


class Plan:
    def __init__(self, mesh, width, hidden):
        self.dp, self.fsdp = mesh.shape["dp"], mesh.shape["fsdp"]
        self.width, self.hidden = width, hidden
        self.kv = KEY_VALUE_HEADS * HEAD_SIZE
        self.lanes = up_to(width, LANES)
        self.nx, self.nc = self.dp // 2, 2
        self.nz, self.ny = self.fsdp // 2, 2
        s, d = self.fsdp, self.dp
        self.direct = (
            d % 2 == 0
            and s % 2 == 0
            and (s // 2) & (s // 2 - 1) == 0
            and (width // s) % 8 == 0
            and (self.kv // s) % 8 == 0
            and ((width + self.kv) // s) % (16 * (d // 2)) == 0
            and (hidden // s // d) % 16 == 0
            and (hidden // d) % LANES == 0
        )
        if not self.direct:
            self.nx = self.nc = self.nz = self.ny = 1
        self.shards = self.nz * self.ny
        self.parts = self.nx * self.nc
        self.out_rows = width // self.shards
        self.kv_rows = self.kv // self.shards
        self.half_rows = self.out_rows + self.kv_rows
        self.ff_rows = hidden // self.shards // self.parts
        self.ff_cols = hidden // self.parts

    def key(self):
        return (self.dp, self.fsdp, self.width, self.hidden)


def attention_forward_kernel(plan, n_half, place, x_ref, cos_ref, sin_ref, *refs):
    pieces, refs = refs[: 2 * n_half], refs[2 * n_half :]
    (q_ref, k_ref, v_ref, attn_ref, prob_ref, wq_ref, wk_ref, wv_ref, wo_ref, gain_ref, pack, xs, sem) = refs
    width, lanes, kv = plan.width, plan.lanes, plan.kv
    c_at, z_at, y_at = place[1], place[2], place[3]
    copies = []
    count = 0
    for at, piece in enumerate(pieces):
        rc, ry = at // n_half, at % n_half
        half = (c_at + rc) % 2
        for k in range(plan.nz):
            shard = (z_at ^ k) * plan.ny + (y_at + ry) % plan.ny
            copies.append(pltpu.make_async_copy(piece.at[k], pack.at[half, shard], sem.at[count]))
            count += 1
    for copy in copies:
        copy.start()
    xs[:, lanes - LANES :] = jnp.zeros((xs.shape[0], LANES), F32)
    xs[:, :width] = x_ref[...].astype(F32)
    xfull = xs[...]
    inv = lax.rsqrt(jnp.sum(xfull * xfull, -1, keepdims=True) * (1.0 / width) + EPS_NORM)
    for copy in copies:
        copy.wait()
    rows, krows = plan.out_rows, plan.kv_rows
    qs, ks, vs, os = [], [], [], []
    for s in range(plan.shards):
        first = pack[0, s].astype(F32)
        second = pack[1, s].astype(F32)
        qs.append(first[:rows])
        ks.append(first[rows:])
        vs.append(second[:krows])
        os.append(second[krows:])
    tail = jnp.zeros((lanes - width, lanes), F32)
    wq_full = jnp.concatenate(qs + [tail], 0)
    lane = lax.broadcasted_iota(jnp.int32, (lanes, lanes), 1)
    wq_ref[...] = jnp.where(lane < width, wq_full, 0.0).astype(BF16)
    kv_pad = 2 * LANES
    ktail = jnp.zeros((kv_pad - kv, lanes), F32)
    wk_ref[...] = jnp.concatenate(ks + [ktail], 0).astype(BF16)
    wv_ref[...] = jnp.concatenate(vs + [ktail], 0).astype(BF16)
    wo_ref[...] = jnp.concatenate(os + [tail], 0).astype(BF16)
    turned = wq_full[:, lanes - LANES :].T
    at = width - (lanes - LANES)
    gain_ref[...] = turned[at : at + 8]
    gain = turned[at : at + 1]
    normed = (xfull * inv * gain).astype(BF16)
    tokens = xs.shape[0]
    n_seq = tokens // SEQUENCE_LENGTH
    cos = cos_ref[...][None]
    sin = sin_ref[...][None]

    def rotate(block):
        cube = block.reshape(n_seq, SEQUENCE_LENGTH, LANES)
        return (cube * cos + swap_halves(cube) * sin).reshape(tokens, LANES)

    q = dot_nt(normed, wq_ref[...])
    for b in range(lanes // LANES):
        q_ref[:, b * LANES : (b + 1) * LANES] = rotate(q[:, b * LANES : (b + 1) * LANES]).astype(BF16)
    k = dot_nt(normed, wk_ref[...])
    v = dot_nt(normed, wv_ref[...])
    for b in range(2):
        kb = rotate(k[:, b * LANES : (b + 1) * LANES])
        vb = v[:, b * LANES : (b + 1) * LANES]
        k_ref[:, b * LANES : (b + 1) * LANES] = kb.astype(BF16)
        v_ref[:, b * LANES : (b + 1) * LANES] = vb.astype(BF16)
        k_ref[:, (b + 2) * LANES : (b + 3) * LANES] = pltpu.roll(kb, HEAD_SIZE, 1).astype(BF16)
        v_ref[:, (b + 2) * LANES : (b + 3) * LANES] = pltpu.roll(vb, HEAD_SIZE, 1).astype(BF16)

    shape = (SEQUENCE_LENGTH, SEQUENCE_LENGTH)
    allowed = lax.broadcasted_iota(jnp.int32, shape, 0) >= lax.broadcasted_iota(jnp.int32, shape, 1)

    def one_sequence(n, carry):
        at_rows = pl.ds(pl.multiple_of(n * SEQUENCE_LENGTH, SEQUENCE_LENGTH), SEQUENCE_LENGTH)
        for pair in range(lanes // LANES):
            q2 = q_ref[at_rows, pair * LANES : (pair + 1) * LANES]
            total = None
            for odd in range(2):
                h = pair * 2 + odd
                if h >= QUERY_HEADS:
                    continue
                kf = head_form(k_ref, at_rows, h)
                vf = head_form(v_ref, at_rows, h)
                scores = dot_nt(q2, kf) * HEAD_SIZE ** (-0.5)
                expo = jnp.where(allowed, jnp.exp(jnp.where(allowed, scores, 0.0)), 0.0)
                p = (expo * (1.0 / jnp.sum(expo, -1, keepdims=True))).astype(BF16)
                prob_ref[n, h] = p
                part = dot_nn(p, vf)
                total = part if total is None else total + part
            attn_ref[at_rows, pair * LANES : (pair + 1) * LANES] = total.astype(BF16)
        return carry

    lax.fori_loop(0, n_seq, one_sequence, 0)


def head_form(ref, at_rows, h):
    group, odd = h // (QUERY_HEADS // KEY_VALUE_HEADS), h % 2
    block = group // 2 + (2 if group % 2 != odd else 0)
    return lane_half(ref[at_rows, block * LANES : (block + 1) * LANES], odd)


def mlp_kernel(plan, first, last, place, dy_ref, gain_ref, *refs):
    if first:
        x_ref, attn_ref, wo_ref, refs = refs[0], refs[1], refs[2], refs[3:]
    else:
        mid_in, out_in, dn_in, refs = refs[0], refs[1], refs[2], refs[3:]
    n_pieces = plan.nc * plan.ny
    gates, refs = refs[:n_pieces], refs[n_pieces:]
    downs, refs = refs[:n_pieces], refs[n_pieces:]
    if last:
        out_ref, dmid_ref, dgain_ref, refs = refs[0], refs[1], refs[2], refs[3:]
    else:
        mid_ref, out_ref, dn_ref, refs = refs[0], refs[1], refs[2], refs[3:]
    gg_out, refs = refs[: plan.nc], refs[plan.nc :]
    gd_out, refs = refs[: plan.nc], refs[plan.nc :]
    (wg, wu, wd3, wd, gg, gu, gd, xs, sem) = refs
    width, lanes = plan.width, plan.lanes
    z_at, y_at = place[2], place[3]
    rows, cols = plan.ff_rows, plan.ff_cols
    loads, late = [], []
    count = 0
    blocks = [(rc, ry, rz) for rc in range(plan.nc) for ry in range(plan.ny) for rz in range(plan.nz)]

    def spot(rc, ry, rz):
        shard = (z_at ^ rz) * plan.ny + (y_at + ry) % plan.ny
        return shard, pl.multiple_of(rc * cols + shard * rows, rows)

    for rc, ry, rz in blocks:
        shard, at = spot(rc, ry, rz)
        piece = gates[rc * plan.ny + ry]
        for which, dest in enumerate((wg, wu)):
            loads.append(
                pltpu.make_async_copy(
                    piece.at[rz, pl.ds(which * rows, rows)], dest.at[pl.ds(at, rows)], sem.at[count]
                )
            )
            count += 1
    for rc, ry, rz in blocks:
        shard, at = spot(rc, ry, rz)
        piece = downs[rc * plan.ny + ry]
        late.append(
            pltpu.make_async_copy(piece.at[rz], wd3.at[shard, :, pl.ds(rc * cols, cols)], sem.at[count])
        )
        count += 1
    for copy in loads + late:
        copy.start()
    tokens = xs.shape[0]
    gain = gain_ref[1:2]
    xs[:, lanes - LANES :] = jnp.zeros((tokens, LANES), F32)
    if first:
        xs[:, :width] = x_ref[...].astype(F32)
        mid = xs[...] + dot_nt(attn_ref[...], wo_ref[...])
    else:
        mid = mid_in[...]
    inv = lax.rsqrt(jnp.sum(mid * mid, -1, keepdims=True) * (1.0 / width) + EPS_NORM)
    unit = mid * inv
    normed = (unit * gain).astype(BF16)
    xs[:, :width] = dy_ref[...].astype(F32)
    dy = xs[...].astype(BF16)
    for copy in loads:
        copy.wait()
    gate = dot_nt(normed, wg[...])
    upper = dot_nt(normed, wu[...])
    for copy in late:
        copy.wait()
    units = plan.nc * cols
    wd[width:, :] = jnp.zeros((lanes - width, units), BF16)
    wd[:width, :] = jnp.concatenate([wd3[s].astype(F32) for s in range(plan.shards)], 0).astype(BF16)
    dhidden = dot_nn(dy, wd[...])
    sigma = 1.0 / (1.0 + jnp.exp(-gate))
    act = gate * sigma
    hid = (act * upper).astype(BF16)
    dgate = (dhidden * upper * sigma * (1.0 + gate * (1.0 - sigma))).astype(BF16)
    dupper = (dhidden * act).astype(BF16)
    gg[...] = dot_tn(dgate, normed).astype(BF16)
    gu[...] = dot_tn(dupper, normed).astype(BF16)
    down = dot_tn(dy, hid)
    for s in range(plan.shards):
        gd[s] = down[s * plan.out_rows : (s + 1) * plan.out_rows].astype(BF16)
    stores = []
    count = 0
    for rc, ry, rz in blocks:
        shard, at = spot(rc, ry, rz)
        for which, grad in enumerate((gg, gu)):
            stores.append(
                pltpu.make_async_copy(
                    grad.at[pl.ds(at, rows)], gg_out[rc].at[ry, rz, pl.ds(which * rows, rows)], sem.at[count]
                )
            )
            count += 1
        stores.append(
            pltpu.make_async_copy(gd.at[shard, :, pl.ds(rc * cols, cols)], gd_out[rc].at[ry, rz], sem.at[count])
        )
        count += 1
    for copy in stores:
        copy.start()
    out = (mid if first else out_in[...]) + dot_nt(hid, wd[...])
    dnormed = dot_nn(dgate, wg[...]) + dot_nn(dupper, wu[...])
    if not first:
        dnormed = dnormed + dn_in[...]
    if last:
        out_ref[...] = out[:, :width].astype(BF16)
        total = jnp.sum(dnormed * unit, 0, keepdims=True)
        dgain_ref[...] = jnp.broadcast_to(total, dgain_ref.shape)
        scaled = dnormed * gain
        dmid_ref[...] = (
            inv * (scaled - unit * (jnp.sum(scaled * unit, -1, keepdims=True) * (1.0 / width))) + xs[...]
        )
    else:
        mid_ref[...] = mid
        out_ref[...] = out
        dn_ref[...] = dnormed
    for copy in stores:
        copy.wait()


def backward_in_kernel(dmid_ref, attn_ref, wo_ref, da_ref, grad_ref):
    dmid_b = dmid_ref[...].astype(BF16)
    da_ref[...] = dot_nn(dmid_b, wo_ref[...]).astype(BF16)
    grad_ref[...] = dot_tn(dmid_b, attn_ref[...]).astype(BF16)


def backward_rest_kernel(plan, place, x_ref, dmid_ref, dgain_ref, go_ref, da_ref, attn_ref, q_ref, k_ref, v_ref,
                         prob_ref, wq_ref, wk_ref, wv_ref, gain_ref, cos_ref, sin_ref, dx_ref, *refs):
    packs, refs = refs[: plan.nc], refs[plan.nc :]
    (dq_ref, dkv_ref, pack, xs, sem) = refs
    width, lanes = plan.width, plan.lanes
    x_at, c_at, z_at, y_at = place[0], place[1], place[2], place[3]
    tokens = xs.shape[0]
    n_seq = tokens // SEQUENCE_LENGTH
    cos = cos_ref[...]
    sin = sin_ref[...]

    def unrotate(block):
        return block * cos - swap_halves(block) * sin

    def one_sequence(n, carry):
        at_rows = pl.ds(pl.multiple_of(n * SEQUENCE_LENGTH, SEQUENCE_LENGTH), SEQUENCE_LENGTH)
        dk = [None] * KEY_VALUE_HEADS
        dv = [None] * KEY_VALUE_HEADS
        for pair in range(lanes // LANES):
            at = slice(pair * LANES, (pair + 1) * LANES)
            q2 = q_ref[at_rows, at]
            da2 = da_ref[at_rows, at]
            prod = da2.astype(F32) * attn_ref[at_rows, at].astype(F32)
            total = None
            for odd in range(2):
                h = pair * 2 + odd
                if h >= QUERY_HEADS:
                    continue
                group = h // (QUERY_HEADS // KEY_VALUE_HEADS)
                kf = head_form(k_ref, at_rows, h)
                vf = head_form(v_ref, at_rows, h)
                p = prob_ref[n, h]
                delta = jnp.sum(lane_half(prod, odd), -1, keepdims=True)
                dp = dot_nt(da2, vf)
                ds = (p.astype(F32) * (dp - delta) * HEAD_SIZE ** (-0.5)).astype(BF16)
                part = dot_nn(ds, kf)
                total = part if total is None else total + part
                dvp = dot_tn(p, lane_half(da2, odd))
                dkp = dot_tn(ds, lane_half(q2, odd))
                dv[group] = dvp if dv[group] is None else dv[group] + dvp
                dk[group] = dkp if dk[group] is None else dk[group] + dkp
            dq_ref[at_rows, at] = unrotate(total).astype(BF16)
        for slot, (parts, turn) in enumerate(((dk, unrotate), (dv, lambda b: b))):
            whole = [g + pltpu.roll(g, HEAD_SIZE, 1) for g in parts]
            for b in range(2):
                block = lane_half(whole[2 * b], 0)
                if 2 * b + 1 < KEY_VALUE_HEADS:
                    block = block + lane_half(whole[2 * b + 1], 1)
                dkv_ref[slot, at_rows, b * LANES : (b + 1) * LANES] = turn(block).astype(BF16)
        return carry

    lax.fori_loop(0, n_seq, one_sequence, 0)
    xs[:, lanes - LANES :] = jnp.zeros((tokens, LANES), F32)
    xs[:, :width] = x_ref[...].astype(F32)
    dq, dk, dv = dq_ref[...], dkv_ref[0], dkv_ref[1]
    xfull = xs[...]
    inv = lax.rsqrt(jnp.sum(xfull * xfull, -1, keepdims=True) * (1.0 / width) + EPS_NORM)
    gain = gain_ref[0:1]
    unit = xfull * inv
    normed = (unit * gain).astype(BF16)
    dnormed = dot_nn(dq, wq_ref[...]) + dot_nn(dk, wk_ref[...]) + dot_nn(dv, wv_ref[...])
    lane = lax.broadcasted_iota(jnp.int32, (1, lanes), 1)
    dnormed = jnp.where(lane < width, dnormed, 0.0)
    dgain = jnp.sum(dnormed * unit, 0, keepdims=True)
    grad_q = dot_tn(dq, normed)
    grad_k = dot_tn(dk, normed)
    grad_v = dot_tn(dv, normed)
    grad_out = go_ref[...].astype(F32)
    at = width - (lanes - LANES)
    row = lax.broadcasted_iota(jnp.int32, (LANES, lanes), 0)
    sheet = jnp.where(row == at, dgain, 0.0) + jnp.where(row == at + 1, dgain_ref[0:1], 0.0)
    side = sheet.T
    grad_q = jnp.concatenate([grad_q[:, : lanes - LANES], grad_q[:, lanes - LANES :] + side], 1)
    rows, krows = plan.out_rows, plan.kv_rows
    for s in range(plan.shards):
        a, b = slice(s * rows, (s + 1) * rows), slice(s * krows, (s + 1) * krows)
        pack[0, s] = jnp.concatenate([grad_q[a], grad_k[b]], 0).astype(BF16)
        pack[1, s] = jnp.concatenate([grad_v[b], grad_out[a]], 0).astype(BF16)
    stores = []
    count = 0
    part_rows = plan.half_rows // plan.nx
    for rc in range(2):
        for rx in range(plan.nx):
            for ry in range(plan.ny):
                for rz in range(plan.nz):
                    shard = (z_at ^ rz) * plan.ny + (y_at + ry) % plan.ny
                    half = (c_at + rc) % 2
                    at = pl.multiple_of((x_at + rx) % plan.nx * part_rows, part_rows)
                    target = packs[rc] if plan.nc == 2 else packs[0].at[rc]
                    stores.append(
                        pltpu.make_async_copy(
                            pack.at[half, shard, pl.ds(at, part_rows)], target.at[rx, ry, rz], sem.at[count]
                        )
                    )
                    count += 1
    for copy in stores:
        copy.start()
    scaled = dnormed * gain
    dx = inv * (scaled - unit * (jnp.sum(scaled * unit, -1, keepdims=True) * (1.0 / width))) + dmid_ref[...]
    dx_ref[...] = dx[:, :width].astype(BF16)
    for copy in stores:
        copy.wait()


VMEM = pl.BlockSpec(memory_space=pltpu.VMEM)
SMEM = pl.BlockSpec(memory_space=pltpu.SMEM)
ANY = pl.BlockSpec(memory_space=pl.ANY)


def shape_of(dims, kind):
    return jax.ShapeDtypeStruct(dims, kind)


def cost(micros):
    return pl.CostEstimate(flops=int(micros * 1e9), transcendentals=0, bytes_accessed=int(micros * 1e6))


def attention_forward(plan, place, tokens, cos, sin, pieces):
    rows, lanes = tokens.shape[0], plan.lanes
    n_seq = rows // SEQUENCE_LENGTH
    return pl.pallas_call(
        functools.partial(attention_forward_kernel, plan, len(pieces) // 2),
        name="attention_forward",
        in_specs=[SMEM, VMEM, VMEM, VMEM] + [ANY] * len(pieces),
        out_specs=[VMEM] * 10,
        out_shape=[
            shape_of((rows, lanes), BF16),
            shape_of((rows, 4 * LANES), BF16),
            shape_of((rows, 4 * LANES), BF16),
            shape_of((rows, lanes), BF16),
            shape_of((n_seq, QUERY_HEADS, SEQUENCE_LENGTH, SEQUENCE_LENGTH), BF16),
            shape_of((lanes, lanes), BF16),
            shape_of((2 * LANES, lanes), BF16),
            shape_of((2 * LANES, lanes), BF16),
            shape_of((lanes, lanes), BF16),
            shape_of((8, lanes), F32),
        ],
        scratch_shapes=[
            pltpu.VMEM((2, plan.shards, plan.half_rows, lanes), BF16),
            pltpu.VMEM((rows, lanes), F32),
            pltpu.SemaphoreType.DMA((len(pieces) * plan.nz,)),
        ],
        cost_estimate=cost(10),
    )(place, tokens, cos, sin, *pieces)


def mlp(plan, place, first, last, cotangent, gain, inputs, gates, downs):
    rows, lanes = cotangent.shape[0], plan.lanes
    units = plan.nc * plan.ff_cols
    ff = shape_of((plan.ny, plan.nz, 2 * plan.ff_rows, lanes), BF16)
    dn = shape_of((plan.ny, plan.nz, plan.out_rows, plan.ff_cols), BF16)
    whole = shape_of((rows, lanes), F32)
    results = [shape_of((rows, plan.width), BF16), whole, shape_of((8, lanes), F32)] if last else [whole] * 3
    return pl.pallas_call(
        functools.partial(mlp_kernel, plan, first, last),
        name="mlp",
        in_specs=[SMEM] + [VMEM] * 5 + [ANY] * (len(gates) + len(downs)),
        out_specs=[VMEM] * 3 + [ANY] * (2 * plan.nc),
        out_shape=results + [ff] * plan.nc + [dn] * plan.nc,
        scratch_shapes=[
            pltpu.VMEM((units, lanes), BF16),
            pltpu.VMEM((units, lanes), BF16),
            pltpu.VMEM((plan.shards, plan.out_rows, units), BF16),
            pltpu.VMEM((lanes, units), BF16),
            pltpu.VMEM((units, lanes), BF16),
            pltpu.VMEM((units, lanes), BF16),
            pltpu.VMEM((plan.shards, plan.out_rows, units), BF16),
            pltpu.VMEM((rows, lanes), F32),
            pltpu.SemaphoreType.DMA((3 * plan.shards * plan.nc,)),
        ],
        cost_estimate=cost(12),
    )(place, cotangent, gain, *inputs, *gates, *downs)


def attention_backward(plan, place, tokens, dmid, dgain, attn, q, k, v, prob, wq, wk, wv, wo, gain, cos, sin):
    rows, lanes = tokens.shape[0], plan.lanes
    da, grad_out = pl.pallas_call(
        backward_in_kernel,
        name="backward_in",
        in_specs=[VMEM] * 3,
        out_specs=[VMEM] * 2,
        out_shape=[shape_of((rows, lanes), BF16), shape_of((lanes, lanes), BF16)],
        cost_estimate=cost(4),
    )(dmid, attn, wo)
    block = (plan.nx, plan.ny, plan.nz, plan.half_rows // plan.nx, lanes)
    if plan.nc == 2:
        packs = [shape_of(block, BF16)] * 2
    else:
        packs = [shape_of((2,) + block, BF16)]
    return pl.pallas_call(
        functools.partial(backward_rest_kernel, plan),
        name="backward_rest",
        in_specs=[SMEM] + [VMEM] * 16,
        out_specs=[VMEM] + [ANY] * len(packs),
        out_shape=[shape_of((rows, plan.width), BF16)] + packs,
        scratch_shapes=[
            pltpu.VMEM((rows, lanes), BF16),
            pltpu.VMEM((2, rows, 2 * LANES), BF16),
            pltpu.VMEM((2, plan.shards, plan.half_rows, lanes), BF16),
            pltpu.VMEM((rows, lanes), F32),
            pltpu.SemaphoreType.DMA((2 * plan.nx * plan.shards,)),
        ],
        cost_estimate=cost(14),
    )(place, tokens, dmid, dgain, grad_out, da, attn, q, k, v, prob, wq, wk, wv, gain, cos, sin)


def shift(plan, dim, amount):
    if dim in "xc":
        axis, outer, inner, first = "dp", plan.nx, plan.nc, dim == "x"
    else:
        axis, outer, inner, first = "fsdp", plan.nz, plan.ny, dim == "z"
    pairs = []
    for o in range(outer):
        for i in range(inner):
            if dim == "z":
                to = (o ^ amount, i)
            else:
                to = ((o + amount) % outer, i) if first else (o, (i + amount) % inner)
            pairs.append((o * inner + i, to[0] * inner + to[1]))
    return axis, pairs


def send(plan, value, dim, amount=1):
    axis, pairs = shift(plan, dim, amount)
    return lax.ppermute(value, axis, pairs)


def spread(plan, piece, dims):
    stack = jnp.stack([piece] + [send(plan, piece, "z", k) for k in range(1, plan.nz)])
    held = {(0, 0, 0): stack}
    for dim in dims:
        at = "cxy".index(dim)
        for place, value in list(held.items()):
            place = list(place)
            place[at] = 1
            held[tuple(place)] = send(plan, value, dim)
    return held


def add(a, b):
    return (a.astype(F32) + b.astype(F32)).astype(BF16)


def reduce_z(plan, stack):
    total = stack[0].astype(F32)
    for k in range(1, plan.nz):
        total = total + send(plan, stack[k], "z", k).astype(F32)
    return total.astype(BF16)


def pad_four(results, nc):
    results = list(results)
    return results if nc == 2 else results[:4] + [None, results[4], None]


def layer(plan, tokens, cotangent, w_query, w_key, w_value, w_out, w_gate, w_up, w_down, gain_attn, gain_mlp):
    cos, sin = rope_tables()
    width, lanes, hidden = plan.width, plan.lanes, plan.hidden
    d_at, s_at = lax.axis_index("dp"), lax.axis_index("fsdp")
    if plan.direct:
        place = jnp.stack([d_at // plan.nc, d_at % plan.nc, s_at // plan.ny, s_at % plan.ny]).astype(jnp.int32)
    else:
        place = jnp.zeros((4,), jnp.int32)

    def widen(rows, extra=None):
        rest = lanes - width
        if extra is None:
            return jnp.pad(rows, ((0, 0), (0, rest)))
        side = jnp.pad(extra, ((0, rows.shape[0] - extra.shape[0]), (0, rest - extra.shape[1])))
        return jnp.concatenate([rows, side], 1)

    def all_rows(w):
        return lax.all_gather(w.T, "fsdp", axis=0, tiled=True)

    if plan.direct:
        gains = jnp.stack([gain_attn, gain_mlp], 1)
        first = widen(jnp.concatenate([w_query.T, w_key.T], 0), gains)
        second = widen(jnp.concatenate([w_value.T, w_out.T], 0))
        own = jnp.where(d_at % plan.nc == 0, first, second)
        gate_own = widen(
            jnp.concatenate(
                [lax.dynamic_slice_in_dim(w, d_at * plan.ff_rows, plan.ff_rows, 1).T for w in (w_gate, w_up)], 0
            )
        )
        down_own = w_down.reshape(plan.shards, plan.parts, plan.ff_rows, plan.out_rows)
        down_own = lax.dynamic_index_in_dim(down_own, d_at, 1, False).reshape(plan.ff_cols, plan.out_rows).T
        held = spread(plan, own, "yc")
        pieces = [held[rc, 0, ry] for rc in range(2) for ry in range(2)]
        held_f = spread(plan, gate_own, "xyc")
        held_d = spread(plan, down_own, "yxc")
        keys = [[(rc, rx, ry) for rc in range(plan.nc) for ry in range(plan.ny)] for rx in range(plan.nx)]
        gates = [[held_f[key] for key in part] for part in keys]
        downs = [[held_d[key] for key in part] for part in keys]
    else:
        gains = jnp.stack(
            [lax.all_gather(g, "fsdp", axis=0, tiled=True) for g in (gain_attn, gain_mlp)], 1
        )
        pieces = [
            widen(jnp.concatenate([all_rows(w_query), all_rows(w_key)], 0), gains)[None],
            widen(jnp.concatenate([all_rows(w_value), all_rows(w_out)], 0))[None],
        ]
        gates = [[widen(jnp.concatenate([all_rows(w_gate), all_rows(w_up)], 0))[None]]]
        downs = [[all_rows(w_down)[None]]]

    q, k, v, attn, prob, wq, wk, wv, wo, gain = attention_forward(plan, place, tokens, cos, sin, pieces)
    carried, grads = (tokens, attn, wo), []
    for i in range(plan.nx):
        *carried, gate_a, gate_b, down_a, down_b = pad_four(
            mlp(plan, place, i == 0, i == plan.nx - 1, cotangent, gain, carried, gates[i], downs[i]), plan.nc
        )
        grads.append(((gate_a, gate_b), (down_a, down_b)))
    output, dmid, dgain = carried
    grad_tokens, *packs = attention_backward(
        plan, place, tokens, dmid, dgain, attn, q, k, v, prob, wq, wk, wv, wo, gain, cos, sin
    )
    rows, krows = plan.out_rows, plan.kv_rows

    if plan.direct:

        def fold(pieces, dims):
            mine = [add(a, send(plan, b, "c")) for a, b in pieces]
            away, keep = mine
            if dims == "xy":
                part = add(keep, send(plan, away, "x"))
                part = add(part[0], send(plan, part[1], "y"))
            else:
                both = jnp.stack([keep[1], away[1]])
                got = send(plan, both, "y")
                part = add(add(keep[0], got[0]), send(plan, add(away[0], got[1]), "x"))
            part = reduce_z(plan, part)
            both = jnp.stack([part, send(plan, part, "x")])
            other = send(plan, both, "c")
            quads = jnp.stack([both, other], 1)
            x_at, c_at = d_at // plan.nc, d_at % plan.nc
            quads = jnp.where(c_at == 0, quads, quads[:, ::-1])
            return jnp.where(x_at == 0, quads[::-1], quads)

        def ff(quads):
            return quads.reshape(plan.parts * plan.ff_rows, lanes)[:, :width].astype(F32).T

        ff_rows = plan.ff_rows

        quads = fold([g[0] for g in grads], "xy")
        grad_gate, grad_up = ff(quads[:, :, :ff_rows]), ff(quads[:, :, ff_rows:])
        quads = fold([g[1] for g in grads], "yx")
        quads = quads.reshape(plan.parts, rows, plan.shards, ff_rows)
        grad_down = quads.transpose(2, 0, 3, 1).reshape(hidden, rows).astype(F32)
        got = send(plan, packs[1], "c")
        there = send(plan, add(packs[0][1], got[1]), "x")
        part = add(add(packs[0][0], got[0]), there)
        part = add(part[0], send(plan, part[1], "y"))
        part = reduce_z(plan, part)
        there = send(plan, part, "x")
        x_at, c_at = d_at // plan.nc, d_at % plan.nc
        both = jnp.where(x_at == 0, jnp.concatenate([part, there], 0), jnp.concatenate([there, part], 0))
        other = send(plan, both, "c")
        one = jnp.where(c_at == 0, both, other).astype(F32)
        two = jnp.where(c_at == 0, other, both).astype(F32)
    else:

        def total(value):
            part = lax.psum_scatter(value.astype(F32), "fsdp", scatter_dimension=0, tiled=True)
            return lax.psum(part, "dp")

        both = grads[0][0][0].reshape(2, hidden, lanes)[:, :, :width]
        grad_gate, grad_up = total(both[0]).T, total(both[1]).T
        grad_down = total(grads[0][1][0].reshape(width, hidden)).T
        whole = packs[0].reshape(2, width + plan.kv, lanes)
        one = jnp.concatenate([total(whole[0, :width]), total(whole[0, width:])], 0)
        two = jnp.concatenate([total(whole[1, : plan.kv]), total(whole[1, plan.kv :])], 0)
        rows, krows = width // plan.fsdp, plan.kv // plan.fsdp
    return (
        output,
        grad_tokens,
        one[:rows, :width].T,
        one[rows:, :width].T,
        two[:krows, :width].T,
        two[krows:, :width].T,
        grad_gate,
        grad_up,
        grad_down,
        one[:rows, width],
        one[:rows, width + 1],
    )


def solution(mesh):
    rows = P(("dp", "fsdp"), None)
    cols = P(None, "fsdp")
    one = P("fsdp")

    def run(*args):
        plan = Plan(mesh, args[0].shape[1], args[8].shape[0])
        step = jax.shard_map(
            functools.partial(layer, plan),
            mesh=mesh,
            in_specs=(rows, rows) + (cols,) * 7 + (one, one),
            out_specs=(rows, rows) + (cols,) * 7 + (one, one),
            check_vma=False,
        )
        return step(*args)

    return run
```

profile of v0, /device:TPU:0, one launch (start us, length us, event | category | flops | bytes accessed | tf_op | source)
XLA Modules:
  0.0 204.5 jit_solution(8807688619514979036)
XLA Ops:
  2.5 5.1 %collective-permute-start.2 = (bf16[96,640]{1,0:T(8,128)(2,1)S(1)}, bf16[96,640]{1,0:T(8,128)(2,1)S(1)}, u32[]{:S(2)}, u32[]{:S(2)}) collective-permute-start(bf16[96,640]{1,0:T(8,128)(2,1)S(1)} %fusion.18), channel_id=1, source_target_pairs={{0,6},{1,7},{2,4},{3,5},{4,2},{5,3},{6,0},{7,1},{8,14},{9,15},{10,... | collective-permute-start | bytes 368648 | tf_op jit(solution)/shard_map/ppermute | solution.py:551
  9.6 2.4 %collective-permute-start.13 = (bf16[72,384]{1,0:T(8,128)(2,1)S(1)}, bf16[72,384]{1,0:T(8,128)(2,1)S(1)}, u32[]{:S(2)}, u32[]{:S(2)}) collective-permute-start(bf16[72,384]{1,0:T(8,128)(2,1)S(1)} %bitcast.129), channel_id=1, source_target_pairs={{0,4},{1,5},{2,6},{3,7},{4,0},{5,1},{6,2},{7,3},{8,12},{9,13},{10,... | collective-permute-start | bytes 165896 | tf_op jit(solution)/shard_map/ppermute | solution.py:551
  12.0 2.0 collective-permute-start.12
  15.7 5.6 %collective-permute-done.1 = bf16[96,640]{1,0:T(8,128)(2,1)S(1)} collective-permute-done((bf16[96,640]{1,0:T(8,128)(2,1)S(1)}, bf16[96,640]{1,0:T(8,128)(2,1)S(1)}, u32[]{:S(2)}, u32[]{:S(2)}) %collective-permute-start.1) | collective-permute-done | bytes 122912 | tf_op jit(solution)/shard_map/ppermute | solution.py:551
  24.0 3.2 %collective-permute-start.7 = (bf16[96,640]{1,0:T(8,128)(2,1)S(1)}, bf16[96,640]{1,0:T(8,128)(2,1)S(1)}, u32[]{:S(2)}, u32[]{:S(2)}) collective-permute-start(bf16[96,640]{1,0:T(8,128)(2,1)S(1)} %get-tuple-element.109), channel_id=1, source_target_pairs={{0,4},{1,5},{2,6},{3,7},{4,0},{5,1},{6,2},{7,3},{8,12},{9,13},{10,... | collective-permute-start | bytes 368648 | tf_op jit(solution)/shard_map/ppermute | solution.py:551
  30.8 3.4 %collective-permute-done.7 = bf16[96,640]{1,0:T(8,128)(2,1)S(1)} collective-permute-done((bf16[96,640]{1,0:T(8,128)(2,1)S(1)}, bf16[96,640]{1,0:T(8,128)(2,1)S(1)}, u32[]{:S(2)}, u32[]{:S(2)}) %collective-permute-start.7) | collective-permute-done | bytes 122912 | tf_op jit(solution)/shard_map/ppermute | solution.py:551
  41.3 9.3 %collective-permute-done.15.refs_8_ = bf16[4,72,384]{2,1,0:T(8,128)(2,1)} collective-permute-done((bf16[4,72,384]{2,1,0:T(8,128)(2,1)S(1)}, bf16[4,72,384]{2,1,0:T(8,128)(2,1)}, u32[]{:S(2)}, u32[]{:S(2)}) %collective-permute-start.15) | collective-permute-done | bytes 221216 | tf_op jit(solution)/shard_map/ppermute | solution.py:551
  52.3 9.5 %attention_forward.1 = (bf16[576,640]{1,0:T(8,128)(2,1)}, bf16[576,512]{1,0:T(8,128)(2,1)}, bf16[576,512]{1,0:T(8,128)(2,1)}, bf16[576,640]{1,0:T(8,128)(2,1)}, ...) custom-call(s32[4]{0:T(128)} %pad_add_fusion.place, ...), custom_call_target="tpu_custom_call" | custom-call | flops 10000000000 | bytes 10000000 | tf_op jit(solution)/shard_map/attention_forward/pallas_call | solution.py:447
  62.9 2.1 %collective-permute-done.19.refs_4_ = bf16[4,96,640]{2,1,0:T(8,128)(2,1)} collective-permute-done((bf16[4,96,640]{2,1,0:T(8,128)(2,1)S(1)}, bf16[4,96,640]{2,1,0:T(8,128)(2,1)}, u32[]{:S(2)}, u32[]{:S(2)}) %collective-permute-start.19) | collective-permute-done | bytes 491552 | tf_op jit(solution)/shard_map/ppermute | solution.py:551
  65.0 13.6 %mlp.2 = (f32[576,640]{1,0:T(8,128)}, f32[576,640]{1,0:T(8,128)}, f32[576,640]{1,0:T(8,128)}, bf16[2,4,96,640]{3,2,1,0:T(8,128)(2,1)}, bf16[2,4,96,640]{3,2,1,0:...) custom-call(s32[4]{0:T(128)} %pad_add_fusion.place, bf16[576,576]{1,0:T(8,128)(2,1)} %dy_ref.3, ...), custom_call_target="tpu_custom_call" | custom-call | flops 12000000000 | bytes 12000000 | tf_op jit(solution)/shard_map/mlp/pallas_call | solution.py:480
  80.2 14.1 %mlp.3 = (bf16[576,576]{1,0:T(8,128)(2,1)}, f32[576,640]{1,0:T(8,128)}, f32[8,640]{1,0:T(8,128)}, bf16[2,4,96,640]{3,2,1,0:T(8,128)(2,1)}, bf16[2,4,96,640]{3,2,...) custom-call(s32[4]{0:T(128)} %pad_add_fusion.place, bf16[576,576]{1,0:T(8,128)(2,1)} %dy_ref.3, ...), custom_call_target="tpu_custom_call" | custom-call | flops 12000000000 | bytes 12000000 | tf_op jit(solution)/shard_map/mlp/pallas_call | solution.py:480
  94.6 4.3 %backward_in.1 = (bf16[576,640]{1,0:T(8,128)(2,1)}, bf16[640,640]{1,0:T(8,128)(2,1)}) custom-call(f32[576,640]{1,0:T(8,128)} %get-tuple-element.47.dmid_ref, bf16[576,640]{1,0:T(8,128)(2,1)} %get-tuple-element.41.refs_1_.attn_ref, bf16[640,640]{1,0:T(8,128)(2,1)} %get-tuple-element.42.refs_2_.wo_ref), custom_call_target="tpu_custom_call" | custom-call | flops 4000000000 | bytes 4000000 | tf_op jit(solution)/shard_map/backward_in/pallas_call | solution.py:503
  100.7 15.6 %backward_rest.1 = (bf16[576,576]{1,0:T(8,128)(2,1)}, bf16[2,2,4,48,640]{4,3,2,1,0:T(8,128)(2,1)}, bf16[2,2,4,48,640]{4,3,2,1,0:T(8,128)(2,1)}) custom-call(s32[4]{0:T(128)} %pad_add_fusion.place, bf16[576,576]{1,0:T(8,128)(2,1)} %x_ref.3, f32[576,640]{1,0:T(8,128)} %get-tuple-element.47.dmid_ref, f32[8,640]{1,0:T(8,128)} %get-tuple-element.48.dgain_ref, ...), custom_call_target="tpu_custom_call" | custom-call | flops 14000000000 | bytes 14000000 | tf_op jit(solution)/shard_map/backward_rest/pallas_call | solution.py:516
  119.3 6.0 %collective-permute-done.46 = bf16[4,72,384]{2,1,0:T(8,128)(2,1)} collective-permute-done((bf16[4,72,384]{2,1,0:T(8,128)(2,1)}, bf16[4,72,384]{2,1,0:T(8,128)(2,1)}, u32[]{:S(2)}, u32[]{:S(2)}) %collective-permute-start.46) | collective-permute-done | bytes 221216 | tf_op jit(solution)/shard_map/ppermute | solution.py:551
  126.5 4.0 %collective-permute-start.47 = (bf16[72,384]{1,0:T(8,128)(2,1)S(1)}, bf16[72,384]{1,0:T(8,128)(2,1)S(1)}, u32[]{:S(2)}, u32[]{:S(2)}) collective-permute-start(bf16[72,384]{1,0:T(8,128)(2,1)S(1)} %get-tuple-element.105), channel_id=1, source_target_pairs={{0,2},{1,3},{2,0},{3,1},{4,6},{5,7},{6,4},{7,5},{8,10},{9,11},{10,... | collective-permute-start | bytes 165896 | tf_op jit(solution)/shard_map/ppermute | solution.py:551
  140.2 8.4 %collective-permute-done.50 = bf16[72,384]{1,0:T(8,128)(2,1)S(1)} collective-permute-done((bf16[72,384]{1,0:T(8,128)(2,1)S(1)}, bf16[72,384]{1,0:T(8,128)(2,1)S(1)}, u32[]{:S(2)}, u32[]{:S(2)}) %collective-permute-start.50) | collective-permute-done | bytes 55328 | tf_op jit(solution)/shard_map/ppermute | solution.py:551
  150.1 7.3 %collective-permute-done.28 = bf16[4,48,640]{2,1,0:T(8,128)(2,1)S(1)} collective-permute-done((bf16[4,48,640]{2,1,0:T(8,128)(2,1)S(1)}, bf16[4,48,640]{2,1,0:T(8,128)(2,1)S(1)}, u32[]{:S(2)}, u32[]{:S(2)}) %collective-permute-start.28) | collective-permute-done | bytes 245792 | tf_op jit(solution)/shard_map/ppermute | solution.py:551
  157.5 2.9 %collective-permute-start.29 = (bf16[48,640]{1,0:T(8,128)(2,1)S(1)}, bf16[48,640]{1,0:T(8,128)(2,1)S(1)}, u32[]{:S(2)}, u32[]{:S(2)}) collective-permute-start(bf16[48,640]{1,0:T(8,128)(2,1)S(1)} %get-tuple-element.102), channel_id=1, source_target_pairs={{0,2},{1,3},{2,0},{3,1},{4,6},{5,7},{6,4},{7,5},{8,10},{9,11},{10,... | collective-permute-start | bytes 184328 | tf_op jit(solution)/shard_map/ppermute | solution.py:551
  161.9 5.8 %collective-permute-done.36 = bf16[2,4,96,640]{3,2,1,0:T(8,128)(2,1)S(1)} collective-permute-done((bf16[2,4,96,640]{3,2,1,0:T(8,128)(2,1)S(1)}, bf16[2,4,96,640]{3,2,1,0:T(8,128)(2,1)S(1)}, u32[]{:S(2)}, u32[]{:S(2)}) %collective-permute-start.36) | collective-permute-done | bytes 983072 | tf_op jit(solution)/shard_map/ppermute | solution.py:551
  174.7 8.3 %collective-permute-done.37 = bf16[4,96,640]{2,1,0:T(8,128)(2,1)S(1)} collective-permute-done((bf16[4,96,640]{2,1,0:T(8,128)(2,1)}, bf16[4,96,640]{2,1,0:T(8,128)(2,1)S(1)}, u32[]{:S(2)}, u32[]{:S(2)}) %collective-permute-start.37) | collective-permute-done | bytes 491552 | tf_op jit(solution)/shard_map/ppermute | solution.py:551
  184.8 1.9 collective-permute-start.39
  187.3 2.1 %collective-permute-done.38 = bf16[96,640]{1,0:T(8,128)(2,1)S(1)} collective-permute-done((bf16[96,640]{1,0:T(8,128)(2,1)S(1)}, bf16[96,640]{1,0:T(8,128)(2,1)S(1)}, u32[]{:S(2)}, u32[]{:S(2)}) %collective-permute-start.38) | collective-permute-done | bytes 122912 | tf_op jit(solution)/shard_map/ppermute | solution.py:551
  191.3 4.6 %collective-permute-done.39 = bf16[96,640]{1,0:T(8,128)(2,1)S(1)} collective-permute-done((bf16[96,640]{1,0:T(8,128)(2,1)S(1)}, bf16[96,640]{1,0:T(8,128)(2,1)S(1)}, u32[]{:S(2)}, u32[]{:S(2)}) %collective-permute-start.39) | collective-permute-done | bytes 122912 | tf_op jit(solution)/shard_map/ppermute | solution.py:551
  197.2 3.7 %collective-permute-done.41 = bf16[96,640]{1,0:T(8,128)(2,1)S(1)} collective-permute-done((bf16[96,640]{1,0:T(8,128)(2,1)S(1)}, bf16[96,640]{1,0:T(8,128)(2,1)S(1)}, u32[]{:S(2)}, u32[]{:S(2)}) %collective-permute-start.41) | collective-permute-done | bytes 122912 | tf_op jit(solution)/shard_map/ppermute | solution.py:551
  (177 shorter events, 57.9 us)
Async XLA Ops:
  7.7 13.7 %collective-permute-start.1 = (bf16[96,640]{1,0:T(8,128)(2,1)S(1)}, bf16[96,640]{1,0:T(8,128)(2,1)S(1)}, u32[]{:S(2)}, u32[]{:S(2)}) collective-permute-start(bf16[96,640]{1,0:T(8,128)(2,1)S(1)} %fusion.18), channel_id=1, source_target_pairs={{0,4},{1,5},{2,6},{3,7},{4,0},{5,1},{6,2},{7,3},{8,12},{9,13},{10,... | collective-permute-start | bytes 368648 | tf_op jit(solution)/shard_map/ppermute | solution.py:551
  7.7 13.7 %collective-permute-start = (bf16[96,640]{1,0:T(8,128)(2,1)S(1)}, bf16[96,640]{1,0:T(8,128)(2,1)S(1)}, u32[]{:S(2)}, u32[]{:S(2)}) collective-permute-start(bf16[96,640]{1,0:T(8,128)(2,1)S(1)} %fusion.18), channel_id=1, source_target_pairs={{0,2},{1,3},{2,0},{3,1},{4,6},{5,7},{6,4},{7,5},{8,10},{9,11},{10,... | collective-permute-start | bytes 368648 | tf_op jit(solution)/shard_map/ppermute | solution.py:551
  9.6 14.4 %collective-permute-start.13 = (bf16[72,384]{1,0:T(8,128)(2,1)S(1)}, bf16[72,384]{1,0:T(8,128)(2,1)S(1)}, u32[]{:S(2)}, u32[]{:S(2)}) collective-permute-start(bf16[72,384]{1,0:T(8,128)(2,1)S(1)} %bitcast.129), channel_id=1, source_target_pairs={{0,4},{1,5},{2,6},{3,7},{4,0},{5,1},{6,2},{7,3},{8,12},{9,13},{10,... | collective-permute-start | bytes 165896 | tf_op jit(solution)/shard_map/ppermute | solution.py:551
  12.0 15.3 %collective-permute-start.12 = (bf16[72,384]{1,0:T(8,128)(2,1)S(1)}, bf16[72,384]{1,0:T(8,128)(2,1)S(1)}, u32[]{:S(2)}, u32[]{:S(2)}) collective-permute-start(bf16[72,384]{1,0:T(8,128)(2,1)S(1)} %bitcast.130), channel_id=1, source_target_pairs={{0,2},{1,3},{2,0},{3,1},{4,6},{5,7},{6,4},{7,5},{8,10},{9,11},{10,... | collective-permute-start | bytes 165896 | tf_op jit(solution)/shard_map/ppermute | solution.py:551
  14.0 14.4 %collective-permute-start.14 = (bf16[72,384]{1,0:T(8,128)(2,1)S(1)}, bf16[72,384]{1,0:T(8,128)(2,1)S(1)}, u32[]{:S(2)}, u32[]{:S(2)}) collective-permute-start(bf16[72,384]{1,0:T(8,128)(2,1)S(1)} %bitcast.131), channel_id=1, source_target_pairs={{0,6},{1,7},{2,4},{3,5},{4,2},{5,3},{6,0},{7,1},{8,14},{9,15},{10,... | collective-permute-start | bytes 165896 | tf_op jit(solution)/shard_map/ppermute | solution.py:551
  21.4 15.0 %collective-permute-start.3 = (bf16[4,96,640]{2,1,0:T(8,128)(2,1)S(1)}, bf16[4,96,640]{2,1,0:T(8,128)(2,1)S(1)}, u32[]{:S(2)}, u32[]{:S(2)}) collective-permute-start(bf16[4,96,640]{2,1,0:T(8,128)(2,1)S(1)} %pad_maximum_fusion.refs_0_), channel_id=1, source_target_pairs={{0,1},{1,0},{2,3},{3,2},{4,5},{5,4},{6,7},{7,6},{8,9},{9,8},{10,11... | collective-permute-start | bytes 1474568 | tf_op jit(solution)/shard_map/ppermute | solution.py:551
  30.8 19.9 %collective-permute-start.4 = (bf16[4,96,640]{2,1,0:T(8,128)(2,1)S(1)}, bf16[4,96,640]{2,1,0:T(8,128)(2,1)S(1)}, u32[]{:S(2)}, u32[]{:S(2)}) collective-permute-start(bf16[4,96,640]{2,1,0:T(8,128)(2,1)S(1)} %pad_maximum_fusion.refs_0_), channel_id=1, source_target_pairs={{0,8},{8,0},{16,24},{24,16},{1,9},{9,1},{17,25},{25,17},{2,10},{10... | collective-permute-start | bytes 1474568 | tf_op jit(solution)/shard_map/ppermute | solution.py:551
  34.3 17.0 %collective-permute-start.18 = (bf16[4,96,640]{2,1,0:T(8,128)(2,1)S(1)}, bf16[4,96,640]{2,1,0:T(8,128)(2,1)S(1)}, u32[]{:S(2)}, u32[]{:S(2)}) collective-permute-start(bf16[4,96,640]{2,1,0:T(8,128)(2,1)S(1)} %pad_maximum_fusion.1.refs_3_), channel_id=1, source_target_pairs={{0,16},{8,24},{16,0},{24,8},{1,17},{9,25},{17,1},{25,9},{2,18},{10... | collective-permute-start | bytes 1474568 | tf_op jit(solution)/shard_map/ppermute | solution.py:551
  35.9 15.6 %collective-permute-start.9 = (bf16[4,96,640]{2,1,0:T(8,128)(2,1)S(1)}, bf16[4,96,640]{2,1,0:T(8,128)(2,1)S(1)}, u32[]{:S(2)}, u32[]{:S(2)}) collective-permute-start(bf16[4,96,640]{2,1,0:T(8,128)(2,1)S(1)} %pad_maximum_fusion.1.refs_3_), channel_id=1, source_target_pairs={{0,1},{1,0},{2,3},{3,2},{4,5},{5,4},{6,7},{7,6},{8,9},{9,8},{10,11... | collective-permute-start | bytes 1474568 | tf_op jit(solution)/shard_map/ppermute | solution.py:551
  36.5 15.8 %collective-permute-start.5 = (bf16[4,96,640]{2,1,0:T(8,128)(2,1)S(1)}, bf16[4,96,640]{2,1,0:T(8,128)(2,1)}, u32[]{:S(2)}, u32[]{:S(2)}) collective-permute-start(bf16[4,96,640]{2,1,0:T(8,128)(2,1)S(1)} %collective-permute-done.3.refs_1_), channel_id=1, source_target_pairs={{0,8},{8,0},{16,24},{24,16},{1,9},{9,1},{17,25},{25,17},{2,10},{10... | collective-permute-start | bytes 1474568 | tf_op jit(solution)/shard_map/ppermute | solution.py:551
  51.5 13.6 %collective-permute-start.19 = (bf16[4,96,640]{2,1,0:T(8,128)(2,1)S(1)}, bf16[4,96,640]{2,1,0:T(8,128)(2,1)}, u32[]{:S(2)}, u32[]{:S(2)}) collective-permute-start(bf16[4,96,640]{2,1,0:T(8,128)(2,1)S(1)} %collective-permute-done.18.refs_3_), channel_id=1, source_target_pairs={{0,1},{1,0},{2,3},{3,2},{4,5},{5,4},{6,7},{7,6},{8,9},{9,8},{10,11... | collective-permute-start | bytes 1474568 | tf_op jit(solution)/shard_map/ppermute | solution.py:551
  52.2 12.8 %collective-permute-start.11 = (bf16[4,96,640]{2,1,0:T(8,128)(2,1)S(1)}, bf16[4,96,640]{2,1,0:T(8,128)(2,1)}, u32[]{:S(2)}, u32[]{:S(2)}) collective-permute-start(bf16[4,96,640]{2,1,0:T(8,128)(2,1)S(1)} %collective-permute-done.9.refs_4_), channel_id=1, source_target_pairs={{0,8},{8,0},{16,24},{24,16},{1,9},{9,1},{17,25},{25,17},{2,10},{10... | collective-permute-start | bytes 1474568 | tf_op jit(solution)/shard_map/ppermute | solution.py:551
  61.9 17.3 %collective-permute-start.24 = (bf16[4,72,384]{2,1,0:T(8,128)(2,1)S(1)}, bf16[4,72,384]{2,1,0:T(8,128)(2,1)S(1)}, u32[]{:S(2)}, u32[]{:S(2)}) collective-permute-start(bf16[4,72,384]{2,1,0:T(8,128)(2,1)S(1)} %collective-permute-done.22.refs_7_), channel_id=1, source_target_pairs={{0,8},{8,0},{16,24},{24,16},{1,9},{9,1},{17,25},{25,17},{2,10},{10... | collective-permute-start | bytes 663560 | tf_op jit(solution)/shard_map/ppermute | solution.py:551
  62.4 16.8 %collective-permute-start.25 = (bf16[4,72,384]{2,1,0:T(8,128)(2,1)}, bf16[4,72,384]{2,1,0:T(8,128)(2,1)}, u32[]{:S(2)}, u32[]{:S(2)}) collective-permute-start(bf16[4,72,384]{2,1,0:T(8,128)(2,1)} %collective-permute-done.23.refs_8_), channel_id=1, source_target_pairs={{0,8},{8,0},{16,24},{24,16},{1,9},{9,1},{17,25},{25,17},{2,10},{10... | collective-permute-start | bytes 663560 | tf_op jit(solution)/shard_map/ppermute | solution.py:551
  62.5 16.7 %collective-permute-start.20 = (bf16[4,96,640]{2,1,0:T(8,128)(2,1)S(1)}, bf16[4,96,640]{2,1,0:T(8,128)(2,1)S(1)}, u32[]{:S(2)}, u32[]{:S(2)}) collective-permute-start(bf16[4,96,640]{2,1,0:T(8,128)(2,1)S(1)} %collective-permute-done.18.refs_3_), channel_id=1, source_target_pairs={{0,8},{8,0},{16,24},{24,16},{1,9},{9,1},{17,25},{25,17},{2,10},{10... | collective-permute-start | bytes 1474568 | tf_op jit(solution)/shard_map/ppermute | solution.py:551
  65.0 14.2 %collective-permute-start.21 = (bf16[4,96,640]{2,1,0:T(8,128)(2,1)}, bf16[4,96,640]{2,1,0:T(8,128)(2,1)S(1)}, u32[]{:S(2)}, u32[]{:S(2)}) collective-permute-start(bf16[4,96,640]{2,1,0:T(8,128)(2,1)} %collective-permute-done.19.refs_4_), channel_id=1, source_target_pairs={{0,8},{8,0},{16,24},{24,16},{1,9},{9,1},{17,25},{25,17},{2,10},{10... | collective-permute-start | bytes 1474568 | tf_op jit(solution)/shard_map/ppermute | solution.py:551
  78.7 15.8 %collective-permute-start.44 = (bf16[2,4,72,384]{3,2,1,0:T(8,128)(2,1)}, bf16[2,4,72,384]{3,2,1,0:T(8,128)(2,1)S(1)}, u32[]{:S(2)}, u32[]{:S(2)}) collective-permute-start(bf16[2,4,72,384]{3,2,1,0:T(8,128)(2,1)} %get-tuple-element.68), channel_id=1, source_target_pairs={{0,8},{8,0},{16,24},{24,16},{1,9},{9,1},{17,25},{25,17},{2,10},{10... | collective-permute-start | bytes 1327112 | tf_op jit(solution)/shard_map/ppermute | solution.py:551
  99.9 16.7 %collective-permute-start.45 = (bf16[2,4,72,384]{3,2,1,0:T(8,128)(2,1)}, bf16[2,4,72,384]{3,2,1,0:T(8,128)(2,1)S(1)}, u32[]{:S(2)}, u32[]{:S(2)}) collective-permute-start(bf16[2,4,72,384]{3,2,1,0:T(8,128)(2,1)} %pad_maximum_fusion.3), channel_id=1, source_target_pairs={{0,1},{1,0},{2,3},{3,2},{4,5},{5,4},{6,7},{7,6},{8,9},{9,8},{10,11... | collective-permute-start | bytes 1327112 | tf_op jit(solution)/shard_map/ppermute | solution.py:551
  116.3 14.8 %collective-permute-start.26 = (bf16[2,2,4,48,640]{4,3,2,1,0:T(8,128)(2,1)}, bf16[2,2,4,48,640]{4,3,2,1,0:T(8,128)(2,1)S(1)}, u32[]{:S(2)}, u32[]{:S(2)}) collective-permute-start(bf16[2,2,4,48,640]{4,3,2,1,0:T(8,128)(2,1)} %get-tuple-element.60), channel_id=1, source_target_pairs={{0,8},{8,0},{16,24},{24,16},{1,9},{9,1},{17,25},{25,17},{2,10},{10... | collective-permute-start | bytes 2949128 | tf_op jit(solution)/shard_map/ppermute | solution.py:551
  118.8 20.4 %collective-permute-start.35 = (bf16[2,4,96,640]{3,2,1,0:T(8,128)(2,1)}, bf16[2,4,96,640]{3,2,1,0:T(8,128)(2,1)S(1)}, u32[]{:S(2)}, u32[]{:S(2)}) collective-permute-start(bf16[2,4,96,640]{3,2,1,0:T(8,128)(2,1)} %get-tuple-element.64), channel_id=1, source_target_pairs={{0,8},{8,0},{16,24},{24,16},{1,9},{9,1},{17,25},{25,17},{2,10},{10... | collective-permute-start | bytes 2949128 | tf_op jit(solution)/shard_map/ppermute | solution.py:551
  119.0 43.0 %collective-permute-start.34 = (bf16[2,4,96,640]{3,2,1,0:T(8,128)(2,1)}, bf16[2,4,96,640]{3,2,1,0:T(8,128)(2,1)S(1)}, u32[]{:S(2)}, u32[]{:S(2)}) collective-permute-start(bf16[2,4,96,640]{3,2,1,0:T(8,128)(2,1)} %get-tuple-element.62), channel_id=1, source_target_pairs={{0,8},{8,0},{16,24},{24,16},{1,9},{9,1},{17,25},{25,17},{2,10},{10... | collective-permute-start | bytes 2949128 | tf_op jit(solution)/shard_map/ppermute | solution.py:551
  133.3 15.5 %collective-permute-start.27 = (bf16[2,4,48,640]{3,2,1,0:T(8,128)(2,1)S(1)}, bf16[2,4,48,640]{3,2,1,0:T(8,128)(2,1)S(1)}, u32[]{:S(2)}, u32[]{:S(2)}) collective-permute-start(bf16[2,4,48,640]{3,2,1,0:T(8,128)(2,1)S(1)} %fusion.3), channel_id=1, source_target_pairs={{0,16},{8,24},{16,0},{24,8},{1,17},{9,25},{17,1},{25,9},{2,18},{10... | collective-permute-start | bytes 1474568 | tf_op jit(solution)/shard_map/ppermute | solution.py:551
  139.5 28.2 %collective-permute-start.36 = (bf16[2,4,96,640]{3,2,1,0:T(8,128)(2,1)S(1)}, bf16[2,4,96,640]{3,2,1,0:T(8,128)(2,1)S(1)}, u32[]{:S(2)}, u32[]{:S(2)}) collective-permute-start(bf16[2,4,96,640]{3,2,1,0:T(8,128)(2,1)S(1)} %add_convert_fusion.1), channel_id=1, source_target_pairs={{0,16},{8,24},{16,0},{24,8},{1,17},{9,25},{17,1},{25,9},{2,18},{10... | collective-permute-start | bytes 2949128 | tf_op jit(solution)/shard_map/ppermute | solution.py:551
  170.4 12.6 %collective-permute-start.37 = (bf16[4,96,640]{2,1,0:T(8,128)(2,1)}, bf16[4,96,640]{2,1,0:T(8,128)(2,1)S(1)}, u32[]{:S(2)}, u32[]{:S(2)}) collective-permute-start(bf16[4,96,640]{2,1,0:T(8,128)(2,1)} %slice_bitcast_fusion), channel_id=1, source_target_pairs={{0,1},{1,0},{2,3},{3,2},{4,5},{5,4},{6,7},{7,6},{8,9},{9,8},{10,11... | collective-permute-start | bytes 1474568 | tf_op jit(solution)/shard_map/ppermute | solution.py:551
  (46 other events, 444.0 us)
where the time goes:
time: 205 us
  waiting for transfers between devices  76.2 us (37%)
  Pallas kernels  57.2 us (28%)
  starting transfers between devices  50.4 us (25%)
  other arithmetic  9.79 us (5%)
  local copies, waits for them, and re-layouts  9.7 us (5%)
    ppermute x52, waiting for transfers between devices, send(): return lax.ppermute(value, axis, pairs)  76.2 us
    ppermute x52, starting transfers between devices, send(): return lax.ppermute(value, axis, pairs)  50.4 us
    pallas_call x2, Pallas kernels, mlp(): pl.pallas_call(functools.partial(mlp_kernel, plan, first, last), name='ml...  27.7 us
    pallas_call x1, Pallas kernels, attention_backward(): pl.pallas_call(functools.partial(backward_rest_kernel, plan), name='backw...  15.6 us
    pallas_call x1, Pallas kernels, attention_forward(): pl.pallas_call(functools.partial(attention_forward_kernel, plan, len(piec...  9.54 us
    pallas_call x1, Pallas kernels, attention_backward(): pl.pallas_call(backward_in_kernel, name='backward_in', in_specs=[VMEM] *...  4.31 us
    convert_element_type x10, other arithmetic, add(): return (a.astype(F32) + b.astype(F32)).astype(BF16)  4.2 us
  transfers between devices with their start and end apart: 52, of which 20 were waited for; matrix products, arithmetic and copies ran while one was open for 6% of the time, Pallas kernels for 28%

commit v1 on v0

--- a/solution.py
+++ b/solution.py
@@ -81,9 +81,8 @@
         self.nz, self.ny = self.fsdp // 2, 2
         s, d = self.fsdp, self.dp
         self.direct = (
-            d % 2 == 0
-            and s % 2 == 0
-            and (s // 2) & (s // 2 - 1) == 0
+            d == 4
+            and s == 8
             and (width // s) % 8 == 0
             and (self.kv // s) % 8 == 0
             and ((width + self.kv) // s) % (16 * (d // 2)) == 0
@@ -104,28 +103,23 @@
         return (self.dp, self.fsdp, self.width, self.hidden)
 
 
-def attention_forward_kernel(plan, n_half, place, x_ref, cos_ref, sin_ref, *refs):
-    pieces, refs = refs[: 2 * n_half], refs[2 * n_half :]
-    (q_ref, k_ref, v_ref, attn_ref, prob_ref, wq_ref, wk_ref, wv_ref, wo_ref, gain_ref, pack, xs, sem) = refs
+def attention_forward_kernel(plan, n_pieces, place, x_ref, cos_ref, sin_ref, *refs):
+    pieces, refs = refs[:n_pieces], refs[n_pieces:]
+    (q_ref, k_ref, v_ref, attn_ref, prob_ref, wq_ref, wk_ref, wv_ref, wo_ref, gain_ref, pack, xs) = refs
     width, lanes, kv = plan.width, plan.lanes, plan.kv
-    c_at, z_at, y_at = place[1], place[2], place[3]
-    copies = []
-    count = 0
-    for at, piece in enumerate(pieces):
-        rc, ry = at // n_half, at % n_half
+    x_at, c_at, z_at, y_at = place[0], place[1], place[2], place[3]
+    part_rows = plan.half_rows // plan.nx
+    spots = [(rc, rx, ry) for rc in range(2) for rx in range(plan.nx) for ry in range(plan.ny)]
+    for (rc, rx, ry), piece in zip(spots, pieces):
         half = (c_at + rc) % 2
+        at = pl.multiple_of((x_at + rx) % plan.nx * part_rows, part_rows)
         for k in range(plan.nz):
             shard = (z_at ^ k) * plan.ny + (y_at + ry) % plan.ny
-            copies.append(pltpu.make_async_copy(piece.at[k], pack.at[half, shard], sem.at[count]))
-            count += 1
-    for copy in copies:
-        copy.start()
+            pack[half, shard, pl.ds(at, part_rows)] = piece[k]
     xs[:, lanes - LANES :] = jnp.zeros((xs.shape[0], LANES), F32)
     xs[:, :width] = x_ref[...].astype(F32)
     xfull = xs[...]
     inv = lax.rsqrt(jnp.sum(xfull * xfull, -1, keepdims=True) * (1.0 / width) + EPS_NORM)
-    for copy in copies:
-        copy.wait()
     rows, krows = plan.out_rows, plan.kv_rows
     qs, ks, vs, os = [], [], [], []
     for s in range(plan.shards):
@@ -217,37 +211,22 @@
         mid_ref, out_ref, dn_ref, refs = refs[0], refs[1], refs[2], refs[3:]
     gg_out, refs = refs[: plan.nc], refs[plan.nc :]
     gd_out, refs = refs[: plan.nc], refs[plan.nc :]
-    (wg, wu, wd3, wd, gg, gu, gd, xs, sem) = refs
+    (wg, wu, wd3, wd, gg, gu, gd, xs) = refs
     width, lanes = plan.width, plan.lanes
     z_at, y_at = place[2], place[3]
     rows, cols = plan.ff_rows, plan.ff_cols
-    loads, late = [], []
-    count = 0
     blocks = [(rc, ry, rz) for rc in range(plan.nc) for ry in range(plan.ny) for rz in range(plan.nz)]
 
     def spot(rc, ry, rz):
         shard = (z_at ^ rz) * plan.ny + (y_at + ry) % plan.ny
-        return shard, pl.multiple_of(rc * cols + shard * rows, rows)
+        return shard, pl.ds(pl.multiple_of(rc * cols + shard * rows, rows), rows)
 
     for rc, ry, rz in blocks:
         shard, at = spot(rc, ry, rz)
         piece = gates[rc * plan.ny + ry]
-        for which, dest in enumerate((wg, wu)):
-            loads.append(
-                pltpu.make_async_copy(
-                    piece.at[rz, pl.ds(which * rows, rows)], dest.at[pl.ds(at, rows)], sem.at[count]
-                )
-            )
-            count += 1
-    for rc, ry, rz in blocks:
-        shard, at = spot(rc, ry, rz)
-        piece = downs[rc * plan.ny + ry]
-        late.append(
-            pltpu.make_async_copy(piece.at[rz], wd3.at[shard, :, pl.ds(rc * cols, cols)], sem.at[count])
-        )
-        count += 1
-    for copy in loads + late:
-        copy.start()
+        wg[at, :] = piece[rz, :rows]
+        wu[at, :] = piece[rz, rows:]
+        wd3[shard, :, rc * cols : (rc + 1) * cols] = downs[rc * plan.ny + ry][rz]
     tokens = xs.shape[0]
     gain = gain_ref[1:2]
     xs[:, lanes - LANES :] = jnp.zeros((tokens, LANES), F32)
@@ -261,12 +240,8 @@
     normed = (unit * gain).astype(BF16)
     xs[:, :width] = dy_ref[...].astype(F32)
     dy = xs[...].astype(BF16)
-    for copy in loads:
-        copy.wait()
     gate = dot_nt(normed, wg[...])
     upper = dot_nt(normed, wu[...])
-    for copy in late:
-        copy.wait()
     units = plan.nc * cols
     wd[width:, :] = jnp.zeros((lanes - width, units), BF16)
     wd[:width, :] = jnp.concatenate([wd3[s].astype(F32) for s in range(plan.shards)], 0).astype(BF16)
@@ -281,23 +256,11 @@
     down = dot_tn(dy, hid)
     for s in range(plan.shards):
         gd[s] = down[s * plan.out_rows : (s + 1) * plan.out_rows].astype(BF16)
-    stores = []
-    count = 0
     for rc, ry, rz in blocks:
         shard, at = spot(rc, ry, rz)
-        for which, grad in enumerate((gg, gu)):
-            stores.append(
-                pltpu.make_async_copy(
-                    grad.at[pl.ds(at, rows)], gg_out[rc].at[ry, rz, pl.ds(which * rows, rows)], sem.at[count]
-                )
-            )
-            count += 1
-        stores.append(
-            pltpu.make_async_copy(gd.at[shard, :, pl.ds(rc * cols, cols)], gd_out[rc].at[ry, rz], sem.at[count])
-        )
-        count += 1
-    for copy in stores:
-        copy.start()
+        gg_out[rc][ry, rz, :rows] = gg[at, :]
+        gg_out[rc][ry, rz, rows:] = gu[at, :]
+        gd_out[rc][ry, rz] = gd[shard, :, rc * cols : (rc + 1) * cols]
     out = (mid if first else out_in[...]) + dot_nt(hid, wd[...])
     dnormed = dot_nn(dgate, wg[...]) + dot_nn(dupper, wu[...])
     if not first:
@@ -314,8 +277,6 @@
         mid_ref[...] = mid
         out_ref[...] = out
         dn_ref[...] = dnormed
-    for copy in stores:
-        copy.wait()
 
 
 def backward_in_kernel(dmid_ref, attn_ref, wo_ref, da_ref, grad_ref):
@@ -327,7 +288,7 @@
 def backward_rest_kernel(plan, place, x_ref, dmid_ref, dgain_ref, go_ref, da_ref, attn_ref, q_ref, k_ref, v_ref,
                          prob_ref, wq_ref, wk_ref, wv_ref, gain_ref, cos_ref, sin_ref, dx_ref, *refs):
     packs, refs = refs[: plan.nc], refs[plan.nc :]
-    (dq_ref, dkv_ref, pack, xs, sem) = refs
+    (dq_ref, dkv_ref, pack, xs) = refs
     width, lanes = plan.width, plan.lanes
     x_at, c_at, z_at, y_at = place[0], place[1], place[2], place[3]
     tokens = xs.shape[0]
@@ -402,39 +363,37 @@
         a, b = slice(s * rows, (s + 1) * rows), slice(s * krows, (s + 1) * krows)
         pack[0, s] = jnp.concatenate([grad_q[a], grad_k[b]], 0).astype(BF16)
         pack[1, s] = jnp.concatenate([grad_v[b], grad_out[a]], 0).astype(BF16)
-    stores = []
-    count = 0
     part_rows = plan.half_rows // plan.nx
     for rc in range(2):
         for rx in range(plan.nx):
             for ry in range(plan.ny):
                 for rz in range(plan.nz):
                     shard = (z_at ^ rz) * plan.ny + (y_at + ry) % plan.ny
-                    half = (c_at + rc) % 2
                     at = pl.multiple_of((x_at + rx) % plan.nx * part_rows, part_rows)
-                    target = packs[rc] if plan.nc == 2 else packs[0].at[rc]
-                    stores.append(
-                        pltpu.make_async_copy(
-                            pack.at[half, shard, pl.ds(at, part_rows)], target.at[rx, ry, rz], sem.at[count]
-                        )
-                    )
-                    count += 1
-    for copy in stores:
-        copy.start()
+                    block = pack[(c_at + rc) % 2, shard, pl.ds(at, part_rows)]
+                    if plan.nc == 2:
+                        packs[rc][rx, ry, rz] = block
+                    else:
+                        packs[0][rc, rx, ry, rz] = block
     scaled = dnormed * gain
     dx = inv * (scaled - unit * (jnp.sum(scaled * unit, -1, keepdims=True) * (1.0 / width))) + dmid_ref[...]
     dx_ref[...] = dx[:, :width].astype(BF16)
-    for copy in stores:
-        copy.wait()
 
 
 VMEM = pl.BlockSpec(memory_space=pltpu.VMEM)
 SMEM = pl.BlockSpec(memory_space=pltpu.SMEM)
-ANY = pl.BlockSpec(memory_space=pl.ANY)
 
 
 def shape_of(dims, kind):
     return jax.ShapeDtypeStruct(dims, kind)
+
+
+def limit(plan, mib):
+    return pltpu.CompilerParams(vmem_limit_bytes=(mib if plan.direct else 60) * 2**20)
+
+
+def kept(plan):
+    return pltpu.VMEM if plan.direct else shape_of
 
 
 def cost(micros):
@@ -444,44 +403,46 @@
 def attention_forward(plan, place, tokens, cos, sin, pieces):
     rows, lanes = tokens.shape[0], plan.lanes
     n_seq = rows // SEQUENCE_LENGTH
+    held = kept(plan)
     return pl.pallas_call(
-        functools.partial(attention_forward_kernel, plan, len(pieces) // 2),
+        functools.partial(attention_forward_kernel, plan, len(pieces)),
         name="attention_forward",
-        in_specs=[SMEM, VMEM, VMEM, VMEM] + [ANY] * len(pieces),
+        in_specs=[SMEM] + [VMEM] * (3 + len(pieces)),
         out_specs=[VMEM] * 10,
         out_shape=[
-            shape_of((rows, lanes), BF16),
-            shape_of((rows, 4 * LANES), BF16),
-            shape_of((rows, 4 * LANES), BF16),
-            shape_of((rows, lanes), BF16),
-            shape_of((n_seq, QUERY_HEADS, SEQUENCE_LENGTH, SEQUENCE_LENGTH), BF16),
-            shape_of((lanes, lanes), BF16),
-            shape_of((2 * LANES, lanes), BF16),
-            shape_of((2 * LANES, lanes), BF16),
-            shape_of((lanes, lanes), BF16),
-            shape_of((8, lanes), F32),
+            held((rows, lanes), BF16),
+            held((rows, 4 * LANES), BF16),
+            held((rows, 4 * LANES), BF16),
+            held((rows, lanes), BF16),
+            held((n_seq, QUERY_HEADS, SEQUENCE_LENGTH, SEQUENCE_LENGTH), BF16),
+            held((lanes, lanes), BF16),
+            held((2 * LANES, lanes), BF16),
+            held((2 * LANES, lanes), BF16),
+            held((lanes, lanes), BF16),
+            held((8, lanes), F32),
         ],
         scratch_shapes=[
             pltpu.VMEM((2, plan.shards, plan.half_rows, lanes), BF16),
             pltpu.VMEM((rows, lanes), F32),
-            pltpu.SemaphoreType.DMA((len(pieces) * plan.nz,)),
         ],
         cost_estimate=cost(10),
+            compiler_params=limit(plan, 12),
     )(place, tokens, cos, sin, *pieces)
 
 
 def mlp(plan, place, first, last, cotangent, gain, inputs, gates, downs):
     rows, lanes = cotangent.shape[0], plan.lanes
+    held = kept(plan)
     units = plan.nc * plan.ff_cols
-    ff = shape_of((plan.ny, plan.nz, 2 * plan.ff_rows, lanes), BF16)
-    dn = shape_of((plan.ny, plan.nz, plan.out_rows, plan.ff_cols), BF16)
-    whole = shape_of((rows, lanes), F32)
-    results = [shape_of((rows, plan.width), BF16), whole, shape_of((8, lanes), F32)] if last else [whole] * 3
+    ff = held((plan.ny, plan.nz, 2 * plan.ff_rows, lanes), BF16)
+    dn = held((plan.ny, plan.nz, plan.out_rows, plan.ff_cols), BF16)
+    whole = held((rows, lanes), F32)
+    results = [shape_of((rows, plan.width), BF16), whole, held((8, lanes), F32)] if last else [whole] * 3
     return pl.pallas_call(
         functools.partial(mlp_kernel, plan, first, last),
         name="mlp",
-        in_specs=[SMEM] + [VMEM] * 5 + [ANY] * (len(gates) + len(downs)),
-        out_specs=[VMEM] * 3 + [ANY] * (2 * plan.nc),
+        in_specs=[SMEM] + [VMEM] * (5 + len(gates) + len(downs)),
+        out_specs=[VMEM] * (3 + 2 * plan.nc),
         out_shape=results + [ff] * plan.nc + [dn] * plan.nc,
         scratch_shapes=[
             pltpu.VMEM((units, lanes), BF16),
@@ -492,41 +453,43 @@
             pltpu.VMEM((units, lanes), BF16),
             pltpu.VMEM((plan.shards, plan.out_rows, units), BF16),
             pltpu.VMEM((rows, lanes), F32),
-            pltpu.SemaphoreType.DMA((3 * plan.shards * plan.nc,)),
         ],
         cost_estimate=cost(12),
+            compiler_params=limit(plan, 24),
     )(place, cotangent, gain, *inputs, *gates, *downs)
 
 
 def attention_backward(plan, place, tokens, dmid, dgain, attn, q, k, v, prob, wq, wk, wv, wo, gain, cos, sin):
     rows, lanes = tokens.shape[0], plan.lanes
+    held = kept(plan)
     da, grad_out = pl.pallas_call(
         backward_in_kernel,
         name="backward_in",
         in_specs=[VMEM] * 3,
         out_specs=[VMEM] * 2,
-        out_shape=[shape_of((rows, lanes), BF16), shape_of((lanes, lanes), BF16)],
+        out_shape=[held((rows, lanes), BF16), held((lanes, lanes), BF16)],
         cost_estimate=cost(4),
+        compiler_params=limit(plan, 6),
     )(dmid, attn, wo)
     block = (plan.nx, plan.ny, plan.nz, plan.half_rows // plan.nx, lanes)
     if plan.nc == 2:
-        packs = [shape_of(block, BF16)] * 2
+        packs = [held(block, BF16)] * 2
     else:
         packs = [shape_of((2,) + block, BF16)]
     return pl.pallas_call(
         functools.partial(backward_rest_kernel, plan),
         name="backward_rest",
         in_specs=[SMEM] + [VMEM] * 16,
-        out_specs=[VMEM] + [ANY] * len(packs),
+        out_specs=[VMEM] * (1 + len(packs)),
         out_shape=[shape_of((rows, plan.width), BF16)] + packs,
         scratch_shapes=[
             pltpu.VMEM((rows, lanes), BF16),
             pltpu.VMEM((2, rows, 2 * LANES), BF16),
             pltpu.VMEM((2, plan.shards, plan.half_rows, lanes), BF16),
             pltpu.VMEM((rows, lanes), F32),
-            pltpu.SemaphoreType.DMA((2 * plan.nx * plan.shards,)),
         ],
         cost_estimate=cost(14),
+        compiler_params=limit(plan, 16),
     )(place, tokens, dmid, dgain, grad_out, da, attn, q, k, v, prob, wq, wk, wv, gain, cos, sin)
 
 
@@ -584,7 +547,11 @@
     width, lanes, hidden = plan.width, plan.lanes, plan.hidden
     d_at, s_at = lax.axis_index("dp"), lax.axis_index("fsdp")
     if plan.direct:
-        place = jnp.stack([d_at // plan.nc, d_at % plan.nc, s_at // plan.ny, s_at % plan.ny]).astype(jnp.int32)
+        x_at, c_at = d_at // plan.nc, d_at % plan.nc
+        place = jnp.stack([x_at, c_at, s_at // plan.ny, s_at % plan.ny]).astype(jnp.int32)
+        place, x_first, c_first, ff_at, d_at, w_query = lax.optimization_barrier(
+            (place, x_at == 0, c_at == 0, d_at * plan.ff_rows, d_at, w_query)
+        )
     else:
         place = jnp.zeros((4,), jnp.int32)
 
@@ -602,16 +569,19 @@
         gains = jnp.stack([gain_attn, gain_mlp], 1)
         first = widen(jnp.concatenate([w_query.T, w_key.T], 0), gains)
         second = widen(jnp.concatenate([w_value.T, w_out.T], 0))
-        own = jnp.where(d_at % plan.nc == 0, first, second)
+        own = jnp.where(c_first, first, second)
+        part_rows = plan.half_rows // plan.nx
+        own = jnp.where(x_first, own[:part_rows], own[part_rows:])
         gate_own = widen(
             jnp.concatenate(
-                [lax.dynamic_slice_in_dim(w, d_at * plan.ff_rows, plan.ff_rows, 1).T for w in (w_gate, w_up)], 0
+                [lax.dynamic_slice_in_dim(w, ff_at, plan.ff_rows, 1).T for w in (w_gate, w_up)], 0
             )
         )
         down_own = w_down.reshape(plan.shards, plan.parts, plan.ff_rows, plan.out_rows)
         down_own = lax.dynamic_index_in_dim(down_own, d_at, 1, False).reshape(plan.ff_cols, plan.out_rows).T
-        held = spread(plan, own, "yc")
-        pieces = [held[rc, 0, ry] for rc in range(2) for ry in range(2)]
+        held_a = spread(plan, own, "yxc")
+        spots = [(rc, rx, ry) for rc in range(plan.nc) for rx in range(plan.nx) for ry in range(plan.ny)]
+        pieces = [held_a[spot] for spot in spots]
         held_f = spread(plan, gate_own, "xyc")
         held_d = spread(plan, down_own, "yxc")
         keys = [[(rc, rx, ry) for rc in range(plan.nc) for ry in range(plan.ny)] for rx in range(plan.nx)]
@@ -657,9 +627,8 @@
             both = jnp.stack([part, send(plan, part, "x")])
             other = send(plan, both, "c")
             quads = jnp.stack([both, other], 1)
-            x_at, c_at = d_at // plan.nc, d_at % plan.nc
-            quads = jnp.where(c_at == 0, quads, quads[:, ::-1])
-            return jnp.where(x_at == 0, quads[::-1], quads)
+            quads = jnp.where(c_first, quads, quads[:, ::-1])
+            return jnp.where(x_first, quads[::-1], quads)
 
         def ff(quads):
             return quads.reshape(plan.parts * plan.ff_rows, lanes)[:, :width].astype(F32).T
@@ -677,11 +646,10 @@
         part = add(part[0], send(plan, part[1], "y"))
         part = reduce_z(plan, part)
         there = send(plan, part, "x")
-        x_at, c_at = d_at // plan.nc, d_at % plan.nc
-        both = jnp.where(x_at == 0, jnp.concatenate([part, there], 0), jnp.concatenate([there, part], 0))
+        both = jnp.where(x_first, jnp.concatenate([part, there], 0), jnp.concatenate([there, part], 0))
         other = send(plan, both, "c")
-        one = jnp.where(c_at == 0, both, other).astype(F32)
-        two = jnp.where(c_at == 0, other, both).astype(F32)
+        one = jnp.where(c_first, both, other).astype(F32)
+        two = jnp.where(c_first, other, both).astype(F32)
     else:
 
         def total(value):

time: 205 us -> 184 us (0.90)
  Pallas kernels: 57.2 us -> 35.9 us
  other arithmetic: 9.79 us -> 5.81 us
  starting transfers between devices: 50.4 us -> 53.9 us
  waiting for transfers between devices: 76.2 us -> 78.8 us
    pallas_call x2, Pallas kernels: 27.7 us -> 18.1 us  [mlp(): pl.pallas_call(functools.partial(mlp_kernel, plan, first, last), name='ml...]
    pallas_call x1, Pallas kernels: 15.6 us -> 10.8 us  [attention_backward(): pl.pallas_call(functools.partial(backward_rest_kernel, plan), name='backw...]
    pallas_call x1, Pallas kernels: 9.54 us -> 5.45 us  [attention_forward(): pl.pallas_call(functools.partial(attention_forward_kernel, plan, len(piec...]
    ppermute x52 -> x56, starting transfers between devices: 50.4 us -> 53.9 us  [send(): return lax.ppermute(value, axis, pairs)]
    pallas_call x1, Pallas kernels: 4.31 us -> 1.55 us  [attention_backward(): pl.pallas_call(backward_in_kernel, name='backward_in', in_specs=[VMEM] *...]
    convert_element_type x10, other arithmetic: 4.2 us -> 1.5 us  [add(): return (a.astype(F32) + b.astype(F32)).astype(BF16)]
    ppermute x52 -> x56, waiting for transfers between devices: 76.2 us -> 78.8 us  [send(): return lax.ppermute(value, axis, pairs)]
  transfers between devices with their start and end apart: 52 -> 56, of which waited for: 20 -> 21; matrix products, arithmetic and copies ran while one was open for 6% -> 5% of each run, Pallas kernels for 28% -> 20%
where the time goes in v1:
time: 184 us
  waiting for transfers between devices  78.8 us (43%)
  starting transfers between devices  53.9 us (29%)
  Pallas kernels  35.9 us (20%)
  local copies, waits for them, and re-layouts  8.09 us (4%)
  other arithmetic  5.81 us (3%)
    ppermute x56, waiting for transfers between devices, send(): return lax.ppermute(value, axis, pairs)  78.8 us
    ppermute x56, starting transfers between devices, send(): return lax.ppermute(value, axis, pairs)  53.9 us
    pallas_call x2, Pallas kernels, mlp(): pl.pallas_call(functools.partial(mlp_kernel, plan, first, last), name='ml...  18.1 us
    pallas_call x1, Pallas kernels, attention_backward(): pl.pallas_call(functools.partial(backward_rest_kernel, plan), name='backw...  10.8 us
    pallas_call x1, Pallas kernels, attention_forward(): pl.pallas_call(functools.partial(attention_forward_kernel, plan, len(piec...  5.45 us
  transfers between devices with their start and end apart: 56, of which 21 were waited for; matrix products, arithmetic and copies ran while one was open for 5% of the time, Pallas kernels for 20%

profile of v1, /device:TPU:0, one launch (start us, length us, event | category | flops | bytes accessed | tf_op | source)
XLA Modules:
  0.0 183.7 jit_solution(13590743680266542716)
XLA Ops:
  2.7 4.1 %collective-permute-start.1 = (bf16[48,640]{1,0:T(8,128)(2,1)S(1)}, bf16[48,640]{1,0:T(8,128)(2,1)S(1)}, u32[]{:S(2)}, u32[]{:S(2)}) collective-permute-start(bf16[48,640]{1,0:T(8,128)(2,1)S(1)} %slice_select_fusion), channel_id=1, source_target_pairs={{0,4},{1,5},{2,6},{3,7},{4,0},{5,1},{6,2},{7,3},{8,12},{9,13},{10,... | collective-permute-start | bytes 184328 | tf_op jit(solution)/shard_map/ppermute | solution.py:514
  10.3 3.5 %collective-permute-start.11 = (bf16[96,640]{1,0:T(8,128)(2,1)S(1)}, bf16[96,640]{1,0:T(8,128)(2,1)S(1)}, u32[]{:S(2)}, u32[]{:S(2)}) collective-permute-start(bf16[96,640]{1,0:T(8,128)(2,1)S(1)} %get-tuple-element.121), channel_id=1, source_target_pairs={{0,4},{1,5},{2,6},{3,7},{4,0},{5,1},{6,2},{7,3},{8,12},{9,13},{10,... | collective-permute-start | bytes 368648 | tf_op jit(solution)/shard_map/ppermute | solution.py:514
  15.8 3.8 %collective-permute-start.18 = (bf16[72,384]{1,0:T(8,128)(2,1)S(1)}, bf16[72,384]{1,0:T(8,128)(2,1)S(1)}, u32[]{:S(2)}, u32[]{:S(2)}) collective-permute-start(bf16[72,384]{1,0:T(8,128)(2,1)S(1)} %bitcast.131), channel_id=1, source_target_pairs={{0,6},{1,7},{2,4},{3,5},{4,2},{5,3},{6,0},{7,1},{8,14},{9,15},{10,... | collective-permute-start | bytes 165896 | tf_op jit(solution)/shard_map/ppermute | solution.py:514
  19.7 3.9 %collective-permute-done.17 = bf16[72,384]{1,0:T(8,128)(2,1)S(1)} collective-permute-done((bf16[72,384]{1,0:T(8,128)(2,1)S(1)}, bf16[72,384]{1,0:T(8,128)(2,1)S(1)}, u32[]{:S(2)}, u32[]{:S(2)}) %collective-permute-start.17) | collective-permute-done | bytes 55328 | tf_op jit(solution)/shard_map/ppermute | solution.py:514
  23.5 2.8 %collective-permute-start.12 = (bf16[96,640]{1,0:T(8,128)(2,1)S(1)}, bf16[96,640]{1,0:T(8,128)(2,1)S(1)}, u32[]{:S(2)}, u32[]{:S(2)}) collective-permute-start(bf16[96,640]{1,0:T(8,128)(2,1)S(1)} %get-tuple-element.121), channel_id=1, source_target_pairs={{0,6},{1,7},{2,4},{3,5},{4,2},{5,3},{6,0},{7,1},{8,14},{9,15},{10,... | collective-permute-start | bytes 368648 | tf_op jit(solution)/shard_map/ppermute | solution.py:514
  31.8 3.2 %collective-permute-done.26.refs_7_ = bf16[4,72,384]{2,1,0:T(8,128)(2,1)S(1)} collective-permute-done((bf16[4,72,384]{2,1,0:T(8,128)(2,1)S(1)}, bf16[4,72,384]{2,1,0:T(8,128)(2,1)S(1)}, u32[]{:S(2)}, u32[]{:S(2)}) %collective-permute-start.26) | collective-permute-done | bytes 221216 | tf_op jit(solution)/shard_map/ppermute | solution.py:514
  35.0 2.4 %collective-permute-start.22 = (bf16[4,96,640]{2,1,0:T(8,128)(2,1)S(1)}, bf16[4,96,640]{2,1,0:T(8,128)(2,1)S(1)}, u32[]{:S(2)}, u32[]{:S(2)}) collective-permute-start(bf16[4,96,640]{2,1,0:T(8,128)(2,1)S(1)} %pad_maximum_fusion.refs_3_), channel_id=1, source_target_pairs={{0,16},{8,24},{16,0},{24,8},{1,17},{9,25},{17,1},{25,9},{2,18},{10... | collective-permute-start | bytes 1474568 | tf_op jit(solution)/shard_map/ppermute | solution.py:514
  40.8 14.2 %collective-permute-done.5.refs_3_ = bf16[4,48,640]{2,1,0:T(8,128)(2,1)S(1)} collective-permute-done((bf16[4,48,640]{2,1,0:T(8,128)(2,1)S(1)}, bf16[4,48,640]{2,1,0:T(8,128)(2,1)S(1)}, u32[]{:S(2)}, u32[]{:S(2)}) %collective-permute-start.5) | collective-permute-done | bytes 245792 | tf_op jit(solution)/shard_map/ppermute | solution.py:514
  57.7 5.5 %attention_forward.1 = (bf16[576,640]{1,0:T(8,128)(2,1)S(1)}, bf16[576,512]{1,0:T(8,128)(2,1)S(1)}, bf16[576,512]{1,0:T(8,128)(2,1)S(1)}, bf16[576,640]{1,0:T(8,...) custom-call(s32[4]{0:T(128)S(1)} %pad_add_fusion.place, ...), custom_call_target="tpu_custom_call" | custom-call | flops 10000000000 | bytes 10000000 | tf_op jit(solution)/shard_map/attention_forward/pallas_call | solution.py:407
  64.1 6.5 %collective-permute-done.23.refs_4_ = bf16[4,96,640]{2,1,0:T(8,128)(2,1)S(1)} collective-permute-done((bf16[4,96,640]{2,1,0:T(8,128)(2,1)S(1)}, bf16[4,96,640]{2,1,0:T(8,128)(2,1)S(1)}, u32[]{:S(2)}, u32[]{:S(2)}) %collective-permute-start.23) | collective-permute-done | bytes 491552 | tf_op jit(solution)/shard_map/ppermute | solution.py:514
  70.6 9.1 %mlp.2 = (f32[576,640]{1,0:T(8,128)S(1)}, f32[576,640]{1,0:T(8,128)S(1)}, f32[576,640]{1,0:T(8,128)S(1)}, bf16[2,4,96,640]{3,2,1,0:T(8,128)(2,1)S(1)}, bf16[2,4,...) custom-call(s32[4]{0:T(128)S(1)} %pad_add_fusion.place, ...), custom_call_target="tpu_custom_call" | custom-call | flops 12000000000 | bytes 12000000 | tf_op jit(solution)/shard_map/mlp/pallas_call | solution.py:441
  80.3 9.1 %mlp.3 = (bf16[576,576]{1,0:T(8,128)(2,1)}, f32[576,640]{1,0:T(8,128)S(1)}, f32[8,640]{1,0:T(8,128)S(1)}, bf16[2,4,96,640]{3,2,1,0:T(8,128)(2,1)S(1)}, bf16[2,4,...) custom-call(s32[4]{0:T(128)S(1)} %pad_add_fusion.place, ...), custom_call_target="tpu_custom_call" | custom-call | flops 12000000000 | bytes 12000000 | tf_op jit(solution)/shard_map/mlp/pallas_call | solution.py:441
  92.0 10.8 %backward_rest.1 = (bf16[576,576]{1,0:T(8,128)(2,1)}, bf16[2,2,4,48,640]{4,3,2,1,0:T(8,128)(2,1)S(1)}, bf16[2,2,4,48,640]{4,3,2,1,0:T(8,128)(2,1)S(1)}) custom-call(s32[4]{0:T(128)S(1)} %pad_add_fusion.place, bf16[576,576]{1,0:T(8,128)(2,1)S(1)} %copy-done.1, f32[576,640]{1,0:T(8,128)S(1)} %get-tuple-element.59.dmid_ref, ...), custom_call_target="tpu_custom_call" | custom-call | flops 14000000000 | bytes 14000000 | tf_op jit(solution)/shard_map/backward_rest/pallas_call | solution.py:479
  105.2 5.9 %collective-permute-done.50 = bf16[4,72,384]{2,1,0:T(8,128)(2,1)S(1)} collective-permute-done((bf16[4,72,384]{2,1,0:T(8,128)(2,1)S(1)}, bf16[4,72,384]{2,1,0:T(8,128)(2,1)S(1)}, u32[]{:S(2)}, u32[]{:S(2)}) %collective-permute-start.50) | collective-permute-done | bytes 221216 | tf_op jit(solution)/shard_map/ppermute | solution.py:514
  112.3 2.4 %collective-permute-start.52 = (bf16[72,384]{1,0:T(8,128)(2,1)S(1)}, bf16[72,384]{1,0:T(8,128)(2,1)S(1)}, u32[]{:S(2)}, u32[]{:S(2)}) collective-permute-start(bf16[72,384]{1,0:T(8,128)(2,1)S(1)} %get-tuple-element.119), channel_id=1, source_target_pairs={{0,4},{1,5},{2,6},{3,7},{4,0},{5,1},{6,2},{7,3},{8,12},{9,13},{10,... | collective-permute-start | bytes 165896 | tf_op jit(solution)/shard_map/ppermute | solution.py:514
  121.1 9.9 %collective-permute-done.54 = bf16[72,384]{1,0:T(8,128)(2,1)S(1)} collective-permute-done((bf16[72,384]{1,0:T(8,128)(2,1)S(1)}, bf16[72,384]{1,0:T(8,128)(2,1)S(1)}, u32[]{:S(2)}, u32[]{:S(2)}) %collective-permute-start.54) | collective-permute-done | bytes 55328 | tf_op jit(solution)/shard_map/ppermute | solution.py:514
  133.2 6.6 %collective-permute-done.32 = bf16[4,48,640]{2,1,0:T(8,128)(2,1)S(1)} collective-permute-done((bf16[4,48,640]{2,1,0:T(8,128)(2,1)S(1)}, bf16[4,48,640]{2,1,0:T(8,128)(2,1)S(1)}, u32[]{:S(2)}, u32[]{:S(2)}) %collective-permute-start.32) | collective-permute-done | bytes 245792 | tf_op jit(solution)/shard_map/ppermute | solution.py:514
  141.1 2.2 %collective-permute-start.34 = (bf16[48,640]{1,0:T(8,128)(2,1)S(1)}, bf16[48,640]{1,0:T(8,128)(2,1)S(1)}, u32[]{:S(2)}, u32[]{:S(2)}) collective-permute-start(bf16[48,640]{1,0:T(8,128)(2,1)S(1)} %get-tuple-element.116), channel_id=1, source_target_pairs={{0,4},{1,5},{2,6},{3,7},{4,0},{5,1},{6,2},{7,3},{8,12},{9,13},{10,... | collective-permute-start | bytes 184328 | tf_op jit(solution)/shard_map/ppermute | solution.py:514
  143.4 5.0 %collective-permute-done.40 = bf16[2,4,96,640]{3,2,1,0:T(8,128)(2,1)S(1)} collective-permute-done((bf16[2,4,96,640]{3,2,1,0:T(8,128)(2,1)S(1)}, bf16[2,4,96,640]{3,2,1,0:T(8,128)(2,1)S(1)}, u32[]{:S(2)}, u32[]{:S(2)}) %collective-permute-start.40) | collective-permute-done | bytes 983072 | tf_op jit(solution)/shard_map/ppermute | solution.py:514
  150.2 1.9 %collective-permute-start.41 = (bf16[4,96,640]{2,1,0:T(8,128)(2,1)}, bf16[4,96,640]{2,1,0:T(8,128)(2,1)S(1)}, u32[]{:S(2)}, u32[]{:S(2)}) collective-permute-start(bf16[4,96,640]{2,1,0:T(8,128)(2,1)} %slice_bitcast_fusion), channel_id=1, source_target_pairs={{0,1},{1,0},{2,3},{3,2},{4,5},{5,4},{6,7},{7,6},{8,9},{9,8},{10,11... | collective-permute-start | bytes 1474568 | tf_op jit(solution)/shard_map/ppermute | solution.py:514
  155.3 6.8 %collective-permute-done.41 = bf16[4,96,640]{2,1,0:T(8,128)(2,1)S(1)} collective-permute-done((bf16[4,96,640]{2,1,0:T(8,128)(2,1)}, bf16[4,96,640]{2,1,0:T(8,128)(2,1)S(1)}, u32[]{:S(2)}, u32[]{:S(2)}) %collective-permute-start.41) | collective-permute-done | bytes 491552 | tf_op jit(solution)/shard_map/ppermute | solution.py:514
  166.5 2.6 %collective-permute-done.42 = bf16[96,640]{1,0:T(8,128)(2,1)S(1)} collective-permute-done((bf16[96,640]{1,0:T(8,128)(2,1)S(1)}, bf16[96,640]{1,0:T(8,128)(2,1)S(1)}, u32[]{:S(2)}, u32[]{:S(2)}) %collective-permute-start.42) | collective-permute-done | bytes 122912 | tf_op jit(solution)/shard_map/ppermute | solution.py:514
  170.8 4.2 %collective-permute-done.43 = bf16[96,640]{1,0:T(8,128)(2,1)S(1)} collective-permute-done((bf16[96,640]{1,0:T(8,128)(2,1)S(1)}, bf16[96,640]{1,0:T(8,128)(2,1)S(1)}, u32[]{:S(2)}, u32[]{:S(2)}) %collective-permute-start.43) | collective-permute-done | bytes 122912 | tf_op jit(solution)/shard_map/ppermute | solution.py:514
  177.3 2.7 %collective-permute-done.45 = bf16[96,640]{1,0:T(8,128)(2,1)S(1)} collective-permute-done((bf16[96,640]{1,0:T(8,128)(2,1)S(1)}, bf16[96,640]{1,0:T(8,128)(2,1)S(1)}, u32[]{:S(2)}, u32[]{:S(2)}) %collective-permute-start.45) | collective-permute-done | bytes 122912 | tf_op jit(solution)/shard_map/ppermute | solution.py:514
  (159 shorter events, 53.5 us)
Async XLA Ops:
  2.7 12.5 %collective-permute-start.1 = (bf16[48,640]{1,0:T(8,128)(2,1)S(1)}, bf16[48,640]{1,0:T(8,128)(2,1)S(1)}, u32[]{:S(2)}, u32[]{:S(2)}) collective-permute-start(bf16[48,640]{1,0:T(8,128)(2,1)S(1)} %slice_select_fusion), channel_id=1, source_target_pairs={{0,4},{1,5},{2,6},{3,7},{4,0},{5,1},{6,2},{7,3},{8,12},{9,13},{10,... | collective-permute-start | bytes 184328 | tf_op jit(solution)/shard_map/ppermute | solution.py:514
  9.4 20.1 %collective-permute-start.10 = (bf16[96,640]{1,0:T(8,128)(2,1)S(1)}, bf16[96,640]{1,0:T(8,128)(2,1)S(1)}, u32[]{:S(2)}, u32[]{:S(2)}) collective-permute-start(bf16[96,640]{1,0:T(8,128)(2,1)S(1)} %get-tuple-element.121), channel_id=1, source_target_pairs={{0,2},{1,3},{2,0},{3,1},{4,6},{5,7},{6,4},{7,5},{8,10},{9,11},{10,... | collective-permute-start | bytes 368648 | tf_op jit(solution)/shard_map/ppermute | solution.py:514
  10.3 19.1 %collective-permute-start.11 = (bf16[96,640]{1,0:T(8,128)(2,1)S(1)}, bf16[96,640]{1,0:T(8,128)(2,1)S(1)}, u32[]{:S(2)}, u32[]{:S(2)}) collective-permute-start(bf16[96,640]{1,0:T(8,128)(2,1)S(1)} %get-tuple-element.121), channel_id=1, source_target_pairs={{0,4},{1,5},{2,6},{3,7},{4,0},{5,1},{6,2},{7,3},{8,12},{9,13},{10,... | collective-permute-start | bytes 368648 | tf_op jit(solution)/shard_map/ppermute | solution.py:514
  15.2 11.1 %collective-permute-start.16 = (bf16[72,384]{1,0:T(8,128)(2,1)S(1)}, bf16[72,384]{1,0:T(8,128)(2,1)S(1)}, u32[]{:S(2)}, u32[]{:S(2)}) collective-permute-start(bf16[72,384]{1,0:T(8,128)(2,1)S(1)} %bitcast.130), channel_id=1, source_target_pairs={{0,2},{1,3},{2,0},{3,1},{4,6},{5,7},{6,4},{7,5},{8,10},{9,11},{10,... | collective-permute-start | bytes 165896 | tf_op jit(solution)/shard_map/ppermute | solution.py:514
  15.8 12.0 %collective-permute-start.18 = (bf16[72,384]{1,0:T(8,128)(2,1)S(1)}, bf16[72,384]{1,0:T(8,128)(2,1)S(1)}, u32[]{:S(2)}, u32[]{:S(2)}) collective-permute-start(bf16[72,384]{1,0:T(8,128)(2,1)S(1)} %bitcast.131), channel_id=1, source_target_pairs={{0,6},{1,7},{2,4},{3,5},{4,2},{5,3},{6,0},{7,1},{8,14},{9,15},{10,... | collective-permute-start | bytes 165896 | tf_op jit(solution)/shard_map/ppermute | solution.py:514
  26.3 12.5 %collective-permute-start.3 = (bf16[4,48,640]{2,1,0:T(8,128)(2,1)S(1)}, bf16[4,48,640]{2,1,0:T(8,128)(2,1)S(1)}, u32[]{:S(2)}, u32[]{:S(2)}) collective-permute-start(bf16[4,48,640]{2,1,0:T(8,128)(2,1)S(1)} %pad_maximum_fusion.3.refs_0_), channel_id=1, source_target_pairs={{0,1},{1,0},{2,3},{3,2},{4,5},{5,4},{6,7},{7,6},{8,9},{9,8},{10,11... | collective-permute-start | bytes 737288 | tf_op jit(solution)/shard_map/ppermute | solution.py:514
  35.0 22.0 %collective-permute-start.22 = (bf16[4,96,640]{2,1,0:T(8,128)(2,1)S(1)}, bf16[4,96,640]{2,1,0:T(8,128)(2,1)S(1)}, u32[]{:S(2)}, u32[]{:S(2)}) collective-permute-start(bf16[4,96,640]{2,1,0:T(8,128)(2,1)S(1)} %pad_maximum_fusion.refs_3_), channel_id=1, source_target_pairs={{0,16},{8,24},{16,0},{24,8},{1,17},{9,25},{17,1},{25,9},{2,18},{10... | collective-permute-start | bytes 1474568 | tf_op jit(solution)/shard_map/ppermute | solution.py:514
  37.4 19.5 %collective-permute-start.13 = (bf16[4,96,640]{2,1,0:T(8,128)(2,1)S(1)}, bf16[4,96,640]{2,1,0:T(8,128)(2,1)S(1)}, u32[]{:S(2)}, u32[]{:S(2)}) collective-permute-start(bf16[4,96,640]{2,1,0:T(8,128)(2,1)S(1)} %pad_maximum_fusion.refs_3_), channel_id=1, source_target_pairs={{0,1},{1,0},{2,3},{3,2},{4,5},{5,4},{6,7},{7,6},{8,9},{9,8},{10,11... | collective-permute-start | bytes 1474568 | tf_op jit(solution)/shard_map/ppermute | solution.py:514
  38.8 16.2 %collective-permute-start.5 = (bf16[4,48,640]{2,1,0:T(8,128)(2,1)S(1)}, bf16[4,48,640]{2,1,0:T(8,128)(2,1)S(1)}, u32[]{:S(2)}, u32[]{:S(2)}) collective-permute-start(bf16[4,48,640]{2,1,0:T(8,128)(2,1)S(1)} %collective-permute-done.3.refs_1_), channel_id=1, source_target_pairs={{0,16},{8,24},{16,0},{24,8},{1,17},{9,25},{17,1},{25,9},{2,18},{10... | collective-permute-start | bytes 737288 | tf_op jit(solution)/shard_map/ppermute | solution.py:514
  40.3 14.7 %collective-permute-start.8 = (bf16[4,48,640]{2,1,0:T(8,128)(2,1)S(1)}, bf16[4,48,640]{2,1,0:T(8,128)(2,1)S(1)}, u32[]{:S(2)}, u32[]{:S(2)}) collective-permute-start(bf16[4,48,640]{2,1,0:T(8,128)(2,1)S(1)} %collective-permute-done.4.refs_2_), channel_id=1, source_target_pairs={{0,8},{8,0},{16,24},{24,16},{1,9},{9,1},{17,25},{25,17},{2,10},{10... | collective-permute-start | bytes 737288 | tf_op jit(solution)/shard_map/ppermute | solution.py:514
  40.3 15.2 %collective-permute-start.7 = (bf16[4,48,640]{2,1,0:T(8,128)(2,1)S(1)}, bf16[4,48,640]{2,1,0:T(8,128)(2,1)S(1)}, u32[]{:S(2)}, u32[]{:S(2)}) collective-permute-start(bf16[4,48,640]{2,1,0:T(8,128)(2,1)S(1)} %collective-permute-done.3.refs_1_), channel_id=1, source_target_pairs={{0,8},{8,0},{16,24},{24,16},{1,9},{9,1},{17,25},{25,17},{2,10},{10... | collective-permute-start | bytes 737288 | tf_op jit(solution)/shard_map/ppermute | solution.py:514
  57.0 13.6 %collective-permute-start.23 = (bf16[4,96,640]{2,1,0:T(8,128)(2,1)S(1)}, bf16[4,96,640]{2,1,0:T(8,128)(2,1)S(1)}, u32[]{:S(2)}, u32[]{:S(2)}) collective-permute-start(bf16[4,96,640]{2,1,0:T(8,128)(2,1)S(1)} %collective-permute-done.22.refs_3_), channel_id=1, source_target_pairs={{0,1},{1,0},{2,3},{3,2},{4,5},{5,4},{6,7},{7,6},{8,9},{9,8},{10,11... | collective-permute-start | bytes 1474568 | tf_op jit(solution)/shard_map/ppermute | solution.py:514
  57.5 13.1 %collective-permute-start.15 = (bf16[4,96,640]{2,1,0:T(8,128)(2,1)S(1)}, bf16[4,96,640]{2,1,0:T(8,128)(2,1)S(1)}, u32[]{:S(2)}, u32[]{:S(2)}) collective-permute-start(bf16[4,96,640]{2,1,0:T(8,128)(2,1)S(1)} %collective-permute-done.13.refs_4_), channel_id=1, source_target_pairs={{0,8},{8,0},{16,24},{24,16},{1,9},{9,1},{17,25},{25,17},{2,10},{10... | collective-permute-start | bytes 1474568 | tf_op jit(solution)/shard_map/ppermute | solution.py:514
  63.2 17.1 %collective-permute-start.28 = (bf16[4,72,384]{2,1,0:T(8,128)(2,1)S(1)}, bf16[4,72,384]{2,1,0:T(8,128)(2,1)S(1)}, u32[]{:S(2)}, u32[]{:S(2)}) collective-permute-start(bf16[4,72,384]{2,1,0:T(8,128)(2,1)S(1)} %collective-permute-done.26.refs_7_), channel_id=1, source_target_pairs={{0,8},{8,0},{16,24},{24,16},{1,9},{9,1},{17,25},{25,17},{2,10},{10... | collective-permute-start | bytes 663560 | tf_op jit(solution)/shard_map/ppermute | solution.py:514
  63.6 16.7 %collective-permute-start.29 = (bf16[4,72,384]{2,1,0:T(8,128)(2,1)S(1)}, bf16[4,72,384]{2,1,0:T(8,128)(2,1)S(1)}, u32[]{:S(2)}, u32[]{:S(2)}) collective-permute-start(bf16[4,72,384]{2,1,0:T(8,128)(2,1)S(1)} %collective-permute-done.27.refs_8_), channel_id=1, source_target_pairs={{0,8},{8,0},{16,24},{24,16},{1,9},{9,1},{17,25},{25,17},{2,10},{10... | collective-permute-start | bytes 663560 | tf_op jit(solution)/shard_map/ppermute | solution.py:514
  63.8 16.5 %collective-permute-start.24 = (bf16[4,96,640]{2,1,0:T(8,128)(2,1)S(1)}, bf16[4,96,640]{2,1,0:T(8,128)(2,1)S(1)}, u32[]{:S(2)}, u32[]{:S(2)}) collective-permute-start(bf16[4,96,640]{2,1,0:T(8,128)(2,1)S(1)} %collective-permute-done.22.refs_3_), channel_id=1, source_target_pairs={{0,8},{8,0},{16,24},{24,16},{1,9},{9,1},{17,25},{25,17},{2,10},{10... | collective-permute-start | bytes 1474568 | tf_op jit(solution)/shard_map/ppermute | solution.py:514
  91.4 12.6 %collective-permute-start.49 = (bf16[2,4,72,384]{3,2,1,0:T(8,128)(2,1)S(1)}, bf16[2,4,72,384]{3,2,1,0:T(8,128)(2,1)S(1)}, u32[]{:S(2)}, u32[]{:S(2)}) collective-permute-start(bf16[2,4,72,384]{3,2,1,0:T(8,128)(2,1)S(1)} %pad_maximum_fusion.2), channel_id=1, source_target_pairs={{0,1},{1,0},{2,3},{3,2},{4,5},{5,4},{6,7},{7,6},{8,9},{9,8},{10,11... | collective-permute-start | bytes 1327112 | tf_op jit(solution)/shard_map/ppermute | solution.py:514
  104.7 14.6 %collective-permute-start.39 = (bf16[2,4,96,640]{3,2,1,0:T(8,128)(2,1)S(1)}, bf16[2,4,96,640]{3,2,1,0:T(8,128)(2,1)S(1)}, u32[]{:S(2)}, u32[]{:S(2)}) collective-permute-start(bf16[2,4,96,640]{3,2,1,0:T(8,128)(2,1)S(1)} %get-tuple-element.76), channel_id=1, source_target_pairs={{0,8},{8,0},{16,24},{24,16},{1,9},{9,1},{17,25},{25,17},{2,10},{10... | collective-permute-start | bytes 2949128 | tf_op jit(solution)/shard_map/ppermute | solution.py:514
  104.7 38.7 %collective-permute-start.38 = (bf16[2,4,96,640]{3,2,1,0:T(8,128)(2,1)S(1)}, bf16[2,4,96,640]{3,2,1,0:T(8,128)(2,1)S(1)}, u32[]{:S(2)}, u32[]{:S(2)}) collective-permute-start(bf16[2,4,96,640]{3,2,1,0:T(8,128)(2,1)S(1)} %get-tuple-element.74), channel_id=1, source_target_pairs={{0,8},{8,0},{16,24},{24,16},{1,9},{9,1},{17,25},{25,17},{2,10},{10... | collective-permute-start | bytes 2949128 | tf_op jit(solution)/shard_map/ppermute | solution.py:514
  115.7 15.4 %collective-permute-start.31 = (bf16[2,4,48,640]{3,2,1,0:T(8,128)(2,1)S(1)}, bf16[2,4,48,640]{3,2,1,0:T(8,128)(2,1)S(1)}, u32[]{:S(2)}, u32[]{:S(2)}) collective-permute-start(bf16[2,4,48,640]{3,2,1,0:T(8,128)(2,1)S(1)} %fusion.3), channel_id=1, source_target_pairs={{0,16},{8,24},{16,0},{24,8},{1,17},{9,25},{17,1},{25,9},{2,18},{10... | collective-permute-start | bytes 1474568 | tf_op jit(solution)/shard_map/ppermute | solution.py:514
  118.7 12.3 %collective-permute-start.54 = (bf16[72,384]{1,0:T(8,128)(2,1)S(1)}, bf16[72,384]{1,0:T(8,128)(2,1)S(1)}, u32[]{:S(2)}, u32[]{:S(2)}) collective-permute-start(bf16[72,384]{1,0:T(8,128)(2,1)S(1)} %fusion.26), channel_id=1, source_target_pairs={{0,16},{8,24},{16,0},{24,8},{1,17},{9,25},{17,1},{25,9},{2,18},{10... | collective-permute-start | bytes 165896 | tf_op jit(solution)/shard_map/ppermute | solution.py:514
  119.5 28.8 %collective-permute-start.40 = (bf16[2,4,96,640]{3,2,1,0:T(8,128)(2,1)S(1)}, bf16[2,4,96,640]{3,2,1,0:T(8,128)(2,1)S(1)}, u32[]{:S(2)}, u32[]{:S(2)}) collective-permute-start(bf16[2,4,96,640]{3,2,1,0:T(8,128)(2,1)S(1)} %add_convert_fusion.1), channel_id=1, source_target_pairs={{0,16},{8,24},{16,0},{24,8},{1,17},{9,25},{17,1},{25,9},{2,18},{10... | collective-permute-start | bytes 2949128 | tf_op jit(solution)/shard_map/ppermute | solution.py:514
  150.2 11.9 %collective-permute-start.41 = (bf16[4,96,640]{2,1,0:T(8,128)(2,1)}, bf16[4,96,640]{2,1,0:T(8,128)(2,1)S(1)}, u32[]{:S(2)}, u32[]{:S(2)}) collective-permute-start(bf16[4,96,640]{2,1,0:T(8,128)(2,1)} %slice_bitcast_fusion), channel_id=1, source_target_pairs={{0,1},{1,0},{2,3},{3,2},{4,5},{5,4},{6,7},{7,6},{8,9},{9,8},{10,11... | collective-permute-start | bytes 1474568 | tf_op jit(solution)/shard_map/ppermute | solution.py:514
  164.7 10.3 %collective-permute-start.43 = (bf16[96,640]{1,0:T(8,128)(2,1)S(1)}, bf16[96,640]{1,0:T(8,128)(2,1)S(1)}, u32[]{:S(2)}, u32[]{:S(2)}) collective-permute-start(bf16[96,640]{1,0:T(8,128)(2,1)S(1)} %get-tuple-element.109), channel_id=1, source_target_pairs={{0,4},{1,5},{2,6},{3,7},{4,0},{5,1},{6,2},{7,3},{8,12},{9,13},{10,... | collective-permute-start | bytes 368648 | tf_op jit(solution)/shard_map/ppermute | solution.py:514
  (36 other events, 414.1 us)

commit v2 on v1

--- a/solution.py
+++ b/solution.py
@@ -380,6 +380,35 @@
     dx_ref[...] = dx[:, :width].astype(BF16)
 
 
+def unpack_ff_kernel(plan, place, mine_ref, other_ref, gate_ref, up_ref):
+    rows = plan.ff_rows
+    for rc, ref in enumerate((mine_ref, other_ref)):
+        for rx in range(plan.nx):
+            part = (place[0] + rx + 1) % plan.nx * plan.nc + (place[1] + rc) % plan.nc
+            at = pl.ds(pl.multiple_of(part * rows, rows), rows)
+            gate_ref[at, :] = ref[rx, :rows, : plan.width].astype(F32)
+            up_ref[at, :] = ref[rx, rows:, : plan.width].astype(F32)
+
+
+def unpack_attention_kernel(plan, place, mine_ref, other_ref, q_ref, k_ref, v_ref, o_ref, gain_a_ref, gain_m_ref):
+    width, rows, krows, lanes = plan.width, plan.out_rows, plan.kv_rows, plan.lanes
+    mine = [mine_ref[i].astype(F32) for i in range(plan.nx)]
+    other = [other_ref[i].astype(F32) for i in range(plan.nx)]
+    swap = place[0] != 0
+    mine = jnp.where(swap, jnp.concatenate(mine[::-1], 0), jnp.concatenate(mine, 0))
+    other = jnp.where(swap, jnp.concatenate(other[::-1], 0), jnp.concatenate(other, 0))
+    one = jnp.where(place[1] == 0, mine, other)
+    two = jnp.where(place[1] == 0, other, mine)
+    q_ref[...] = one[:rows, :width]
+    k_ref[...] = one[rows:, :width]
+    v_ref[...] = two[:krows, :width]
+    o_ref[...] = two[krows:, :width]
+    last = jnp.concatenate([one[:, lanes - LANES :], jnp.zeros((LANES - rows - krows, LANES), F32)], 0).T
+    at = width - (lanes - LANES)
+    gain_a_ref[...] = last[at : at + 1, :rows]
+    gain_m_ref[...] = last[at + 1 : at + 2, :rows]
+
+
 VMEM = pl.BlockSpec(memory_space=pltpu.VMEM)
 SMEM = pl.BlockSpec(memory_space=pltpu.SMEM)
 
@@ -493,6 +522,17 @@
     )(place, tokens, dmid, dgain, grad_out, da, attn, q, k, v, prob, wq, wk, wv, gain, cos, sin)
 
 
+def unpack(plan, kernel, place, mine, other, shapes):
+    return pl.pallas_call(
+        functools.partial(kernel, plan),
+        in_specs=[SMEM, VMEM, VMEM],
+        out_specs=[VMEM] * len(shapes),
+        out_shape=[shape_of(dims, F32) for dims in shapes],
+        cost_estimate=cost(2),
+        compiler_params=limit(plan, 6),
+    )(place, mine, other)
+
+
 def shift(plan, dim, amount):
     if dim in "xc":
         axis, outer, inner, first = "dp", plan.nx, plan.nc, dim == "x"
@@ -515,7 +555,8 @@
 
 
 def spread(plan, piece, dims):
-    stack = jnp.stack([piece] + [send(plan, piece, "z", k) for k in range(1, plan.nz)])
+    around = [piece] + [send(plan, piece, "z", k) for k in range(1, plan.nz)]
+    stack = jnp.stack(around)
     held = {(0, 0, 0): stack}
     for dim in dims:
         at = "cxy".index(dim)
@@ -531,9 +572,10 @@
 
 
 def reduce_z(plan, stack):
+    got = [send(plan, stack[k], "z", k) for k in range(1, plan.nz)]
     total = stack[0].astype(F32)
-    for k in range(1, plan.nz):
-        total = total + send(plan, stack[k], "z", k).astype(F32)
+    for value in got:
+        total = total + value.astype(F32)
     return total.astype(BF16)
 
 
@@ -622,34 +664,45 @@
             else:
                 both = jnp.stack([keep[1], away[1]])
                 got = send(plan, both, "y")
-                part = add(add(keep[0], got[0]), send(plan, add(away[0], got[1]), "x"))
+                there = send(plan, add(away[0], got[1]), "x")
+                part = add(add(keep[0], got[0]), there)
             part = reduce_z(plan, part)
             both = jnp.stack([part, send(plan, part, "x")])
-            other = send(plan, both, "c")
+            return both, send(plan, both, "c")
+
+        def in_order(both, other):
             quads = jnp.stack([both, other], 1)
             quads = jnp.where(c_first, quads, quads[:, ::-1])
             return jnp.where(x_first, quads[::-1], quads)
 
-        def ff(quads):
-            return quads.reshape(plan.parts * plan.ff_rows, lanes)[:, :width].astype(F32).T
-
         ff_rows = plan.ff_rows
-
-        quads = fold([g[0] for g in grads], "xy")
-        grad_gate, grad_up = ff(quads[:, :, :ff_rows]), ff(quads[:, :, ff_rows:])
-        quads = fold([g[1] for g in grads], "yx")
+        both, other = fold([g[0] for g in grads], "xy")
+        grad_gate, grad_up = unpack(plan, unpack_ff_kernel, place, both, other, [(plan.parts * ff_rows, width)] * 2)
+        quads = in_order(*fold([g[1] for g in grads], "yx"))
         quads = quads.reshape(plan.parts, rows, plan.shards, ff_rows)
-        grad_down = quads.transpose(2, 0, 3, 1).reshape(hidden, rows).astype(F32)
+        grad_down = quads.transpose(1, 2, 0, 3).reshape(rows, hidden).astype(F32)
         got = send(plan, packs[1], "c")
         there = send(plan, add(packs[0][1], got[1]), "x")
         part = add(add(packs[0][0], got[0]), there)
         part = add(part[0], send(plan, part[1], "y"))
         part = reduce_z(plan, part)
+        part, grad_down = lax.optimization_barrier((part, grad_down))
         there = send(plan, part, "x")
-        both = jnp.where(x_first, jnp.concatenate([part, there], 0), jnp.concatenate([there, part], 0))
+        both = jnp.stack([part, there])
+        both, grad_gate, grad_up = lax.optimization_barrier((both, grad_gate, grad_up))
         other = send(plan, both, "c")
-        one = jnp.where(c_first, both, other).astype(F32)
-        two = jnp.where(c_first, other, both).astype(F32)
+        shapes = [(rows, width), (krows, width), (krows, width), (rows, width), (1, rows), (1, rows)]
+        *results, gain_a, gain_m = unpack(plan, unpack_attention_kernel, place, both, other, shapes)
+        return (
+            output,
+            grad_tokens,
+            *[result.T for result in results],
+            grad_gate.T,
+            grad_up.T,
+            grad_down.T,
+            gain_a.reshape(rows),
+            gain_m.reshape(rows),
+        )
     else:
 
         def total(value):

time: 184 us -> 198 us (1.076)
  starting transfers between devices: 53.9 us -> 59.1 us
  other arithmetic: 5.81 us -> 9.07 us
  Pallas kernels: 35.9 us -> 38.7 us
  waiting for transfers between devices: 78.8 us -> 81.2 us
    ppermute x56, starting transfers between devices: 53.9 us -> 59.1 us  [send(): return lax.ppermute(value, axis, pairs)]
    convert_element_type x10, other arithmetic: 1.5 us -> 5.91 us  [add(): return (a.astype(F32) + b.astype(F32)).astype(BF16)]
    convert_element_type x2, local copies, waits for them, and re-layouts: 0.33 us -> 4.3 us  [layer(): grad_down = quads.transpose(1, 2, 0, 3).reshape(rows, hidden).astype(F32)]
    pallas_call x0 -> x2, Pallas kernels: none -> 2.91 us  [unpack(): pl.pallas_call(functools.partial(kernel, plan), in_specs=[SMEM, VMEM, VME...]
    transpose x4 -> x0, local copies, waits for them, and re-layouts: 2.63 us -> none  [the longest x1 0.69 us: layer(): two[krows:, :width]]
    ppermute x56, waiting for transfers between devices: 78.8 us -> 81.2 us  [send(): return lax.ppermute(value, axis, pairs)]
  transfers between devices with their start and end apart: 56 -> 56, of which waited for: 21 -> 19; matrix products, arithmetic and copies ran while one was open for 5% -> 7% of each run, Pallas kernels for 20% -> 18%
where the time goes in v2:
time: 198 us
  waiting for transfers between devices  81.2 us (41%)
  starting transfers between devices  59.1 us (30%)
  Pallas kernels  38.7 us (20%)
  other arithmetic  9.07 us (5%)
  local copies, waits for them, and re-layouts  8.84 us (4%)
    ppermute x56, waiting for transfers between devices, send(): return lax.ppermute(value, axis, pairs)  81.2 us
    ppermute x56, starting transfers between devices, send(): return lax.ppermute(value, axis, pairs)  59.1 us
    pallas_call x2, Pallas kernels, mlp(): pl.pallas_call(functools.partial(mlp_kernel, plan, first, last), name='ml...  18 us
    pallas_call x1, Pallas kernels, attention_backward(): pl.pallas_call(functools.partial(backward_rest_kernel, plan), name='backw...  10.8 us
    convert_element_type x10, other arithmetic, add(): return (a.astype(F32) + b.astype(F32)).astype(BF16)  5.91 us
    pallas_call x1, Pallas kernels, attention_forward(): pl.pallas_call(functools.partial(attention_forward_kernel, plan, len(piec...  5.48 us
    convert_element_type x2, local copies, waits for them, and re-layouts, layer(): grad_down = quads.transpose(1, 2, 0, 3).reshape(rows, hidden).astype(F32)  4.3 us
  transfers between devices with their start and end apart: 56, of which 19 were waited for; matrix products, arithmetic and copies ran while one was open for 7% of the time, Pallas kernels for 18%

profile of v2, /device:TPU:0, one launch (start us, length us, event | category | flops | bytes accessed | tf_op | source)
XLA Modules:
  0.0 198.0 jit_solution(17362638740353293598)
XLA Ops:
  2.7 3.1 %collective-permute-start = (bf16[48,640]{1,0:T(8,128)(2,1)S(1)}, bf16[48,640]{1,0:T(8,128)(2,1)S(1)}, u32[]{:S(2)}, u32[]{:S(2)}) collective-permute-start(bf16[48,640]{1,0:T(8,128)(2,1)S(1)} %slice_select_fusion), channel_id=1, source_target_pairs={{0,2},{1,3},{2,0},{3,1},{4,6},{5,7},{6,4},{7,5},{8,10},{9,11},{10,... | collective-permute-start | bytes 184328 | tf_op jit(solution)/shard_map/ppermute | solution.py:554
  5.8 2.6 %collective-permute-start.1 = (bf16[48,640]{1,0:T(8,128)(2,1)S(1)}, bf16[48,640]{1,0:T(8,128)(2,1)S(1)}, u32[]{:S(2)}, u32[]{:S(2)}) collective-permute-start(bf16[48,640]{1,0:T(8,128)(2,1)S(1)} %slice_select_fusion), channel_id=1, source_target_pairs={{0,4},{1,5},{2,6},{3,7},{4,0},{5,1},{6,2},{7,3},{8,12},{9,13},{10,... | collective-permute-start | bytes 184328 | tf_op jit(solution)/shard_map/ppermute | solution.py:554
  10.3 3.5 %collective-permute-start.11 = (bf16[96,640]{1,0:T(8,128)(2,1)S(1)}, bf16[96,640]{1,0:T(8,128)(2,1)S(1)}, u32[]{:S(2)}, u32[]{:S(2)}) collective-permute-start(bf16[96,640]{1,0:T(8,128)(2,1)S(1)} %get-tuple-element.139), channel_id=1, source_target_pairs={{0,4},{1,5},{2,6},{3,7},{4,0},{5,1},{6,2},{7,3},{8,12},{9,13},{10,... | collective-permute-start | bytes 368648 | tf_op jit(solution)/shard_map/ppermute | solution.py:554
  15.8 3.8 %collective-permute-start.18 = (bf16[72,384]{1,0:T(8,128)(2,1)S(1)}, bf16[72,384]{1,0:T(8,128)(2,1)S(1)}, u32[]{:S(2)}, u32[]{:S(2)}) collective-permute-start(bf16[72,384]{1,0:T(8,128)(2,1)S(1)} %bitcast.123), channel_id=1, source_target_pairs={{0,6},{1,7},{2,4},{3,5},{4,2},{5,3},{6,0},{7,1},{8,14},{9,15},{10,... | collective-permute-start | bytes 165896 | tf_op jit(solution)/shard_map/ppermute | solution.py:554
  21.3 2.3 %collective-permute-done.17 = bf16[72,384]{1,0:T(8,128)(2,1)S(1)} collective-permute-done((bf16[72,384]{1,0:T(8,128)(2,1)S(1)}, bf16[72,384]{1,0:T(8,128)(2,1)S(1)}, u32[]{:S(2)}, u32[]{:S(2)}) %collective-permute-start.17) | collective-permute-done | bytes 55328 | tf_op jit(solution)/shard_map/ppermute | solution.py:554
  23.6 2.8 %collective-permute-start.3 = (bf16[4,48,640]{2,1,0:T(8,128)(2,1)S(1)}, bf16[4,48,640]{2,1,0:T(8,128)(2,1)S(1)}, u32[]{:S(2)}, u32[]{:S(2)}) collective-permute-start(bf16[4,48,640]{2,1,0:T(8,128)(2,1)S(1)} %pad_maximum_fusion.2.refs_0_), channel_id=1, source_target_pairs={{0,1},{1,0},{2,3},{3,2},{4,5},{5,4},{6,7},{7,6},{8,9},{9,8},{10,11... | collective-permute-start | bytes 737288 | tf_op jit(solution)/shard_map/ppermute | solution.py:554
  28.8 4.9 %collective-permute-done.19.refs_8_ = bf16[4,72,384]{2,1,0:T(8,128)(2,1)S(1)} collective-permute-done((bf16[4,72,384]{2,1,0:T(8,128)(2,1)S(1)}, bf16[4,72,384]{2,1,0:T(8,128)(2,1)S(1)}, u32[]{:S(2)}, u32[]{:S(2)}) %collective-permute-start.19) | collective-permute-done | bytes 221216 | tf_op jit(solution)/shard_map/ppermute | solution.py:554
  37.3 3.0 %collective-permute-done.4.refs_2_ = bf16[4,48,640]{2,1,0:T(8,128)(2,1)S(1)} collective-permute-done((bf16[4,48,640]{2,1,0:T(8,128)(2,1)S(1)}, bf16[4,48,640]{2,1,0:T(8,128)(2,1)S(1)}, u32[]{:S(2)}, u32[]{:S(2)}) %collective-permute-start.4) | collective-permute-done | bytes 245792 | tf_op jit(solution)/shard_map/ppermute | solution.py:554
  40.8 14.9 %collective-permute-done.5.refs_3_ = bf16[4,48,640]{2,1,0:T(8,128)(2,1)S(1)} collective-permute-done((bf16[4,48,640]{2,1,0:T(8,128)(2,1)S(1)}, bf16[4,48,640]{2,1,0:T(8,128)(2,1)S(1)}, u32[]{:S(2)}, u32[]{:S(2)}) %collective-permute-start.5) | collective-permute-done | bytes 245792 | tf_op jit(solution)/shard_map/ppermute | solution.py:554
  59.8 5.5 %attention_forward.1 = (bf16[576,640]{1,0:T(8,128)(2,1)S(1)}, bf16[576,512]{1,0:T(8,128)(2,1)S(1)}, bf16[576,512]{1,0:T(8,128)(2,1)S(1)}, bf16[576,640]{1,0:T(8,...) custom-call(s32[4]{0:T(128)S(1)} %pad_add_fusion.place, ...), custom_call_target="tpu_custom_call" | custom-call | flops 10000000000 | bytes 10000000 | tf_op jit(solution)/shard_map/attention_forward/pallas_call | solution.py:436
  65.9 5.8 %collective-permute-done.23.refs_4_ = bf16[4,96,640]{2,1,0:T(8,128)(2,1)S(1)} collective-permute-done((bf16[4,96,640]{2,1,0:T(8,128)(2,1)S(1)}, bf16[4,96,640]{2,1,0:T(8,128)(2,1)S(1)}, u32[]{:S(2)}, u32[]{:S(2)}) %collective-permute-start.23) | collective-permute-done | bytes 491552 | tf_op jit(solution)/shard_map/ppermute | solution.py:554
  71.7 9.1 %mlp.2 = (f32[576,640]{1,0:T(8,128)S(1)}, f32[576,640]{1,0:T(8,128)S(1)}, f32[576,640]{1,0:T(8,128)S(1)}, bf16[2,4,96,640]{3,2,1,0:T(8,128)(2,1)S(1)}, bf16[2,4,...) custom-call(s32[4]{0:T(128)S(1)} %pad_add_fusion.place, ...), custom_call_target="tpu_custom_call" | custom-call | flops 12000000000 | bytes 12000000 | tf_op jit(solution)/shard_map/mlp/pallas_call | solution.py:470
  81.3 8.9 %mlp.3 = (bf16[576,576]{1,0:T(8,128)(2,1)}, f32[576,640]{1,0:T(8,128)S(1)}, f32[8,640]{1,0:T(8,128)S(1)}, bf16[2,4,96,640]{3,2,1,0:T(8,128)(2,1)S(1)}, bf16[2,4,...) custom-call(s32[4]{0:T(128)S(1)} %pad_add_fusion.place, ...), custom_call_target="tpu_custom_call" | custom-call | flops 12000000000 | bytes 12000000 | tf_op jit(solution)/shard_map/mlp/pallas_call | solution.py:470
  95.5 9.1 %collective-permute-done.38 = bf16[2,4,72,384]{3,2,1,0:T(8,128)(2,1)S(1)} collective-permute-done((bf16[2,4,72,384]{3,2,1,0:T(8,128)(2,1)S(1)}, bf16[2,4,72,384]{3,2,1,0:T(8,128)(2,1)S(1)}, u32[]{:S(2)}, u32[]{:S(2)}) %collective-permute-start.38) | collective-permute-done | bytes 442400 | tf_op jit(solution)/shard_map/ppermute | solution.py:554
  105.3 10.8 %backward_rest.1 = (bf16[576,576]{1,0:T(8,128)(2,1)}, bf16[2,2,4,48,640]{4,3,2,1,0:T(8,128)(2,1)S(1)}, bf16[2,2,4,48,640]{4,3,2,1,0:T(8,128)(2,1)S(1)}) custom-call(s32[4]{0:T(128)S(1)} %pad_add_fusion.place, bf16[576,576]{1,0:T(8,128)(2,1)S(1)} %copy-done.2, f32[576,640]{1,0:T(8,128)S(1)} %get-tuple-element.72.dmid_ref, ...), custom_call_target="tpu_custom_call" | custom-call | flops 14000000000 | bytes 14000000 | tf_op jit(solution)/shard_map/backward_rest/pallas_call | solution.py:508
  116.2 2.6 %collective-permute-start.40 = (bf16[72,384]{1,0:T(8,128)(2,1)S(1)}, bf16[72,384]{1,0:T(8,128)(2,1)S(1)}, u32[]{:S(2)}, u32[]{:S(2)}) collective-permute-start(bf16[72,384]{1,0:T(8,128)(2,1)S(1)} %get-tuple-element.135), channel_id=1, source_target_pairs={{0,2},{1,3},{2,0},{3,1},{4,6},{5,7},{6,4},{7,5},{8,10},{9,11},{10,... | collective-permute-start | bytes 165896 | tf_op jit(solution)/shard_map/ppermute | solution.py:554
  121.4 4.4 %collective-permute-done.41 = bf16[72,384]{1,0:T(8,128)(2,1)S(1)} collective-permute-done((bf16[72,384]{1,0:T(8,128)(2,1)S(1)}, bf16[72,384]{1,0:T(8,128)(2,1)S(1)}, u32[]{:S(2)}, u32[]{:S(2)}) %collective-permute-start.41) | collective-permute-done | bytes 55328 | tf_op jit(solution)/shard_map/ppermute | solution.py:554
  140.2 14.2 %collective-permute-done.48 = bf16[2,4,96,640]{3,2,1,0:T(8,128)(2,1)} collective-permute-done((bf16[2,4,96,640]{3,2,1,0:T(8,128)(2,1)}, bf16[2,4,96,640]{3,2,1,0:T(8,128)(2,1)}, u32[]{:S(2)}, u32[]{:S(2)}) %collective-permute-start.48) | collective-permute-done | bytes 983072 | tf_op jit(solution)/shard_map/ppermute | solution.py:554
  158.1 4.6 %collective-permute-done.31 = bf16[2,4,48,640]{3,2,1,0:T(8,128)(2,1)} collective-permute-done((bf16[2,4,48,640]{3,2,1,0:T(8,128)(2,1)}, bf16[2,4,48,640]{3,2,1,0:T(8,128)(2,1)}, u32[]{:S(2)}, u32[]{:S(2)}) %collective-permute-start.31) | collective-permute-done | bytes 491552 | tf_op jit(solution)/shard_map/ppermute | solution.py:554
  166.5 2.8 %collective-permute-start.50 = (bf16[96,640]{1,0:T(8,128)(2,1)S(1)}, bf16[96,640]{1,0:T(8,128)(2,1)S(1)}, u32[]{:S(2)}, u32[]{:S(2)}) collective-permute-start(bf16[96,640]{1,0:T(8,128)(2,1)S(1)} %get-tuple-element.129), channel_id=1, source_target_pairs={{0,2},{1,3},{2,0},{3,1},{4,6},{5,7},{6,4},{7,5},{8,10},{9,11},{10,... | collective-permute-start | bytes 368648 | tf_op jit(solution)/shard_map/ppermute | solution.py:554
  173.6 4.3 %collective-permute-done.51 = bf16[96,640]{1,0:T(8,128)(2,1)S(1)} collective-permute-done((bf16[96,640]{1,0:T(8,128)(2,1)S(1)}, bf16[96,640]{1,0:T(8,128)(2,1)S(1)}, u32[]{:S(2)}, u32[]{:S(2)}) %collective-permute-start.51) | collective-permute-done | bytes 122912 | tf_op jit(solution)/shard_map/ppermute | solution.py:554
  178.7 3.6 %collective-permute-start.33 = (bf16[48,640]{1,0:T(8,128)(2,1)S(1)}, bf16[48,640]{1,0:T(8,128)(2,1)S(1)}, u32[]{:S(2)}, u32[]{:S(2)}) collective-permute-start(bf16[48,640]{1,0:T(8,128)(2,1)S(1)} %get-tuple-element.132), channel_id=1, source_target_pairs={{0,2},{1,3},{2,0},{3,1},{4,6},{5,7},{6,4},{7,5},{8,10},{9,11},{10,... | collective-permute-start | bytes 184328 | tf_op jit(solution)/shard_map/ppermute | solution.py:554
  184.8 3.2 %collective-permute-done.34 = bf16[48,640]{1,0:T(8,128)(2,1)S(1)} collective-permute-done((bf16[48,640]{1,0:T(8,128)(2,1)S(1)}, bf16[48,640]{1,0:T(8,128)(2,1)S(1)}, u32[]{:S(2)}, u32[]{:S(2)}) %collective-permute-start.34) | collective-permute-done | bytes 61472 | tf_op jit(solution)/shard_map/ppermute | solution.py:554
  191.2 2.5 %collective-permute-done.45 = bf16[48,640]{1,0:T(8,128)(2,1)S(1)} collective-permute-done((bf16[48,640]{1,0:T(8,128)(2,1)S(1)}, bf16[48,640]{1,0:T(8,128)(2,1)S(1)}, u32[]{:S(2)}, u32[]{:S(2)}) %collective-permute-start.45) | collective-permute-done | bytes 61472 | tf_op jit(solution)/shard_map/ppermute | solution.py:554
  (155 shorter events, 64.5 us)
Async XLA Ops:
  2.7 12.5 %collective-permute-start = (bf16[48,640]{1,0:T(8,128)(2,1)S(1)}, bf16[48,640]{1,0:T(8,128)(2,1)S(1)}, u32[]{:S(2)}, u32[]{:S(2)}) collective-permute-start(bf16[48,640]{1,0:T(8,128)(2,1)S(1)} %slice_select_fusion), channel_id=1, source_target_pairs={{0,2},{1,3},{2,0},{3,1},{4,6},{5,7},{6,4},{7,5},{8,10},{9,11},{10,... | collective-permute-start | bytes 184328 | tf_op jit(solution)/shard_map/ppermute | solution.py:554
  9.4 17.2 %collective-permute-start.10 = (bf16[96,640]{1,0:T(8,128)(2,1)S(1)}, bf16[96,640]{1,0:T(8,128)(2,1)S(1)}, u32[]{:S(2)}, u32[]{:S(2)}) collective-permute-start(bf16[96,640]{1,0:T(8,128)(2,1)S(1)} %get-tuple-element.139), channel_id=1, source_target_pairs={{0,2},{1,3},{2,0},{3,1},{4,6},{5,7},{6,4},{7,5},{8,10},{9,11},{10,... | collective-permute-start | bytes 368648 | tf_op jit(solution)/shard_map/ppermute | solution.py:554
  10.3 16.3 %collective-permute-start.11 = (bf16[96,640]{1,0:T(8,128)(2,1)S(1)}, bf16[96,640]{1,0:T(8,128)(2,1)S(1)}, u32[]{:S(2)}, u32[]{:S(2)}) collective-permute-start(bf16[96,640]{1,0:T(8,128)(2,1)S(1)} %get-tuple-element.139), channel_id=1, source_target_pairs={{0,4},{1,5},{2,6},{3,7},{4,0},{5,1},{6,2},{7,3},{8,12},{9,13},{10,... | collective-permute-start | bytes 368648 | tf_op jit(solution)/shard_map/ppermute | solution.py:554
  15.8 10.6 %collective-permute-start.18 = (bf16[72,384]{1,0:T(8,128)(2,1)S(1)}, bf16[72,384]{1,0:T(8,128)(2,1)S(1)}, u32[]{:S(2)}, u32[]{:S(2)}) collective-permute-start(bf16[72,384]{1,0:T(8,128)(2,1)S(1)} %bitcast.123), channel_id=1, source_target_pairs={{0,6},{1,7},{2,4},{3,5},{4,2},{5,3},{6,0},{7,1},{8,14},{9,15},{10,... | collective-permute-start | bytes 165896 | tf_op jit(solution)/shard_map/ppermute | solution.py:554
  23.6 13.3 %collective-permute-start.3 = (bf16[4,48,640]{2,1,0:T(8,128)(2,1)S(1)}, bf16[4,48,640]{2,1,0:T(8,128)(2,1)S(1)}, u32[]{:S(2)}, u32[]{:S(2)}) collective-permute-start(bf16[4,48,640]{2,1,0:T(8,128)(2,1)S(1)} %pad_maximum_fusion.2.refs_0_), channel_id=1, source_target_pairs={{0,1},{1,0},{2,3},{3,2},{4,5},{5,4},{6,7},{7,6},{8,9},{9,8},{10,11... | collective-permute-start | bytes 737288 | tf_op jit(solution)/shard_map/ppermute | solution.py:554
  28.6 11.7 %collective-permute-start.4 = (bf16[4,48,640]{2,1,0:T(8,128)(2,1)S(1)}, bf16[4,48,640]{2,1,0:T(8,128)(2,1)S(1)}, u32[]{:S(2)}, u32[]{:S(2)}) collective-permute-start(bf16[4,48,640]{2,1,0:T(8,128)(2,1)S(1)} %pad_maximum_fusion.2.refs_0_), channel_id=1, source_target_pairs={{0,16},{8,24},{16,0},{24,8},{1,17},{9,25},{17,1},{25,9},{2,18},{10... | collective-permute-start | bytes 737288 | tf_op jit(solution)/shard_map/ppermute | solution.py:554
  33.8 22.6 %collective-permute-start.13 = (bf16[4,96,640]{2,1,0:T(8,128)(2,1)S(1)}, bf16[4,96,640]{2,1,0:T(8,128)(2,1)S(1)}, u32[]{:S(2)}, u32[]{:S(2)}) collective-permute-start(bf16[4,96,640]{2,1,0:T(8,128)(2,1)S(1)} %pad_maximum_fusion.refs_3_), channel_id=1, source_target_pairs={{0,1},{1,0},{2,3},{3,2},{4,5},{5,4},{6,7},{7,6},{8,9},{9,8},{10,11... | collective-permute-start | bytes 1474568 | tf_op jit(solution)/shard_map/ppermute | solution.py:554
  35.3 22.8 %collective-permute-start.22 = (bf16[4,96,640]{2,1,0:T(8,128)(2,1)S(1)}, bf16[4,96,640]{2,1,0:T(8,128)(2,1)S(1)}, u32[]{:S(2)}, u32[]{:S(2)}) collective-permute-start(bf16[4,96,640]{2,1,0:T(8,128)(2,1)S(1)} %pad_maximum_fusion.refs_3_), channel_id=1, source_target_pairs={{0,16},{8,24},{16,0},{24,8},{1,17},{9,25},{17,1},{25,9},{2,18},{10... | collective-permute-start | bytes 1474568 | tf_op jit(solution)/shard_map/ppermute | solution.py:554
  36.9 18.8 %collective-permute-start.5 = (bf16[4,48,640]{2,1,0:T(8,128)(2,1)S(1)}, bf16[4,48,640]{2,1,0:T(8,128)(2,1)S(1)}, u32[]{:S(2)}, u32[]{:S(2)}) collective-permute-start(bf16[4,48,640]{2,1,0:T(8,128)(2,1)S(1)} %collective-permute-done.3.refs_1_), channel_id=1, source_target_pairs={{0,16},{8,24},{16,0},{24,8},{1,17},{9,25},{17,1},{25,9},{2,18},{10... | collective-permute-start | bytes 737288 | tf_op jit(solution)/shard_map/ppermute | solution.py:554
  40.3 15.4 %collective-permute-start.7 = (bf16[4,48,640]{2,1,0:T(8,128)(2,1)S(1)}, bf16[4,48,640]{2,1,0:T(8,128)(2,1)S(1)}, u32[]{:S(2)}, u32[]{:S(2)}) collective-permute-start(bf16[4,48,640]{2,1,0:T(8,128)(2,1)S(1)} %collective-permute-done.3.refs_1_), channel_id=1, source_target_pairs={{0,8},{8,0},{16,24},{24,16},{1,9},{9,1},{17,25},{25,17},{2,10},{10... | collective-permute-start | bytes 737288 | tf_op jit(solution)/shard_map/ppermute | solution.py:554
  40.3 15.9 %collective-permute-start.8 = (bf16[4,48,640]{2,1,0:T(8,128)(2,1)S(1)}, bf16[4,48,640]{2,1,0:T(8,128)(2,1)S(1)}, u32[]{:S(2)}, u32[]{:S(2)}) collective-permute-start(bf16[4,48,640]{2,1,0:T(8,128)(2,1)S(1)} %collective-permute-done.4.refs_2_), channel_id=1, source_target_pairs={{0,8},{8,0},{16,24},{24,16},{1,9},{9,1},{17,25},{25,17},{2,10},{10... | collective-permute-start | bytes 737288 | tf_op jit(solution)/shard_map/ppermute | solution.py:554
  55.7 10.1 %collective-permute-start.14 = (bf16[4,96,640]{2,1,0:T(8,128)(2,1)S(1)}, bf16[4,96,640]{2,1,0:T(8,128)(2,1)S(1)}, u32[]{:S(2)}, u32[]{:S(2)}) collective-permute-start(bf16[4,96,640]{2,1,0:T(8,128)(2,1)S(1)} %pad_maximum_fusion.refs_3_), channel_id=1, source_target_pairs={{0,8},{8,0},{16,24},{24,16},{1,9},{9,1},{17,25},{25,17},{2,10},{10... | collective-permute-start | bytes 1474568 | tf_op jit(solution)/shard_map/ppermute | solution.py:554
  58.1 13.6 %collective-permute-start.15 = (bf16[4,96,640]{2,1,0:T(8,128)(2,1)S(1)}, bf16[4,96,640]{2,1,0:T(8,128)(2,1)S(1)}, u32[]{:S(2)}, u32[]{:S(2)}) collective-permute-start(bf16[4,96,640]{2,1,0:T(8,128)(2,1)S(1)} %collective-permute-done.13.refs_4_), channel_id=1, source_target_pairs={{0,8},{8,0},{16,24},{24,16},{1,9},{9,1},{17,25},{25,17},{2,10},{10... | collective-permute-start | bytes 1474568 | tf_op jit(solution)/shard_map/ppermute | solution.py:554
  58.2 13.5 %collective-permute-start.23 = (bf16[4,96,640]{2,1,0:T(8,128)(2,1)S(1)}, bf16[4,96,640]{2,1,0:T(8,128)(2,1)S(1)}, u32[]{:S(2)}, u32[]{:S(2)}) collective-permute-start(bf16[4,96,640]{2,1,0:T(8,128)(2,1)S(1)} %collective-permute-done.22.refs_3_), channel_id=1, source_target_pairs={{0,1},{1,0},{2,3},{3,2},{4,5},{5,4},{6,7},{7,6},{8,9},{9,8},{10,11... | collective-permute-start | bytes 1474568 | tf_op jit(solution)/shard_map/ppermute | solution.py:554
  65.2 16.1 %collective-permute-start.28 = (bf16[4,72,384]{2,1,0:T(8,128)(2,1)S(1)}, bf16[4,72,384]{2,1,0:T(8,128)(2,1)S(1)}, u32[]{:S(2)}, u32[]{:S(2)}) collective-permute-start(bf16[4,72,384]{2,1,0:T(8,128)(2,1)S(1)} %collective-permute-done.26.refs_7_), channel_id=1, source_target_pairs={{0,8},{8,0},{16,24},{24,16},{1,9},{9,1},{17,25},{25,17},{2,10},{10... | collective-permute-start | bytes 663560 | tf_op jit(solution)/shard_map/ppermute | solution.py:554
  65.4 15.9 %collective-permute-start.29 = (bf16[4,72,384]{2,1,0:T(8,128)(2,1)S(1)}, bf16[4,72,384]{2,1,0:T(8,128)(2,1)S(1)}, u32[]{:S(2)}, u32[]{:S(2)}) collective-permute-start(bf16[4,72,384]{2,1,0:T(8,128)(2,1)S(1)} %collective-permute-done.27.refs_8_), channel_id=1, source_target_pairs={{0,8},{8,0},{16,24},{24,16},{1,9},{9,1},{17,25},{25,17},{2,10},{10... | collective-permute-start | bytes 663560 | tf_op jit(solution)/shard_map/ppermute | solution.py:554
  65.8 15.5 %collective-permute-start.24 = (bf16[4,96,640]{2,1,0:T(8,128)(2,1)S(1)}, bf16[4,96,640]{2,1,0:T(8,128)(2,1)S(1)}, u32[]{:S(2)}, u32[]{:S(2)}) collective-permute-start(bf16[4,96,640]{2,1,0:T(8,128)(2,1)S(1)} %collective-permute-done.22.refs_3_), channel_id=1, source_target_pairs={{0,8},{8,0},{16,24},{24,16},{1,9},{9,1},{17,25},{25,17},{2,10},{10... | collective-permute-start | bytes 1474568 | tf_op jit(solution)/shard_map/ppermute | solution.py:554
  92.4 12.3 %collective-permute-start.38 = (bf16[2,4,72,384]{3,2,1,0:T(8,128)(2,1)S(1)}, bf16[2,4,72,384]{3,2,1,0:T(8,128)(2,1)S(1)}, u32[]{:S(2)}, u32[]{:S(2)}) collective-permute-start(bf16[2,4,72,384]{3,2,1,0:T(8,128)(2,1)S(1)} %pad_maximum_fusion.1), channel_id=1, source_target_pairs={{0,1},{1,0},{2,3},{3,2},{4,5},{5,4},{6,7},{7,6},{8,9},{9,8},{10,11... | collective-permute-start | bytes 1327112 | tf_op jit(solution)/shard_map/ppermute | solution.py:554
  93.9 34.3 %collective-permute-start.47 = (bf16[2,4,96,640]{3,2,1,0:T(8,128)(2,1)S(1)}, bf16[2,4,96,640]{3,2,1,0:T(8,128)(2,1)S(1)}, u32[]{:S(2)}, u32[]{:S(2)}) collective-permute-start(bf16[2,4,96,640]{3,2,1,0:T(8,128)(2,1)S(1)} %get-tuple-element.94), channel_id=1, source_target_pairs={{0,8},{8,0},{16,24},{24,16},{1,9},{9,1},{17,25},{25,17},{2,10},{10... | collective-permute-start | bytes 2949128 | tf_op jit(solution)/shard_map/ppermute | solution.py:554
  104.7 11.4 %collective-permute-start.39 = (bf16[4,72,384]{2,1,0:T(8,128)(2,1)S(1)}, bf16[4,72,384]{2,1,0:T(8,128)(2,1)S(1)}, u32[]{:S(2)}, u32[]{:S(2)}) collective-permute-start(bf16[4,72,384]{2,1,0:T(8,128)(2,1)S(1)} %fusion.16), channel_id=1, source_target_pairs={{0,16},{8,24},{16,0},{24,8},{1,17},{9,25},{17,1},{25,9},{2,18},{10... | collective-permute-start | bytes 663560 | tf_op jit(solution)/shard_map/ppermute | solution.py:554
  116.1 15.1 %collective-permute-start.30 = (bf16[2,2,4,48,640]{4,3,2,1,0:T(8,128)(2,1)S(1)}, bf16[2,2,4,48,640]{4,3,2,1,0:T(8,128)(2,1)S(1)}, u32[]{:S(2)}, u32[]{:S(2)}) collective-permute-start(bf16[2,2,4,48,640]{4,3,2,1,0:T(8,128)(2,1)S(1)} %get-tuple-element.85), channel_id=1, source_target_pairs={{0,8},{8,0},{16,24},{24,16},{1,9},{9,1},{17,25},{25,17},{2,10},{10... | collective-permute-start | bytes 2949128 | tf_op jit(solution)/shard_map/ppermute | solution.py:554
  121.4 18.7 %collective-permute-start.46 = (bf16[2,4,96,640]{3,2,1,0:T(8,128)(2,1)S(1)}, bf16[2,4,96,640]{3,2,1,0:T(8,128)(2,1)}, u32[]{:S(2)}, u32[]{:S(2)}) collective-permute-start(bf16[2,4,96,640]{3,2,1,0:T(8,128)(2,1)S(1)} %get-tuple-element.92), channel_id=1, source_target_pairs={{0,8},{8,0},{16,24},{24,16},{1,9},{9,1},{17,25},{25,17},{2,10},{10... | collective-permute-start | bytes 2949128 | tf_op jit(solution)/shard_map/ppermute | solution.py:554
  129.5 24.9 %collective-permute-start.48 = (bf16[2,4,96,640]{3,2,1,0:T(8,128)(2,1)}, bf16[2,4,96,640]{3,2,1,0:T(8,128)(2,1)}, u32[]{:S(2)}, u32[]{:S(2)}) collective-permute-start(bf16[2,4,96,640]{3,2,1,0:T(8,128)(2,1)} %add_convert_fusion.1), channel_id=1, source_target_pairs={{0,16},{8,24},{16,0},{24,8},{1,17},{9,25},{17,1},{25,9},{2,18},{10... | collective-permute-start | bytes 2949128 | tf_op jit(solution)/shard_map/ppermute | solution.py:554
  133.1 29.5 %collective-permute-start.31 = (bf16[2,4,48,640]{3,2,1,0:T(8,128)(2,1)}, bf16[2,4,48,640]{3,2,1,0:T(8,128)(2,1)}, u32[]{:S(2)}, u32[]{:S(2)}) collective-permute-start(bf16[2,4,48,640]{3,2,1,0:T(8,128)(2,1)} %fusion.3), channel_id=1, source_target_pairs={{0,16},{8,24},{16,0},{24,8},{1,17},{9,25},{17,1},{25,9},{2,18},{10... | collective-permute-start | bytes 1474568 | tf_op jit(solution)/shard_map/ppermute | solution.py:554
  (40 other events, 453.1 us)

commit v3 on v2

--- a/solution.py
+++ b/solution.py
@@ -77,6 +77,8 @@
         self.width, self.hidden = width, hidden
         self.kv = KEY_VALUE_HEADS * HEAD_SIZE
         self.lanes = up_to(width, LANES)
+        self.main = self.lanes - LANES
+        assert width - self.main == HEAD_SIZE and 2 * HEAD_SIZE == LANES
         self.nx, self.nc = self.dp // 2, 2
         self.nz, self.ny = self.fsdp // 2, 2
         s, d = self.fsdp, self.dp
@@ -211,10 +213,11 @@
         mid_ref, out_ref, dn_ref, refs = refs[0], refs[1], refs[2], refs[3:]
     gg_out, refs = refs[: plan.nc], refs[plan.nc :]
     gd_out, refs = refs[: plan.nc], refs[plan.nc :]
-    (wg, wu, wd3, wd, gg, gu, gd, xs) = refs
+    (wg, wu, wd3, wd, gg, gd, xs) = refs
     width, lanes = plan.width, plan.lanes
     z_at, y_at = place[2], place[3]
     rows, cols = plan.ff_rows, plan.ff_cols
+    main = plan.main
     blocks = [(rc, ry, rz) for rc in range(plan.nc) for ry in range(plan.ny) for rz in range(plan.nz)]
 
     def spot(rc, ry, rz):
@@ -224,8 +227,10 @@
     for rc, ry, rz in blocks:
         shard, at = spot(rc, ry, rz)
         piece = gates[rc * plan.ny + ry]
-        wg[at, :] = piece[rz, :rows]
-        wu[at, :] = piece[rz, rows:]
+        wg[at, :main] = piece[rz, :, :main]
+        wu[at, :main] = piece[rz, :, main : 2 * main]
+        wg[at, main:] = piece[rz, :, 2 * main :]
+        wu[at, main:] = piece[rz, :, 2 * main :]
         wd3[shard, :, rc * cols : (rc + 1) * cols] = downs[rc * plan.ny + ry][rz]
     tokens = xs.shape[0]
     gain = gain_ref[1:2]
@@ -237,11 +242,14 @@
         mid = mid_in[...]
     inv = lax.rsqrt(jnp.sum(mid * mid, -1, keepdims=True) * (1.0 / width) + EPS_NORM)
     unit = mid * inv
-    normed = (unit * gain).astype(BF16)
+    scaled = unit * gain
+    normed = scaled.astype(BF16)
+    turned = pltpu.roll(scaled[:, main:], HEAD_SIZE, 1).astype(BF16)
+    normed_up = jnp.concatenate([normed[:, :main], turned], 1)
     xs[:, :width] = dy_ref[...].astype(F32)
     dy = xs[...].astype(BF16)
     gate = dot_nt(normed, wg[...])
-    upper = dot_nt(normed, wu[...])
+    upper = dot_nt(normed_up, wu[...])
     units = plan.nc * cols
     wd[width:, :] = jnp.zeros((lanes - width, units), BF16)
     wd[:width, :] = jnp.concatenate([wd3[s].astype(F32) for s in range(plan.shards)], 0).astype(BF16)
@@ -251,18 +259,23 @@
     hid = (act * upper).astype(BF16)
     dgate = (dhidden * upper * sigma * (1.0 + gate * (1.0 - sigma))).astype(BF16)
     dupper = (dhidden * act).astype(BF16)
-    gg[...] = dot_tn(dgate, normed).astype(BF16)
-    gu[...] = dot_tn(dupper, normed).astype(BF16)
+    grad_gate = dot_tn(dgate, normed)
+    grad_up = dot_tn(dupper, normed_up)
+    gg[:, :main] = grad_gate[:, :main].astype(BF16)
+    gg[:, main : 2 * main] = grad_up[:, :main].astype(BF16)
+    gg[:, 2 * main :] = (grad_gate[:, main:] + grad_up[:, main:]).astype(BF16)
     down = dot_tn(dy, hid)
     for s in range(plan.shards):
         gd[s] = down[s * plan.out_rows : (s + 1) * plan.out_rows].astype(BF16)
     for rc, ry, rz in blocks:
         shard, at = spot(rc, ry, rz)
-        gg_out[rc][ry, rz, :rows] = gg[at, :]
-        gg_out[rc][ry, rz, rows:] = gu[at, :]
+        gg_out[rc][ry, rz] = gg[at, :]
         gd_out[rc][ry, rz] = gd[shard, :, rc * cols : (rc + 1) * cols]
     out = (mid if first else out_in[...]) + dot_nt(hid, wd[...])
-    dnormed = dot_nn(dgate, wg[...]) + dot_nn(dupper, wu[...])
+    by_gate = dot_nn(dgate, wg[...])
+    by_up = dot_nn(dupper, wu[...])
+    tail = lane_half(by_gate[:, main:], 0) + pltpu.roll(lane_half(by_up[:, main:], 1), HEAD_SIZE, 1)
+    dnormed = jnp.concatenate([by_gate[:, :main] + by_up[:, :main], tail], 1)
     if not first:
         dnormed = dnormed + dn_in[...]
     if last:
@@ -285,14 +298,9 @@
     grad_ref[...] = dot_tn(dmid_b, attn_ref[...]).astype(BF16)
 
 
-def backward_rest_kernel(plan, place, x_ref, dmid_ref, dgain_ref, go_ref, da_ref, attn_ref, q_ref, k_ref, v_ref,
-                         prob_ref, wq_ref, wk_ref, wv_ref, gain_ref, cos_ref, sin_ref, dx_ref, *refs):
-    packs, refs = refs[: plan.nc], refs[plan.nc :]
-    (dq_ref, dkv_ref, pack, xs) = refs
-    width, lanes = plan.width, plan.lanes
-    x_at, c_at, z_at, y_at = place[0], place[1], place[2], place[3]
-    tokens = xs.shape[0]
-    n_seq = tokens // SEQUENCE_LENGTH
+def backward_attention_kernel(plan, da_ref, attn_ref, q_ref, k_ref, v_ref, prob_ref, cos_ref, sin_ref, dq_ref, dkv_ref):
+    lanes = plan.lanes
+    n_seq = q_ref.shape[0] // SEQUENCE_LENGTH
     cos = cos_ref[...]
     sin = sin_ref[...]
 
@@ -337,6 +345,15 @@
         return carry
 
     lax.fori_loop(0, n_seq, one_sequence, 0)
+
+
+def backward_out_kernel(plan, place, x_ref, dmid_ref, dgain_ref, go_ref, dq_ref, dkv_ref, wq_ref, wk_ref, wv_ref,
+                        gain_ref, dx_ref, *refs):
+    packs, refs = refs[: plan.nc], refs[plan.nc :]
+    (pack, xs) = refs
+    width, lanes = plan.width, plan.lanes
+    x_at, c_at, z_at, y_at = place[0], place[1], place[2], place[3]
+    tokens = xs.shape[0]
     xs[:, lanes - LANES :] = jnp.zeros((tokens, LANES), F32)
     xs[:, :width] = x_ref[...].astype(F32)
     dq, dk, dv = dq_ref[...], dkv_ref[0], dkv_ref[1]
@@ -386,8 +403,12 @@
         for rx in range(plan.nx):
             part = (place[0] + rx + 1) % plan.nx * plan.nc + (place[1] + rc) % plan.nc
             at = pl.ds(pl.multiple_of(part * rows, rows), rows)
-            gate_ref[at, :] = ref[rx, :rows, : plan.width].astype(F32)
-            up_ref[at, :] = ref[rx, rows:, : plan.width].astype(F32)
+            main = plan.main
+            tail = ref[rx, :, 2 * main :].astype(F32)
+            gate_ref[at, :main] = ref[rx, :, :main].astype(F32)
+            gate_ref[at, main:] = tail[:, :HEAD_SIZE]
+            up_ref[at, :main] = ref[rx, :, main : 2 * main].astype(F32)
+            up_ref[at, main:] = pltpu.roll(tail, HEAD_SIZE, 1)[:, :HEAD_SIZE]
 
 
 def unpack_attention_kernel(plan, place, mine_ref, other_ref, q_ref, k_ref, v_ref, o_ref, gain_a_ref, gain_m_ref):
@@ -463,7 +484,7 @@
     rows, lanes = cotangent.shape[0], plan.lanes
     held = kept(plan)
     units = plan.nc * plan.ff_cols
-    ff = held((plan.ny, plan.nz, 2 * plan.ff_rows, lanes), BF16)
+    ff = held((plan.ny, plan.nz, plan.ff_rows, 2 * plan.width), BF16)
     dn = held((plan.ny, plan.nz, plan.out_rows, plan.ff_cols), BF16)
     whole = held((rows, lanes), F32)
     results = [shape_of((rows, plan.width), BF16), whole, held((8, lanes), F32)] if last else [whole] * 3
@@ -478,8 +499,7 @@
             pltpu.VMEM((units, lanes), BF16),
             pltpu.VMEM((plan.shards, plan.out_rows, units), BF16),
             pltpu.VMEM((lanes, units), BF16),
-            pltpu.VMEM((units, lanes), BF16),
-            pltpu.VMEM((units, lanes), BF16),
+            pltpu.VMEM((units, 2 * plan.width), BF16),
             pltpu.VMEM((plan.shards, plan.out_rows, units), BF16),
             pltpu.VMEM((rows, lanes), F32),
         ],
@@ -505,21 +525,28 @@
         packs = [held(block, BF16)] * 2
     else:
         packs = [shape_of((2,) + block, BF16)]
+    dq, dkv = pl.pallas_call(
+        functools.partial(backward_attention_kernel, plan),
+        name="backward_attention",
+        in_specs=[VMEM] * 8,
+        out_specs=[VMEM] * 2,
+        out_shape=[held((rows, lanes), BF16), held((2, rows, 2 * LANES), BF16)],
+        cost_estimate=cost(7),
+        compiler_params=limit(plan, 12),
+    )(da, attn, q, k, v, prob, cos, sin)
     return pl.pallas_call(
-        functools.partial(backward_rest_kernel, plan),
-        name="backward_rest",
-        in_specs=[SMEM] + [VMEM] * 16,
+        functools.partial(backward_out_kernel, plan),
+        name="backward_out",
+        in_specs=[SMEM] + [VMEM] * 10,
         out_specs=[VMEM] * (1 + len(packs)),
         out_shape=[shape_of((rows, plan.width), BF16)] + packs,
         scratch_shapes=[
-            pltpu.VMEM((rows, lanes), BF16),
-            pltpu.VMEM((2, rows, 2 * LANES), BF16),
             pltpu.VMEM((2, plan.shards, plan.half_rows, lanes), BF16),
             pltpu.VMEM((rows, lanes), F32),
         ],
-        cost_estimate=cost(14),
+        cost_estimate=cost(4),
         compiler_params=limit(plan, 16),
-    )(place, tokens, dmid, dgain, grad_out, da, attn, q, k, v, prob, wq, wk, wv, gain, cos, sin)
+    )(place, tokens, dmid, dgain, grad_out, dq, dkv, wq, wk, wv, gain)
 
 
 def unpack(plan, kernel, place, mine, other, shapes):
@@ -604,6 +631,10 @@
         side = jnp.pad(extra, ((0, rows.shape[0] - extra.shape[0]), (0, rest - extra.shape[1])))
         return jnp.concatenate([rows, side], 1)
 
+    def abreast(gate, up):
+        main = plan.main
+        return jnp.concatenate([gate[:, :main], up[:, :main], gate[:, main:], up[:, main:]], 1)
+
     def all_rows(w):
         return lax.all_gather(w.T, "fsdp", axis=0, tiled=True)
 
@@ -614,11 +645,7 @@
         own = jnp.where(c_first, first, second)
         part_rows = plan.half_rows // plan.nx
         own = jnp.where(x_first, own[:part_rows], own[part_rows:])
-        gate_own = widen(
-            jnp.concatenate(
-                [lax.dynamic_slice_in_dim(w, ff_at, plan.ff_rows, 1).T for w in (w_gate, w_up)], 0
-            )
-        )
+        gate_own = abreast(*[lax.dynamic_slice_in_dim(w, ff_at, plan.ff_rows, 1).T for w in (w_gate, w_up)])
         down_own = w_down.reshape(plan.shards, plan.parts, plan.ff_rows, plan.out_rows)
         down_own = lax.dynamic_index_in_dim(down_own, d_at, 1, False).reshape(plan.ff_cols, plan.out_rows).T
         held_a = spread(plan, own, "yxc")
@@ -637,7 +664,7 @@
             widen(jnp.concatenate([all_rows(w_query), all_rows(w_key)], 0), gains)[None],
             widen(jnp.concatenate([all_rows(w_value), all_rows(w_out)], 0))[None],
         ]
-        gates = [[widen(jnp.concatenate([all_rows(w_gate), all_rows(w_up)], 0))[None]]]
+        gates = [[abreast(all_rows(w_gate), all_rows(w_up))[None]]]
         downs = [[all_rows(w_down)[None]]]
 
     q, k, v, attn, prob, wq, wk, wv, wo, gain = attention_forward(plan, place, tokens, cos, sin, pieces)
@@ -660,14 +687,16 @@
             away, keep = mine
             if dims == "xy":
                 part = add(keep, send(plan, away, "x"))
-                part = add(part[0], send(plan, part[1], "y"))
+                there = send(plan, part[1], "y")
+                part = add(part[0], there)
             else:
                 both = jnp.stack([keep[1], away[1]])
                 got = send(plan, both, "y")
                 there = send(plan, add(away[0], got[1]), "x")
                 part = add(add(keep[0], got[0]), there)
             part = reduce_z(plan, part)
-            both = jnp.stack([part, send(plan, part, "x")])
+            there = send(plan, part, "x")
+            both = jnp.stack([part, there])
             return both, send(plan, both, "c")
 
         def in_order(both, other):
@@ -678,7 +707,7 @@
         ff_rows = plan.ff_rows
         both, other = fold([g[0] for g in grads], "xy")
         grad_gate, grad_up = unpack(plan, unpack_ff_kernel, place, both, other, [(plan.parts * ff_rows, width)] * 2)
-        quads = in_order(*fold([g[1] for g in grads], "yx"))
+        quads = in_order(*fold([g[1] for g in grads], "xy"))
         quads = quads.reshape(plan.parts, rows, plan.shards, ff_rows)
         grad_down = quads.transpose(1, 2, 0, 3).reshape(rows, hidden).astype(F32)
         got = send(plan, packs[1], "c")
@@ -686,10 +715,9 @@
         part = add(add(packs[0][0], got[0]), there)
         part = add(part[0], send(plan, part[1], "y"))
         part = reduce_z(plan, part)
-        part, grad_down = lax.optimization_barrier((part, grad_down))
         there = send(plan, part, "x")
         both = jnp.stack([part, there])
-        both, grad_gate, grad_up = lax.optimization_barrier((both, grad_gate, grad_up))
+        both, grad_down = lax.optimization_barrier((both, grad_down))
         other = send(plan, both, "c")
         shapes = [(rows, width), (krows, width), (krows, width), (rows, width), (1, rows), (1, rows)]
         *results, gain_a, gain_m = unpack(plan, unpack_attention_kernel, place, both, other, shapes)
@@ -709,8 +737,10 @@
             part = lax.psum_scatter(value.astype(F32), "fsdp", scatter_dimension=0, tiled=True)
             return lax.psum(part, "dp")
 
-        both = grads[0][0][0].reshape(2, hidden, lanes)[:, :, :width]
-        grad_gate, grad_up = total(both[0]).T, total(both[1]).T
+        both = grads[0][0][0].reshape(hidden, 2 * width)
+        main, half = plan.main, 2 * plan.main + HEAD_SIZE
+        grad_gate = total(jnp.concatenate([both[:, :main], both[:, 2 * main : half]], 1)).T
+        grad_up = total(jnp.concatenate([both[:, main : 2 * main], both[:, half:]], 1)).T
         grad_down = total(grads[0][1][0].reshape(width, hidden)).T
         whole = packs[0].reshape(2, width + plan.kv, lanes)
         one = jnp.concatenate([total(whole[0, :width]), total(whole[0, width:])], 0)

time: 198 us -> 187 us (0.944)
  starting transfers between devices: 59.1 us -> 50.4 us
    ppermute x56, starting transfers between devices: 59.1 us -> 50.4 us  [send(): return lax.ppermute(value, axis, pairs)]
    convert_element_type x10 -> x9, other arithmetic: 5.91 us -> 5.82 us  [add(): return (a.astype(F32) + b.astype(F32)).astype(BF16)]
    pallas_call x1 -> x2, Pallas kernels: 10.8 us -> 10.9 us  [the longest x1 6.35 us: attention_backward(): pl.pallas_call(functools.partial(backward_attention_kernel, plan), name='...]
  transfers between devices with their start and end apart: 56 -> 56, of which waited for: 19 -> 20; matrix products, arithmetic and copies ran while one was open for 7% -> 6% of each run, Pallas kernels for 18% -> 20%
where the time goes in v3:
time: 187 us; the launch traced here: 186 us
  waiting for transfers between devices  80.3 us (43%)
  starting transfers between devices  50.4 us (27%)
  Pallas kernels  39.3 us (21%)
  other arithmetic  8.12 us (4%)
  local copies, waits for them, and re-layouts  7 us (4%)
    ppermute x56, waiting for transfers between devices, send(): return lax.ppermute(value, axis, pairs)  80.3 us
    ppermute x56, starting transfers between devices, send(): return lax.ppermute(value, axis, pairs)  50.4 us
    pallas_call x2, Pallas kernels, mlp(): pl.pallas_call(functools.partial(mlp_kernel, plan, first, last), name='ml...  18.6 us
    pallas_call x1, Pallas kernels, attention_backward(): pl.pallas_call(functools.partial(backward_attention_kernel, plan), name='...  6.35 us
    convert_element_type x9, other arithmetic, add(): return (a.astype(F32) + b.astype(F32)).astype(BF16)  5.82 us
    pallas_call x1, Pallas kernels, attention_forward(): pl.pallas_call(functools.partial(attention_forward_kernel, plan, len(piec...  5.45 us
    pallas_call x1, Pallas kernels, attention_backward(): pl.pallas_call(functools.partial(backward_out_kernel, plan), name='backwa...  4.5 us
  transfers between devices with their start and end apart: 56, of which 20 were waited for; matrix products, arithmetic and copies ran while one was open for 6% of the time, Pallas kernels for 20%

profile of v3, /device:TPU:0, one launch (start us, length us, event | category | flops | bytes accessed | tf_op | source)
XLA Modules:
  0.0 186.3 jit_solution(13827257207248010837)
XLA Ops:
  2.6 3.1 %collective-permute-start = (bf16[48,640]{1,0:T(8,128)(2,1)S(1)}, bf16[48,640]{1,0:T(8,128)(2,1)S(1)}, u32[]{:S(2)}, u32[]{:S(2)}) collective-permute-start(bf16[48,640]{1,0:T(8,128)(2,1)S(1)} %slice_select_fusion), channel_id=1, source_target_pairs={{0,2},{1,3},{2,0},{3,1},{4,6},{5,7},{6,4},{7,5},{8,10},{9,11},{10,... | collective-permute-start | bytes 184328 | tf_op jit(solution)/shard_map/ppermute | solution.py:581
  5.8 2.6 %collective-permute-start.1 = (bf16[48,640]{1,0:T(8,128)(2,1)S(1)}, bf16[48,640]{1,0:T(8,128)(2,1)S(1)}, u32[]{:S(2)}, u32[]{:S(2)}) collective-permute-start(bf16[48,640]{1,0:T(8,128)(2,1)S(1)} %slice_select_fusion), channel_id=1, source_target_pairs={{0,4},{1,5},{2,6},{3,7},{4,0},{5,1},{6,2},{7,3},{8,12},{9,13},{10,... | collective-permute-start | bytes 184328 | tf_op jit(solution)/shard_map/ppermute | solution.py:581
  9.7 2.5 %collective-permute-done.1 = bf16[48,640]{1,0:T(8,128)(2,1)S(1)} collective-permute-done((bf16[48,640]{1,0:T(8,128)(2,1)S(1)}, bf16[48,640]{1,0:T(8,128)(2,1)S(1)}, u32[]{:S(2)}, u32[]{:S(2)}) %collective-permute-start.1) | collective-permute-done | bytes 61472 | tf_op jit(solution)/shard_map/ppermute | solution.py:581
  12.1 2.3 %collective-permute-done.2 = bf16[48,640]{1,0:T(8,128)(2,1)S(1)} collective-permute-done((bf16[48,640]{1,0:T(8,128)(2,1)S(1)}, bf16[48,640]{1,0:T(8,128)(2,1)S(1)}, u32[]{:S(2)}, u32[]{:S(2)}) %collective-permute-start.2) | collective-permute-done | bytes 61472 | tf_op jit(solution)/shard_map/ppermute | solution.py:581
  18.3 2.3 %collective-permute-start.18 = (bf16[72,384]{1,0:T(8,128)(2,1)S(1)}, bf16[72,384]{1,0:T(8,128)(2,1)S(1)}, u32[]{:S(2)}, u32[]{:S(2)}) collective-permute-start(bf16[72,384]{1,0:T(8,128)(2,1)S(1)} %bitcast.123), channel_id=1, source_target_pairs={{0,6},{1,7},{2,4},{3,5},{4,2},{5,3},{6,0},{7,1},{8,14},{9,15},{10,... | collective-permute-start | bytes 165896 | tf_op jit(solution)/shard_map/ppermute | solution.py:581
  23.8 2.3 %collective-permute-start.12 = (bf16[48,1152]{1,0:T(8,128)(2,1)S(1)}, bf16[48,1152]{1,0:T(8,128)(2,1)S(1)}, u32[]{:S(2)}, u32[]{:S(2)}) collective-permute-start(bf16[48,1152]{1,0:T(8,128)(2,1)S(1)} %concatenate.15), channel_id=1, source_target_pairs={{0,6},{1,7},{2,4},{3,5},{4,2},{5,3},{6,0},{7,1},{8,14},{9,15},{10,... | collective-permute-start | bytes 331784 | tf_op jit(solution)/shard_map/ppermute | solution.py:581
  35.3 5.4 %collective-permute-done.5.refs_3_ = bf16[4,48,640]{2,1,0:T(8,128)(2,1)S(1)} collective-permute-done((bf16[4,48,640]{2,1,0:T(8,128)(2,1)S(1)}, bf16[4,48,640]{2,1,0:T(8,128)(2,1)S(1)}, u32[]{:S(2)}, u32[]{:S(2)}) %collective-permute-start.5) | collective-permute-done | bytes 245792 | tf_op jit(solution)/shard_map/ppermute | solution.py:581
  41.3 4.5 %collective-permute-done.13.refs_4_ = bf16[4,48,1152]{2,1,0:T(8,128)(2,1)S(1)} collective-permute-done((bf16[4,48,1152]{2,1,0:T(8,128)(2,1)S(1)}, bf16[4,48,1152]{2,1,0:T(8,128)(2,1)S(1)}, u32[]{:S(2)}, u32[]{:S(2)}) %collective-permute-start.13) | collective-permute-done | bytes 442400 | tf_op jit(solution)/shard_map/ppermute | solution.py:581
  45.7 4.0 %collective-permute-done.22.refs_3_ = bf16[4,48,1152]{2,1,0:T(8,128)(2,1)S(1)} collective-permute-done((bf16[4,48,1152]{2,1,0:T(8,128)(2,1)S(1)}, bf16[4,48,1152]{2,1,0:T(8,128)(2,1)S(1)}, u32[]{:S(2)}, u32[]{:S(2)}) %collective-permute-start.22) | collective-permute-done | bytes 442400 | tf_op jit(solution)/shard_map/ppermute | solution.py:581
  50.2 5.5 %attention_forward.1 = (bf16[576,640]{1,0:T(8,128)(2,1)S(1)}, bf16[576,512]{1,0:T(8,128)(2,1)S(1)}, bf16[576,512]{1,0:T(8,128)(2,1)S(1)}, bf16[576,640]{1,0:T(8,...) custom-call(s32[4]{0:T(128)S(1)} %pad_add_fusion.place, ...), custom_call_target="tpu_custom_call" | custom-call | flops 10000000000 | bytes 10000000 | tf_op jit(solution)/shard_map/attention_forward/pallas_call | solution.py:457
  55.7 9.2 %mlp.2 = (f32[576,640]{1,0:T(8,128)S(1)}, f32[576,640]{1,0:T(8,128)S(1)}, f32[576,640]{1,0:T(8,128)S(1)}, bf16[2,4,48,1152]{3,2,1,0:T(8,128)(2,1)S(1)}, bf16[2,4...) custom-call(s32[4]{0:T(128)S(1)} %pad_add_fusion.place, ...), custom_call_target="tpu_custom_call" | custom-call | flops 12000000000 | bytes 12000000 | tf_op jit(solution)/shard_map/mlp/pallas_call | solution.py:491
  67.7 5.8 %collective-permute-done.26.refs_7_ = bf16[4,72,384]{2,1,0:T(8,128)(2,1)S(1)} collective-permute-done((bf16[4,72,384]{2,1,0:T(8,128)(2,1)S(1)}, bf16[4,72,384]{2,1,0:T(8,128)(2,1)S(1)}, u32[]{:S(2)}, u32[]{:S(2)}) %collective-permute-start.26) | collective-permute-done | bytes 221216 | tf_op jit(solution)/shard_map/ppermute | solution.py:581
  73.5 4.1 %collective-permute-done.27.refs_8_ = bf16[4,72,384]{2,1,0:T(8,128)(2,1)S(1)} collective-permute-done((bf16[4,72,384]{2,1,0:T(8,128)(2,1)S(1)}, bf16[4,72,384]{2,1,0:T(8,128)(2,1)S(1)}, u32[]{:S(2)}, u32[]{:S(2)}) %collective-permute-start.27) | collective-permute-done | bytes 221216 | tf_op jit(solution)/shard_map/ppermute | solution.py:581
  79.2 9.4 %mlp.3 = (bf16[576,576]{1,0:T(8,128)(2,1)}, f32[576,640]{1,0:T(8,128)S(1)}, f32[8,640]{1,0:T(8,128)S(1)}, bf16[2,4,48,1152]{3,2,1,0:T(8,128)(2,1)S(1)}, bf16[2,4...) custom-call(s32[4]{0:T(128)S(1)} %pad_add_fusion.place, ...), custom_call_target="tpu_custom_call" | custom-call | flops 12000000000 | bytes 12000000 | tf_op jit(solution)/shard_map/mlp/pallas_call | solution.py:491
  93.8 4.5 %collective-permute-done.40 = bf16[4,72,384]{2,1,0:T(8,128)(2,1)S(1)} collective-permute-done((bf16[4,72,384]{2,1,0:T(8,128)(2,1)S(1)}, bf16[4,72,384]{2,1,0:T(8,128)(2,1)S(1)}, u32[]{:S(2)}, u32[]{:S(2)}) %collective-permute-start.40) | collective-permute-done | bytes 221216 | tf_op jit(solution)/shard_map/ppermute | solution.py:581
  102.9 6.4 %backward_attention.1 = (bf16[576,640]{1,0:T(8,128)(2,1)S(1)}, bf16[2,576,256]{2,1,0:T(8,128)(2,1)S(1)}) custom-call(bf16[576,640]{1,0:T(8,128)(2,1)S(1)} %get-tuple-element.74.da_ref, bf16[576,640]{1,0:T(8,128)(2,1)S(1)} %get-tuple-element.63.refs_1_.attn_ref, bf16[576,640]{1,0:T(8,128)(2,1)S(1)} %get-tuple-element.75.q_ref, ...), custom_call_target="tpu_custom_call" | custom-call | flops 7000000000 | bytes 7000000 | tf_op jit(solution)/shard_map/backward_attention/pallas_call | solution.py:528
  110.5 4.5 %backward_out.1 = (bf16[576,576]{1,0:T(8,128)(2,1)}, bf16[2,2,4,48,640]{4,3,2,1,0:T(8,128)(2,1)S(1)}, bf16[2,2,4,48,640]{4,3,2,1,0:T(8,128)(2,1)S(1)}) custom-call(s32[4]{0:T(128)S(1)} %pad_add_fusion.place, bf16[576,576]{1,0:T(8,128)(2,1)S(1)} %copy-done.2, f32[576,640]{1,0:T(8,128)S(1)} %get-tuple-element.71.dmid_ref, ...), custom_call_target="tpu_custom_call" | custom-call | flops 4000000000 | bytes 4000000 | tf_op jit(solution)/shard_map/backward_out/pallas_call | solution.py:537
  123.5 16.2 %collective-permute-done.49 = bf16[2,4,48,1152]{3,2,1,0:T(8,128)(2,1)} collective-permute-done((bf16[2,4,48,1152]{3,2,1,0:T(8,128)(2,1)}, bf16[2,4,48,1152]{3,2,1,0:T(8,128)(2,1)}, u32[]{:S(2)}, u32[]{:S(2)}) %collective-permute-start.49) | collective-permute-done | bytes 884768 | tf_op jit(solution)/shard_map/ppermute | solution.py:581
  141.4 7.7 %collective-permute-done.31 = bf16[2,4,48,640]{3,2,1,0:T(8,128)(2,1)S(1)} collective-permute-done((bf16[2,4,48,640]{3,2,1,0:T(8,128)(2,1)S(1)}, bf16[2,4,48,640]{3,2,1,0:T(8,128)(2,1)S(1)}, u32[]{:S(2)}, u32[]{:S(2)}) %collective-permute-start.31) | collective-permute-done | bytes 491552 | tf_op jit(solution)/shard_map/ppermute | solution.py:581
  152.6 6.7 %collective-permute-done.32 = bf16[4,48,640]{2,1,0:T(8,128)(2,1)S(1)} collective-permute-done((bf16[4,48,640]{2,1,0:T(8,128)(2,1)S(1)}, bf16[4,48,640]{2,1,0:T(8,128)(2,1)S(1)}, u32[]{:S(2)}, u32[]{:S(2)}) %collective-permute-start.32) | collective-permute-done | bytes 245792 | tf_op jit(solution)/shard_map/ppermute | solution.py:581
  159.5 2.2 %collective-permute-start.34 = (bf16[48,640]{1,0:T(8,128)(2,1)S(1)}, bf16[48,640]{1,0:T(8,128)(2,1)S(1)}, u32[]{:S(2)}, u32[]{:S(2)}) collective-permute-start(bf16[48,640]{1,0:T(8,128)(2,1)S(1)} %get-tuple-element.132), channel_id=1, source_target_pairs={{0,4},{1,5},{2,6},{3,7},{4,0},{5,1},{6,2},{7,3},{8,12},{9,13},{10,... | collective-permute-start | bytes 184328 | tf_op jit(solution)/shard_map/ppermute | solution.py:581
  163.8 3.1 %collective-permute-done.50 = bf16[4,48,1152]{2,1,0:T(8,128)(2,1)S(1)} collective-permute-done((bf16[4,48,1152]{2,1,0:T(8,128)(2,1)S(1)}, bf16[4,48,1152]{2,1,0:T(8,128)(2,1)S(1)}, u32[]{:S(2)}, u32[]{:S(2)}) %collective-permute-start.50) | collective-permute-done | bytes 442400 | tf_op jit(solution)/shard_map/ppermute | solution.py:581
  172.5 4.9 %collective-permute-done.52 = bf16[48,1152]{1,0:T(8,128)(2,1)S(1)} collective-permute-done((bf16[48,1152]{1,0:T(8,128)(2,1)S(1)}, bf16[48,1152]{1,0:T(8,128)(2,1)S(1)}, u32[]{:S(2)}, u32[]{:S(2)}) %collective-permute-start.52) | collective-permute-done | bytes 110624 | tf_op jit(solution)/shard_map/ppermute | solution.py:581
  178.5 3.8 %collective-permute-done.54 = bf16[48,1152]{1,0:T(8,128)(2,1)S(1)} collective-permute-done((bf16[48,1152]{1,0:T(8,128)(2,1)S(1)}, bf16[48,1152]{1,0:T(8,128)(2,1)S(1)}, u32[]{:S(2)}, u32[]{:S(2)}) %collective-permute-start.54) | collective-permute-done | bytes 110624 | tf_op jit(solution)/shard_map/ppermute | solution.py:581
  (153 shorter events, 62.5 us)
Async XLA Ops:
  14.4 17.4 %collective-permute-start.3 = (bf16[4,48,640]{2,1,0:T(8,128)(2,1)S(1)}, bf16[4,48,640]{2,1,0:T(8,128)(2,1)S(1)}, u32[]{:S(2)}, u32[]{:S(2)}) collective-permute-start(bf16[4,48,640]{2,1,0:T(8,128)(2,1)S(1)} %pad_maximum_fusion.1.refs_0_), channel_id=1, source_target_pairs={{0,1},{1,0},{2,3},{3,2},{4,5},{5,4},{6,7},{7,6},{8,9},{9,8},{10,11... | collective-permute-start | bytes 737288 | tf_op jit(solution)/shard_map/ppermute | solution.py:581
  21.8 10.1 %collective-permute-start.11 = (bf16[48,1152]{1,0:T(8,128)(2,1)S(1)}, bf16[48,1152]{1,0:T(8,128)(2,1)S(1)}, u32[]{:S(2)}, u32[]{:S(2)}) collective-permute-start(bf16[48,1152]{1,0:T(8,128)(2,1)S(1)} %concatenate.15), channel_id=1, source_target_pairs={{0,4},{1,5},{2,6},{3,7},{4,0},{5,1},{6,2},{7,3},{8,12},{9,13},{10,... | collective-permute-start | bytes 331784 | tf_op jit(solution)/shard_map/ppermute | solution.py:581
  33.4 12.4 %collective-permute-start.13 = (bf16[4,48,1152]{2,1,0:T(8,128)(2,1)S(1)}, bf16[4,48,1152]{2,1,0:T(8,128)(2,1)S(1)}, u32[]{:S(2)}, u32[]{:S(2)}) collective-permute-start(bf16[4,48,1152]{2,1,0:T(8,128)(2,1)S(1)} %pad_maximum_fusion.refs_3_), channel_id=1, source_target_pairs={{0,1},{1,0},{2,3},{3,2},{4,5},{5,4},{6,7},{7,6},{8,9},{9,8},{10,11... | collective-permute-start | bytes 1327112 | tf_op jit(solution)/shard_map/ppermute | solution.py:581
  34.0 15.8 %collective-permute-start.22 = (bf16[4,48,1152]{2,1,0:T(8,128)(2,1)S(1)}, bf16[4,48,1152]{2,1,0:T(8,128)(2,1)S(1)}, u32[]{:S(2)}, u32[]{:S(2)}) collective-permute-start(bf16[4,48,1152]{2,1,0:T(8,128)(2,1)S(1)} %pad_maximum_fusion.refs_3_), channel_id=1, source_target_pairs={{0,16},{8,24},{16,0},{24,8},{1,17},{9,25},{17,1},{25,9},{2,18},{10... | collective-permute-start | bytes 1327112 | tf_op jit(solution)/shard_map/ppermute | solution.py:581
  40.7 15.0 %collective-permute-start.20 = (bf16[4,72,384]{2,1,0:T(8,128)(2,1)S(1)}, bf16[4,72,384]{2,1,0:T(8,128)(2,1)S(1)}, u32[]{:S(2)}, u32[]{:S(2)}) collective-permute-start(bf16[4,72,384]{2,1,0:T(8,128)(2,1)S(1)} %pad_maximum_fusion.2.refs_7_), channel_id=1, source_target_pairs={{0,8},{8,0},{16,24},{24,16},{1,9},{9,1},{17,25},{25,17},{2,10},{10... | collective-permute-start | bytes 663560 | tf_op jit(solution)/shard_map/ppermute | solution.py:581
  41.2 14.5 %collective-permute-start.14 = (bf16[4,48,1152]{2,1,0:T(8,128)(2,1)S(1)}, bf16[4,48,1152]{2,1,0:T(8,128)(2,1)S(1)}, u32[]{:S(2)}, u32[]{:S(2)}) collective-permute-start(bf16[4,48,1152]{2,1,0:T(8,128)(2,1)S(1)} %pad_maximum_fusion.refs_3_), channel_id=1, source_target_pairs={{0,8},{8,0},{16,24},{24,16},{1,9},{9,1},{17,25},{25,17},{2,10},{10... | collective-permute-start | bytes 1327112 | tf_op jit(solution)/shard_map/ppermute | solution.py:581
  45.7 10.0 %collective-permute-start.21 = (bf16[4,72,384]{2,1,0:T(8,128)(2,1)S(1)}, bf16[4,72,384]{2,1,0:T(8,128)(2,1)S(1)}, u32[]{:S(2)}, u32[]{:S(2)}) collective-permute-start(bf16[4,72,384]{2,1,0:T(8,128)(2,1)S(1)} %collective-permute-done.19.refs_8_), channel_id=1, source_target_pairs={{0,8},{8,0},{16,24},{24,16},{1,9},{9,1},{17,25},{25,17},{2,10},{10... | collective-permute-start | bytes 663560 | tf_op jit(solution)/shard_map/ppermute | solution.py:581
  49.7 17.5 %collective-permute-start.23 = (bf16[4,48,1152]{2,1,0:T(8,128)(2,1)S(1)}, bf16[4,48,1152]{2,1,0:T(8,128)(2,1)S(1)}, u32[]{:S(2)}, u32[]{:S(2)}) collective-permute-start(bf16[4,48,1152]{2,1,0:T(8,128)(2,1)S(1)} %collective-permute-done.22.refs_3_), channel_id=1, source_target_pairs={{0,1},{1,0},{2,3},{3,2},{4,5},{5,4},{6,7},{7,6},{8,9},{9,8},{10,11... | collective-permute-start | bytes 1327112 | tf_op jit(solution)/shard_map/ppermute | solution.py:581
  64.9 12.7 %collective-permute-start.38 = (bf16[2,4,72,384]{3,2,1,0:T(8,128)(2,1)S(1)}, bf16[2,4,72,384]{3,2,1,0:T(8,128)(2,1)S(1)}, u32[]{:S(2)}, u32[]{:S(2)}) collective-permute-start(bf16[2,4,72,384]{3,2,1,0:T(8,128)(2,1)S(1)} %get-tuple-element.90), channel_id=1, source_target_pairs={{0,8},{8,0},{16,24},{24,16},{1,9},{9,1},{17,25},{25,17},{2,10},{10... | collective-permute-start | bytes 1327112 | tf_op jit(solution)/shard_map/ppermute | solution.py:581
  66.6 10.9 %collective-permute-start.27 = (bf16[4,72,384]{2,1,0:T(8,128)(2,1)S(1)}, bf16[4,72,384]{2,1,0:T(8,128)(2,1)S(1)}, u32[]{:S(2)}, u32[]{:S(2)}) collective-permute-start(bf16[4,72,384]{2,1,0:T(8,128)(2,1)S(1)} %collective-permute-done.19.refs_8_), channel_id=1, source_target_pairs={{0,16},{8,24},{16,0},{24,8},{1,17},{9,25},{17,1},{25,9},{2,18},{10... | collective-permute-start | bytes 663560 | tf_op jit(solution)/shard_map/ppermute | solution.py:581
  67.2 12.0 %collective-permute-start.24 = (bf16[4,48,1152]{2,1,0:T(8,128)(2,1)S(1)}, bf16[4,48,1152]{2,1,0:T(8,128)(2,1)S(1)}, u32[]{:S(2)}, u32[]{:S(2)}) collective-permute-start(bf16[4,48,1152]{2,1,0:T(8,128)(2,1)S(1)} %collective-permute-done.22.refs_3_), channel_id=1, source_target_pairs={{0,8},{8,0},{16,24},{24,16},{1,9},{9,1},{17,25},{25,17},{2,10},{10... | collective-permute-start | bytes 1327112 | tf_op jit(solution)/shard_map/ppermute | solution.py:581
  67.2 12.0 %collective-permute-start.25 = (bf16[4,48,1152]{2,1,0:T(8,128)(2,1)S(1)}, bf16[4,48,1152]{2,1,0:T(8,128)(2,1)S(1)}, u32[]{:S(2)}, u32[]{:S(2)}) collective-permute-start(bf16[4,48,1152]{2,1,0:T(8,128)(2,1)S(1)} %collective-permute-done.23.refs_4_), channel_id=1, source_target_pairs={{0,8},{8,0},{16,24},{24,16},{1,9},{9,1},{17,25},{25,17},{2,10},{10... | collective-permute-start | bytes 1327112 | tf_op jit(solution)/shard_map/ppermute | solution.py:581
  77.7 12.6 %collective-permute-start.39 = (bf16[2,4,72,384]{3,2,1,0:T(8,128)(2,1)S(1)}, bf16[2,4,72,384]{3,2,1,0:T(8,128)(2,1)S(1)}, u32[]{:S(2)}, u32[]{:S(2)}) collective-permute-start(bf16[2,4,72,384]{3,2,1,0:T(8,128)(2,1)S(1)} %add_convert_fusion.6), channel_id=1, source_target_pairs={{0,16},{8,24},{16,0},{24,8},{1,17},{9,25},{17,1},{25,9},{2,18},{10... | collective-permute-start | bytes 1327112 | tf_op jit(solution)/shard_map/ppermute | solution.py:581
  88.9 26.7 %collective-permute-start.48 = (bf16[2,4,48,1152]{3,2,1,0:T(8,128)(2,1)S(1)}, bf16[2,4,48,1152]{3,2,1,0:T(8,128)(2,1)S(1)}, u32[]{:S(2)}, u32[]{:S(2)}) collective-permute-start(bf16[2,4,48,1152]{3,2,1,0:T(8,128)(2,1)S(1)} %get-tuple-element.99), channel_id=1, source_target_pairs={{0,8},{8,0},{16,24},{24,16},{1,9},{9,1},{17,25},{25,17},{2,10},{10... | collective-permute-start | bytes 2654216 | tf_op jit(solution)/shard_map/ppermute | solution.py:581
  89.2 34.3 %collective-permute-start.47 = (bf16[2,4,48,1152]{3,2,1,0:T(8,128)(2,1)}, bf16[2,4,48,1152]{3,2,1,0:T(8,128)(2,1)}, u32[]{:S(2)}, u32[]{:S(2)}) collective-permute-start(bf16[2,4,48,1152]{3,2,1,0:T(8,128)(2,1)} %get-tuple-element.97), channel_id=1, source_target_pairs={{0,8},{8,0},{16,24},{24,16},{1,9},{9,1},{17,25},{25,17},{2,10},{10... | collective-permute-start | bytes 2654216 | tf_op jit(solution)/shard_map/ppermute | solution.py:581
  98.4 10.8 %collective-permute-start.41 = (bf16[72,384]{1,0:T(8,128)(2,1)S(1)}, bf16[72,384]{1,0:T(8,128)(2,1)S(1)}, u32[]{:S(2)}, u32[]{:S(2)}) collective-permute-start(bf16[72,384]{1,0:T(8,128)(2,1)S(1)} %get-tuple-element.133), channel_id=1, source_target_pairs={{0,2},{1,3},{2,0},{3,1},{4,6},{5,7},{6,4},{7,5},{8,10},{9,11},{10,... | collective-permute-start | bytes 165896 | tf_op jit(solution)/shard_map/ppermute | solution.py:581
  98.5 10.7 %collective-permute-start.42 = (bf16[72,384]{1,0:T(8,128)(2,1)S(1)}, bf16[72,384]{1,0:T(8,128)(2,1)S(1)}, u32[]{:S(2)}, u32[]{:S(2)}) collective-permute-start(bf16[72,384]{1,0:T(8,128)(2,1)S(1)} %get-tuple-element.135), channel_id=1, source_target_pairs={{0,4},{1,5},{2,6},{3,7},{4,0},{5,1},{6,2},{7,3},{8,12},{9,13},{10,... | collective-permute-start | bytes 165896 | tf_op jit(solution)/shard_map/ppermute | solution.py:581
  116.8 22.8 %collective-permute-start.49 = (bf16[2,4,48,1152]{3,2,1,0:T(8,128)(2,1)}, bf16[2,4,48,1152]{3,2,1,0:T(8,128)(2,1)}, u32[]{:S(2)}, u32[]{:S(2)}) collective-permute-start(bf16[2,4,48,1152]{3,2,1,0:T(8,128)(2,1)} %add_convert_fusion.1), channel_id=1, source_target_pairs={{0,16},{8,24},{16,0},{24,8},{1,17},{9,25},{17,1},{25,9},{2,18},{10... | collective-permute-start | bytes 2654216 | tf_op jit(solution)/shard_map/ppermute | solution.py:581
  122.3 26.8 %collective-permute-start.31 = (bf16[2,4,48,640]{3,2,1,0:T(8,128)(2,1)S(1)}, bf16[2,4,48,640]{3,2,1,0:T(8,128)(2,1)S(1)}, u32[]{:S(2)}, u32[]{:S(2)}) collective-permute-start(bf16[2,4,48,640]{3,2,1,0:T(8,128)(2,1)S(1)} %fusion.3), channel_id=1, source_target_pairs={{0,16},{8,24},{16,0},{24,8},{1,17},{9,25},{17,1},{25,9},{2,18},{10... | collective-permute-start | bytes 1474568 | tf_op jit(solution)/shard_map/ppermute | solution.py:581
  152.0 15.0 %collective-permute-start.50 = (bf16[4,48,1152]{2,1,0:T(8,128)(2,1)S(1)}, bf16[4,48,1152]{2,1,0:T(8,128)(2,1)S(1)}, u32[]{:S(2)}, u32[]{:S(2)}) collective-permute-start(bf16[4,48,1152]{2,1,0:T(8,128)(2,1)S(1)} %slice_bitcast_fusion), channel_id=1, source_target_pairs={{0,1},{1,0},{2,3},{3,2},{4,5},{5,4},{6,7},{7,6},{8,9},{9,8},{10,11... | collective-permute-start | bytes 1327112 | tf_op jit(solution)/shard_map/ppermute | solution.py:581
  159.4 10.1 %collective-permute-start.33 = (bf16[48,640]{1,0:T(8,128)(2,1)S(1)}, bf16[48,640]{1,0:T(8,128)(2,1)S(1)}, u32[]{:S(2)}, u32[]{:S(2)}) collective-permute-start(bf16[48,640]{1,0:T(8,128)(2,1)S(1)} %get-tuple-element.130), channel_id=1, source_target_pairs={{0,2},{1,3},{2,0},{3,1},{4,6},{5,7},{6,4},{7,5},{8,10},{9,11},{10,... | collective-permute-start | bytes 184328 | tf_op jit(solution)/shard_map/ppermute | solution.py:581
  159.5 12.1 %collective-permute-start.34 = (bf16[48,640]{1,0:T(8,128)(2,1)S(1)}, bf16[48,640]{1,0:T(8,128)(2,1)S(1)}, u32[]{:S(2)}, u32[]{:S(2)}) collective-permute-start(bf16[48,640]{1,0:T(8,128)(2,1)S(1)} %get-tuple-element.132), channel_id=1, source_target_pairs={{0,4},{1,5},{2,6},{3,7},{4,0},{5,1},{6,2},{7,3},{8,12},{9,13},{10,... | collective-permute-start | bytes 184328 | tf_op jit(solution)/shard_map/ppermute | solution.py:581
  161.7 9.9 %collective-permute-start.35 = (bf16[48,640]{1,0:T(8,128)(2,1)S(1)}, bf16[48,640]{1,0:T(8,128)(2,1)S(1)}, u32[]{:S(2)}, u32[]{:S(2)}) collective-permute-start(bf16[48,640]{1,0:T(8,128)(2,1)S(1)} %get-tuple-element.131), channel_id=1, source_target_pairs={{0,6},{1,7},{2,4},{3,5},{4,2},{5,3},{6,0},{7,1},{8,14},{9,15},{10,... | collective-permute-start | bytes 184328 | tf_op jit(solution)/shard_map/ppermute | solution.py:581
  167.2 10.2 %collective-permute-start.52 = (bf16[48,1152]{1,0:T(8,128)(2,1)S(1)}, bf16[48,1152]{1,0:T(8,128)(2,1)S(1)}, u32[]{:S(2)}, u32[]{:S(2)}) collective-permute-start(bf16[48,1152]{1,0:T(8,128)(2,1)S(1)} %get-tuple-element.129), channel_id=1, source_target_pairs={{0,4},{1,5},{2,6},{3,7},{4,0},{5,1},{6,2},{7,3},{8,12},{9,13},{10,... | collective-permute-start | bytes 331784 | tf_op jit(solution)/shard_map/ppermute | solution.py:581
  (38 other events, 375.8 us)
